TPU v7x, 32 devices: a whole 2x2x4 slice. The times are simulated.
32 devices in a mesh: fsdp: 8 (over z, x), ctx: 2 (over core), tp: 2 (over y).
Axes of the slice: x: 2, y: 2, z: 4, core: 2. Of those that a mesh axis runs over, the one named last changes fastest.
Arguments:
- inputs: bfloat16 [8, 320, 1024], P('fsdp', 'ctx'), may hold values from -11 to 11, as said below
- lengths: int32 [8], P('fsdp'), may hold values from 224 to 320, as said below
- grad_out: bfloat16 [8, 320, 1024], P('fsdp', 'ctx'), may hold values from -6 to 6
- ln1_gain: bfloat16 [1024], P(('fsdp', 'ctx')), may hold values from 0.099609375 to 1.8984375
- ln1_shift: bfloat16 [1024], P(('fsdp', 'ctx')), may hold values from -3 to 3
- w_qkv: bfloat16 [1024, 3, 1024], P(('fsdp', 'ctx'), None, 'tp'), may hold values from -0.1875 to 0.1875
- b_qv: bfloat16 [1024, 2], P(('fsdp', 'ctx'), 'tp'), may hold values from -3 to 3
- w_proj: bfloat16 [1024, 1024], P(('fsdp', 'ctx'), 'tp'), may hold values from -0.5 to 0.5
- b_proj: bfloat16 [1024], P(('fsdp', 'ctx')), may hold values from -3 to 3
- ln2_gain: bfloat16 [1024], P(('fsdp', 'ctx')), may hold values from 0.099609375 to 1.8984375
- ln2_shift: bfloat16 [1024], P(('fsdp', 'ctx')), may hold values from -3 to 3
- w_up: bfloat16 [1024, 4096], P(('fsdp', 'ctx'), 'tp'), may hold values from -0.1875 to 0.1875
- b_up: bfloat16 [2048, 2], P(('fsdp', 'ctx'), 'tp'), may hold values from -3 to 3
- w_down: bfloat16 [1024, 4096], P(('fsdp', 'ctx'), 'tp'), may hold values from -0.09375 to 0.09375
- b_down: bfloat16 [1024], P(('fsdp', 'ctx')), may hold values from -3 to 3
Outputs:
- output: bfloat16 [8, 320, 1024], P('fsdp', 'ctx')
- grad_inputs: float32 [8, 320, 1024], P('fsdp', 'ctx')
- grad_ln1_gain: float32 [1024], P(('fsdp', 'ctx'))
- grad_ln1_shift: float32 [1024], P(('fsdp', 'ctx'))
- grad_w_qkv: float32 [1024, 3, 1024], P(('fsdp', 'ctx'), None, 'tp')
- grad_b_qv: float32 [1024, 2], P(('fsdp', 'ctx'), 'tp')
- grad_w_proj: float32 [1024, 1024], P(('fsdp', 'ctx'), 'tp')
- grad_b_proj: float32 [1024], P(('fsdp', 'ctx'))
- grad_ln2_gain: float32 [1024], P(('fsdp', 'ctx'))
- grad_ln2_shift: float32 [1024], P(('fsdp', 'ctx'))
- grad_w_up: float32 [1024, 4096], P(('fsdp', 'ctx'), 'tp')
- grad_b_up: float32 [2048, 2], P(('fsdp', 'ctx'), 'tp')
- grad_w_down: float32 [1024, 4096], P(('fsdp', 'ctx'), 'tp')
- grad_b_down: float32 [1024], P(('fsdp', 'ctx'))
- rms: float32 [5], replicated
Inputs may be any that keep to these rules, and one draw needn't show every extreme that they name: The lengths 320 and 224 both occur in every draw. `inputs`: rows at or past an image's length are never read.
All inputs are finite; a program needn't handle non-finite values.
Results may differ from a plain program's by a relative error of at most 0.014.
Values may be sent and summed in bfloat16 or wider, within the bound.
No kernel may reach another device: no remote copies, remote signals or barrier semaphores. Data moves between devices by JAX's collectives and lax.ppermute only.
A program may use at most 128 MiB of HBM per device.

v0:
```python
from functools import partial

import jax
import jax.numpy as jnp
from jax import lax
from jax.sharding import PartitionSpec as P

D = 1024
HD = 64


EPSILON = 1e-06
MASK_FILL = -1e30


def layer_norm(values_in, gain, shift):
    mean_val = jnp.mean(values_in, axis=-1, keepdims=True)
    centered = values_in - mean_val
    spread = jnp.mean(centered * centered, axis=-1, keepdims=True)
    return centered * lax.rsqrt(spread + EPSILON) * gain + shift


def contract(left, right, left_dim, right_dim):
    return lax.dot_general(
        left, right, (((left_dim,), (right_dim,)), ((), ())), preferred_element_type=jnp.float32
    )


def attn_scores(query_heads, key_all, key_valid):
    scores = jnp.einsum(
        "bqhd,bkhd->bhqk", query_heads, key_all, preferred_element_type=jnp.float32
    ) * HD ** (-0.5)
    return jnp.where(key_valid[:, None, None, :], scores, MASK_FILL)


def body(
    inputs,
    lengths,
    grad_out,
    ln1_gain,
    ln1_shift,
    w_qkv,
    b_qv,
    w_proj,
    b_proj,
    ln2_gain,
    ln2_shift,
    w_up,
    b_up,
    w_down,
    b_down,
):
    gathered = (
        lax.all_gather(ln1_gain, ("fsdp", "ctx"), axis=0, tiled=True),
        lax.all_gather(ln1_shift, ("fsdp", "ctx"), axis=0, tiled=True),
        lax.all_gather(w_qkv, ("fsdp", "ctx"), axis=0, tiled=True),
        lax.all_gather(b_qv, ("fsdp", "ctx"), axis=0, tiled=True),
        lax.all_gather(w_proj, ("fsdp", "ctx"), axis=0, tiled=True),
        lax.all_gather(b_proj, ("fsdp", "ctx"), axis=0, tiled=True),
        lax.all_gather(ln2_gain, ("fsdp", "ctx"), axis=0, tiled=True),
        lax.all_gather(ln2_shift, ("fsdp", "ctx"), axis=0, tiled=True),
        lax.all_gather(w_up, ("fsdp", "ctx"), axis=0, tiled=True),
        lax.all_gather(b_up, ("fsdp", "ctx"), axis=0, tiled=True),
        lax.all_gather(w_down, ("fsdp", "ctx"), axis=0, tiled=True),
        lax.all_gather(b_down, ("fsdp", "ctx"), axis=0, tiled=True),
    )
    (
        gain_first,
        shift_first,
        qkv_full,
        qv_bias,
        proj_full,
        proj_bias,
        gain_second,
        shift_second,
        up_full,
        up_bias,
        down_full,
        down_bias,
    ) = gathered
    images, half_slots = (inputs.shape[0], inputs.shape[1])
    row_count = images * half_slots
    slot_total = half_slots * lax.axis_size("ctx")
    slot_ids = lax.axis_index("ctx") * half_slots + jnp.arange(half_slots, dtype=jnp.int32)
    is_valid = (slot_ids[None, :] < lengths[:, None]).astype(jnp.float32)
    key_valid = jnp.arange(slot_total, dtype=jnp.int32)[None, :] < lengths[:, None]
    row_valid = is_valid.reshape(row_count, 1)
    gain_one = gain_first.astype(jnp.float32)
    shift_one = shift_first.astype(jnp.float32)
    gain_two = gain_second.astype(jnp.float32)
    shift_two = shift_second.astype(jnp.float32)
    entering = inputs.astype(jnp.float32).reshape(row_count, D) * row_valid
    normed = layer_norm(entering, gain_one, shift_one).astype(jnp.bfloat16)
    local_width = qkv_full.shape[2]
    local_heads = local_width // HD
    qkv_flat = qkv_full.reshape(D, 3 * local_width)
    packed = jnp.dot(normed, qkv_flat, preferred_element_type=jnp.float32).reshape(
        row_count, 3, local_width
    )
    bias_values = qv_bias.astype(jnp.float32)[:, 0]
    query_part = (packed[:, 0] + bias_values[:local_width]).astype(jnp.bfloat16)
    key_part = packed[:, 1].astype(jnp.bfloat16)
    value_part = (packed[:, 2] + bias_values[local_width:]).astype(jnp.bfloat16)
    head_shape = (images, half_slots, local_heads, HD)
    query_heads = query_part.reshape(head_shape)
    key_all, value_all = (
        lax.all_gather(key_part.reshape(head_shape), "ctx", axis=1, tiled=True),
        lax.all_gather(value_part.reshape(head_shape), "ctx", axis=1, tiled=True),
    )
    scores = attn_scores(query_heads, key_all, key_valid)
    row_max = jnp.max(scores, axis=-1, keepdims=True)
    raised = jnp.exp(scores - row_max)
    row_total = jnp.sum(raised, axis=-1, keepdims=True)
    attn_prob = raised / row_total
    log_total = row_max + jnp.log(row_total)
    context = jnp.einsum(
        "bhqk,bkhd->bqhd",
        attn_prob.astype(jnp.bfloat16),
        value_all,
        preferred_element_type=jnp.float32,
    )
    context = context.astype(jnp.bfloat16).reshape(row_count, local_width)
    attended = lax.psum(contract(context, proj_full, 1, 1), "tp") + proj_bias.astype(jnp.float32)
    middle = entering + attended
    normed_two = layer_norm(middle, gain_two, shift_two).astype(jnp.bfloat16)
    pre_act = (
        jnp.dot(normed_two, up_full, preferred_element_type=jnp.float32)
        + up_bias.astype(jnp.float32)[:, 0]
    )
    active = jax.nn.gelu(pre_act, approximate=False).astype(jnp.bfloat16)
    branch = lax.psum(contract(active, down_full, 1, 1).astype(jnp.bfloat16), "tp").astype(
        jnp.float32
    ) + down_bias.astype(jnp.float32)
    result = middle + branch
    output = result.astype(jnp.bfloat16).reshape(images, half_slots, D)
    square_sums = jnp.stack(
        [
            jnp.sum(row_valid * stat_term * stat_term)
            for stat_term in (entering, attended, middle, branch, result)
        ]
    )
    valid_count = jnp.sum(is_valid)
    total_squares, total_count = lax.psum((square_sums, valid_count), ("fsdp", "ctx"))
    rms = jnp.sqrt(total_squares / (total_count * D))
    grad_low = grad_out.reshape(row_count, D)
    grad_res = grad_low.astype(jnp.float32)
    grad_down_bias = jnp.sum(grad_res, axis=0)
    grad_down = contract(grad_low, active, 0, 0)
    grad_active = jnp.dot(grad_low, down_full, preferred_element_type=jnp.float32)
    _, gelu_pull = jax.vjp(partial(jax.nn.gelu, approximate=False), pre_act)
    grad_pre = gelu_pull(grad_active)[0].astype(jnp.bfloat16)
    grad_up_bias = jnp.sum(grad_pre.astype(jnp.float32), axis=0)[:, None]
    grad_up = contract(normed_two, grad_pre, 0, 0)
    grad_normed_two = lax.psum(contract(grad_pre, up_full, 1, 1), "tp")
    _, norm_pull_two = jax.vjp(layer_norm, middle, gain_two, shift_two)
    grad_mid_part, grad_gain_two, grad_shift_two = norm_pull_two(grad_normed_two)
    grad_middle = grad_res + grad_mid_part
    grad_att = grad_middle.astype(jnp.bfloat16)
    grad_proj_bias = jnp.sum(grad_att.astype(jnp.float32), axis=0)
    grad_proj = contract(grad_att, context, 0, 0)
    grad_context = (
        jnp.dot(grad_att, proj_full, preferred_element_type=jnp.float32)
        .astype(jnp.bfloat16)
        .reshape(head_shape)
    )
    scores_again = attn_scores(query_heads, key_all, key_valid)
    prob_again = jnp.exp(scores_again - log_total)
    grad_prob = jnp.einsum(
        "bqhd,bkhd->bhqk", grad_context, value_all, preferred_element_type=jnp.float32
    )
    grad_scores = (
        prob_again * (grad_prob - jnp.sum(prob_again * grad_prob, axis=-1, keepdims=True))
    ).astype(jnp.bfloat16)
    score_scale = HD ** (-0.5)
    grad_query = (
        jnp.einsum("bhqk,bkhd->bqhd", grad_scores, key_all, preferred_element_type=jnp.float32)
        * score_scale
    )
    grad_query = grad_query.astype(jnp.bfloat16).reshape(row_count, local_width)
    key_terms = (
        jnp.einsum("bhqk,bqhd->bkhd", grad_scores, query_heads, preferred_element_type=jnp.float32)
        * score_scale
    )
    value_terms = jnp.einsum(
        "bhqk,bqhd->bkhd",
        prob_again.astype(jnp.bfloat16),
        grad_context,
        preferred_element_type=jnp.float32,
    )
    key_summed, value_summed = (
        lax.psum_scatter(key_terms, "ctx", scatter_dimension=1, tiled=True),
        lax.psum_scatter(value_terms, "ctx", scatter_dimension=1, tiled=True),
    )
    grad_key = key_summed.astype(jnp.bfloat16).reshape(row_count, local_width)
    grad_value = value_summed.astype(jnp.bfloat16).reshape(row_count, local_width)
    grad_packed = jnp.stack([grad_query, grad_key, grad_value], axis=1).reshape(
        row_count, 3 * local_width
    )
    grad_qkv = contract(normed, grad_packed, 0, 0).reshape(D, 3, local_width)
    grad_qv_bias = jnp.concatenate(
        [
            jnp.sum(grad_query.astype(jnp.float32), axis=0),
            jnp.sum(grad_value.astype(jnp.float32), axis=0),
        ]
    )[:, None]
    grad_normed = lax.psum(contract(grad_packed, qkv_flat, 1, 1).astype(jnp.bfloat16), "tp").astype(
        jnp.float32
    )
    _, norm_pull_one = jax.vjp(layer_norm, entering, gain_one, shift_one)
    grad_enter_part, grad_gain_one, grad_shift_one = norm_pull_one(grad_normed)
    grad_inputs = ((grad_middle + grad_enter_part) * row_valid).reshape(images, half_slots, D)
    summed = (
        lax.psum_scatter(grad_gain_one, ("fsdp", "ctx"), scatter_dimension=0, tiled=True),
        lax.psum_scatter(grad_shift_one, ("fsdp", "ctx"), scatter_dimension=0, tiled=True),
        lax.psum_scatter(grad_qkv, ("fsdp", "ctx"), scatter_dimension=0, tiled=True),
        lax.psum_scatter(grad_qv_bias, ("fsdp", "ctx"), scatter_dimension=0, tiled=True),
        lax.psum_scatter(grad_proj, ("fsdp", "ctx"), scatter_dimension=0, tiled=True),
        lax.psum_scatter(grad_proj_bias, ("fsdp", "ctx"), scatter_dimension=0, tiled=True),
        lax.psum_scatter(grad_gain_two, ("fsdp", "ctx"), scatter_dimension=0, tiled=True),
        lax.psum_scatter(grad_shift_two, ("fsdp", "ctx"), scatter_dimension=0, tiled=True),
        lax.psum_scatter(grad_up, ("fsdp", "ctx"), scatter_dimension=0, tiled=True),
        lax.psum_scatter(grad_up_bias, ("fsdp", "ctx"), scatter_dimension=0, tiled=True),
        lax.psum_scatter(grad_down, ("fsdp", "ctx"), scatter_dimension=0, tiled=True),
        lax.psum_scatter(grad_down_bias, ("fsdp", "ctx"), scatter_dimension=0, tiled=True),
    )
    return (
        output,
        grad_inputs,
        summed[0],
        summed[1],
        summed[2],
        summed[3],
        summed[4],
        summed[5],
        summed[6],
        summed[7],
        summed[8],
        summed[9],
        summed[10],
        summed[11],
        rms,
    )


def solution(mesh):
    in_specs = (
        P("fsdp", "ctx", None),
        P("fsdp"),
        P("fsdp", "ctx", None),
        P(("fsdp", "ctx")),
        P(("fsdp", "ctx")),
        P(("fsdp", "ctx"), None, "tp"),
        P(("fsdp", "ctx"), "tp"),
        P(("fsdp", "ctx"), "tp"),
        P(("fsdp", "ctx")),
        P(("fsdp", "ctx")),
        P(("fsdp", "ctx")),
        P(("fsdp", "ctx"), "tp"),
        P(("fsdp", "ctx"), "tp"),
        P(("fsdp", "ctx"), "tp"),
        P(("fsdp", "ctx")),
    )
    out_specs = (
        P("fsdp", "ctx", None),
        P("fsdp", "ctx", None),
        P(("fsdp", "ctx")),
        P(("fsdp", "ctx")),
        P(("fsdp", "ctx"), None, "tp"),
        P(("fsdp", "ctx"), "tp"),
        P(("fsdp", "ctx"), "tp"),
        P(("fsdp", "ctx")),
        P(("fsdp", "ctx")),
        P(("fsdp", "ctx")),
        P(("fsdp", "ctx"), "tp"),
        P(("fsdp", "ctx"), "tp"),
        P(("fsdp", "ctx"), "tp"),
        P(("fsdp", "ctx")),
        P(),
    )
    return jax.shard_map(body, mesh=mesh, in_specs=in_specs, out_specs=out_specs, check_vma=False)
```

profile of v0, /device:TPU:0, one launch (start us, length us, event | category | flops | bytes accessed | tf_op | source)
XLA Modules:
  0.0 852.9 jit_solution(4844973030946835387)
XLA Ops:
  16.6 63.5 %all-reduce.14 = (bf16[1024]{0:T(1024)(128)(2,1)S(1)}, bf16[1024]{0:T(1024)(128)(2,1)S(1)}, bf16[1024]{0:T(1024)(128)(2,1)S(1)}, bf16[1024]{0:T(1024)(128)(2,1)S...) all-reduce(bf16[1024]{0:T(1024)(128)(2,1)S(1)} %dynamic-update-slic, ...), channel_id=1, replica_groups=mesh['fsdp'=8,'ctx'=2,'tp'=2] {'fsdp','ctx'}, use_global_device_ids=true, to_apply=%add.2 | all-reduce | flops 7168 | bytes 28672
  103.3 17.4 %all_gather.53 = bf16[2048,1]{0,1:T(2,128)(2,1)S(1)} all-gather(bf16[128,1]{0,1:T(2,128)(2,1)S(1)} %copy-done.27), channel_id=1, replica_groups=mesh['fsdp'=8,'ctx'=2,'tp'=2] {'fsdp','ctx'}, dimensions={0}, use_global_device_ids=true | all-gather | bytes 4352 | tf_op jit(solution)/shard_map/all_gather | solution.py:63
  120.8 10.3 %all-reduce.20.cloned.1.call-done = f32[160,1024]{1,0:T(8,128)} async-done(((f32[160,1024]{1,0:T(8,128)}), f32[160,1024]{1,0:T(8,128)}) %all-reduce.20.cloned.1.call-update) | async-done | bytes 655376 | tf_op jit(solution)/shard_map/psum | solution.py:123
  132.6 50.9 %all-gather.9.cloned.1.call-done = bf16[1024,2048]{1,0:T(8,128)(2,1)} async-done(((bf16[64,2048]{1,0:T(8,128)(2,1)}), bf16[1024,2048]{1,0:T(8,128)(2,1)}) %all-gather.9.cloned.1.call-update) | async-done | bytes 4194320 | tf_op jit(solution)/shard_map/all_gather | solution.py:62
  183.5 7.1 multiply_convert_fusion.1
  190.6 43.8 %all-gather.11.cloned.1.call-done = bf16[1024,2048]{1,0:T(8,128)(2,1)} async-done(((bf16[64,2048]{1,0:T(8,128)(2,1)}), bf16[1024,2048]{1,0:T(8,128)(2,1)}) %all-gather.11.cloned.1.call-update) | async-done | bytes 4194320 | tf_op jit(solution)/shard_map/all_gather | solution.py:64
  234.4 4.7 convolution_convert_fusion
  239.1 7.2 convert_reduce_fusion
  249.9 12.2 %all-reduce.22.cloned.1.call-done = bf16[160,1024]{1,0:T(8,128)(2,1)} async-done(((bf16[160,1024]{1,0:T(8,128)(2,1)}), bf16[160,1024]{1,0:T(8,128)(2,1)}) %all-reduce.22.cloned.1.call-update) | async-done | bytes 327696 | tf_op jit(solution)/shard_map/psum | solution.py:131
  262.1 33.8 %all-reduce.24.cloned.1.call-done = f32[160,1024]{1,0:T(8,128)} async-done(((f32[160,1024]{1,0:T(8,128)}), f32[160,1024]{1,0:T(8,128)}) %all-reduce.24.cloned.1.call-update) | async-done | bytes 655376 | tf_op jit(solution)/shard_map/psum | solution.py:154
  296.0 3.4 fusion.36
  322.3 8.1 reduce-scatter.25.cloned.1.call-done
  333.3 3.9 fusion.11
  339.1 3.9 fusion.38
  344.1 4.6 fusion.62
  349.9 4.5 convolution_bitcast_fusion
  354.4 9.1 %copy.92 = f32[1024,2048]{1,0:T(8,128)} copy(f32[1024,2048]{0,1:T(8,128)} %convolution_bitcast_fusion) | data formatting | bytes 16777216
  364.9 27.8 %reduce-scatter.31.cloned.1.call-done = f32[128,1]{1,0:T(8,128)} async-done(((f32[2048,1]{1,0:T(8,128)}), f32[128,1]{1,0:T(8,128)}) %reduce-scatter.31.cloned.1.call-update) | async-done | bytes 528
  394.1 57.4 %reduce-scatter.29.cloned.1.call-done = f32[64,1]{1,0:T(8,128)} async-done(((f32[1024,1]{1,0:T(8,128)}), f32[64,1]{1,0:T(8,128)}) %reduce-scatter.29.cloned.1.call-update) | async-done | bytes 272
  452.8 24.2 %all-reduce.26.cloned.1.call-done = bf16[160,1024]{1,0:T(8,128)(2,1)} async-done(((bf16[160,1024]{1,0:T(8,128)(2,1)}), bf16[160,1024]{1,0:T(8,128)(2,1)}) %all-reduce.26.cloned.1.call-update) | async-done | bytes 327696 | tf_op jit(solution)/shard_map/psum | solution.py:206
  485.2 61.3 %all-reduce.13 = (f32[1024]{0:T(1024)S(1)}, f32[1024]{0:T(1024)S(1)}, f32[1024]{0:T(1024)S(1)}, f32[1024]{0:T(1024)S(1)}, f32[1024]{0:T(1024)S(1)}, /*index=5*/f32[1024]{0:T(1024)S(1)}, f32[5]{0:T(128)S(1)}, f32[]{:T(128)}) all-reduce(f32[1024]{0:T(1024)S(1)} %get-tuple-element.77, ...), channel_id=4, replica_groups=mesh['fsdp'=8,'ctx'=2,'tp'=2] {'fsdp','ctx'}, use_global_device_ids=true, to_apply=%region_18.19.clone | all-reduce | flops 6150 | bytes 49200
  551.2 80.4 %reduce-scatter.19.cloned.1.call-done = f32[64,3,512]{2,0,1:T(8,128)} async-done(((f32[1024,3,512]{2,0,1:T(8,128)}), f32[64,3,512]{2,0,1:T(8,128)}) %reduce-scatter.19.cloned.1.call-update) | async-done | bytes 393232 | tf_op jit(solution)/shard_map/reduce_scatter | solution.py:215
  631.7 107.0 %reduce-scatter.23.cloned.1.call-done = f32[64,2048]{1,0:T(8,128)} async-done(((f32[1024,2048]{1,0:T(8,128)}), f32[64,2048]{1,0:T(8,128)}) %reduce-scatter.23.cloned.1.call-update) | async-done | bytes 524304 | tf_op jit(solution)/shard_map/reduce_scatter | solution.py:221
  738.7 107.6 %reduce-scatter.33.cloned.1.call-done = f32[64,2048]{1,0:T(8,128)} async-done(((f32[1024,2048]{1,0:T(8,128)}), f32[64,2048]{1,0:T(8,128)}) %reduce-scatter.33.cloned.1.call-update) | async-done | bytes 524304
  (192 shorter events, 81.5 us)
Async XLA Ops:
  7.2 76.6 %all-gather.5.cloned.1.call-start = ((), (), s32[]{:S(2)}) async-start(), calls=%async_computation.8 | async-start | bytes 3342336 | tf_op jit(solution)/shard_map/all_gather | solution.py:56
  7.9 91.4 %all-gather.7.cloned.1.call-start = ((), (), s32[]{:S(2)}) async-start(), calls=%async_computation.9 | async-start | bytes 1114112 | tf_op jit(solution)/shard_map/all_gather | solution.py:58
  8.7 122.4 %all-reduce.20.cloned.1.call-start = ((), (), s32[]{:S(2)}) async-start(), calls=%async_computation.10 | async-start | bytes 1310720 | tf_op jit(solution)/shard_map/psum | solution.py:123
  99.4 3.9 copy-start.27
  102.1 81.4 %all-gather.9.cloned.1.call-start = ((), (), s32[]{:S(2)}) async-start(), calls=%async_computation.11 | async-start | bytes 4456448 | tf_op jit(solution)/shard_map/all_gather | solution.py:62
  102.6 131.8 %all-gather.11.cloned.1.call-start = ((), (), s32[]{:S(2)}) async-start(), calls=%async_computation.12 | async-start | bytes 4456448 | tf_op jit(solution)/shard_map/all_gather | solution.py:64
  103.2 158.9 %all-reduce.22.cloned.1.call-start = ((), (), s32[]{:S(2)}) async-start(), calls=%async_computation.13 | async-start | bytes 655360 | tf_op jit(solution)/shard_map/psum | solution.py:131
  239.1 56.9 %all-reduce.24.cloned.1.call-start = ((), (), s32[]{:S(2)}) async-start(), calls=%async_computation.14 | async-start | bytes 1310720 | tf_op jit(solution)/shard_map/psum | solution.py:154
  239.1 8.1 copy-start.5
  249.6 71.1 %reduce-scatter.27.cloned.1.call-start = ((), (), s32[]{:S(2)}) async-start(), calls=%async_computation.20 | async-start | bytes 983040
  310.8 19.6 %reduce-scatter.25.cloned.1.call-start = ((), (), s32[]{:S(2)}) async-start(), calls=%async_computation.19 | async-start | bytes 983040
  318.3 74.3 %reduce-scatter.31.cloned.1.call-start = ((), (), s32[]{:S(2)}) async-start(), calls=%async_computation.22 | async-start | bytes 1114112
  319.8 131.7 %reduce-scatter.29.cloned.1.call-start = ((), (), s32[]{:S(2)}) async-start(), calls=%async_computation.21 | async-start | bytes 557056
  333.2 4.0 copy-start.10
  333.2 4.0 copy-start.19
  333.2 143.8 %all-reduce.26.cloned.1.call-start = ((), (), s32[]{:S(2)}) async-start(), calls=%async_computation.15 | async-start | bytes 655360 | tf_op jit(solution)/shard_map/psum | solution.py:206
  337.2 214.1 %reduce-scatter.21.cloned.1.call-start = ((), (), s32[]{:S(2)}) async-start(), calls=%async_computation.17 | async-start | bytes 2228224 | tf_op jit(solution)/shard_map/reduce_scatter | solution.py:217
  339.1 292.6 %reduce-scatter.19.cloned.1.call-start = ((), (), s32[]{:S(2)}) async-start(), calls=%async_computation.16 | async-start | bytes 6684672 | tf_op jit(solution)/shard_map/reduce_scatter | solution.py:215
  343.0 395.7 %reduce-scatter.23.cloned.1.call-start = ((), (), s32[]{:S(2)}) async-start(), calls=%async_computation.18 | async-start | bytes 8912896 | tf_op jit(solution)/shard_map/reduce_scatter | solution.py:221
  348.7 497.6 %reduce-scatter.33.cloned.1.call-start = ((), (), s32[]{:S(2)}) async-start(), calls=%async_computation.23 | async-start | bytes 8912896
  363.5 119.0 %copy-start.23 = (f32[160]{0:T(256)S(1)}, f32[160]{0:T(256)}, u32[]{:S(2)}) copy-start(f32[160]{0:T(256)} %copy-done.22) | copy-start | bytes 1924
  363.5 120.4 %copy-start.4 = (f32[160,1024]{1,0:T(8,128)S(1)}, f32[160,1024]{1,0:T(8,128)}, u32[]{:S(2)}) copy-start(f32[160,1024]{1,0:T(8,128)} %copy-done.3) | copy-start | bytes 1966084
  363.5 120.4 %copy-start.25 = (f32[160]{0:T(256)S(1)}, f32[160]{0:T(256)}, u32[]{:S(2)}) copy-start(f32[160]{0:T(256)} %copy-done.24) | copy-start | bytes 1924
  477.0 6.9 copy-start.8
  (20 other events, 30.0 us)
Sparse Core Ops, SparseCore 0:
  10.2 48.3 all-gather.4
  60.7 36.5 all-gather.6
  102.2 28.8 all-reduce.19
  133.1 50.3 all-gather.8
  185.5 48.8 all-gather.10
  239.2 22.8 all-reduce.21
  264.4 31.5 all-reduce.23
  310.9 8.0 reduce-scatter.26
  321.3 9.1 reduce-scatter.24
  333.9 58.6 reduce-scatter.30
  396.2 55.2 reduce-scatter.28
  453.6 23.3 all-reduce.25
  481.4 61.9 reduce-scatter.20
  547.7 83.9 reduce-scatter.18
  636.1 102.5 reduce-scatter.22
  743.2 103.0 reduce-scatter.32
where the time goes:
time: 854 us; the launch traced here: 853 us
  waiting for transfers between devices  566 us (66%)
  blocking collectives  147 us (17%)
  local copies, waits for them, and re-layouts  52.8 us (6%)
  matrix products  52.7 us (6%)
  between operations  17.2 us (2%)
  other arithmetic  15.9 us (2%)
    unnamed x21, waiting for transfers between devices  204 us
    unnamed x2, blocking collectives  125 us
    reduce_scatter x1, waiting for transfers between devices, body(): lax.psum_scatter(grad_up, ('fsdp', 'ctx'), scatter_dimension=0, tiled=True)  107 us
    reduce_scatter x1, waiting for transfers between devices, body(): lax.psum_scatter(grad_qkv, ('fsdp', 'ctx'), scatter_dimension=0, tiled=True)  80.4 us
    all_gather x1, waiting for transfers between devices, body(): lax.all_gather(w_up, ('fsdp', 'ctx'), axis=0, tiled=True)  50.9 us
    all_gather x1, waiting for transfers between devices, body(): lax.all_gather(w_down, ('fsdp', 'ctx'), axis=0, tiled=True)  43.8 us
    unnamed x90, local copies, waits for them, and re-layouts  41.7 us
    psum x1, waiting for transfers between devices, body(): grad_normed_two = lax.psum(contract(grad_pre, up_full, 1, 1), 'tp')  33.8 us
  transfers between devices with their start and end apart: 16, of which 12 were waited for; matrix products, arithmetic and copies ran while one was open for 11% of the time, Pallas kernels for 0%

commit v1 on v0

v1 whole, which is shorter than its diff:
```python
import jax
import jax.numpy as jnp
from jax import lax
from jax.sharding import PartitionSpec as P

D = 1024
HD = 64
EPSILON = 1e-06
MASK_FILL = -1e30
ROOT_HALF = 0.7071067811865476
INV_ROOT_TWO_PI = 0.3989422804014327
F32 = jnp.float32
BF16 = jnp.bfloat16
MAX_DEPTH = 4


def contract(left, right, left_dim, right_dim):
    return lax.dot_general(
        left, right, (((left_dim,), (right_dim,)), ((), ())), preferred_element_type=F32
    )


def round_low(values):
    return lax.reduce_precision(values, 8, 7).astype(BF16)


def swap(array, axis):
    return lax.ppermute(array, axis, [(0, 1), (1, 0)])


def swap_x(array):
    n = lax.axis_size("fsdp")
    return lax.ppermute(array, "fsdp", [(i, i ^ 1) for i in range(n)])


def shift_z(array, steps):
    n = lax.axis_size("fsdp")
    return lax.ppermute(array, "fsdp", [(i, (i + 2 * steps) % n) for i in range(n)])


def relative_blocks():
    depth = lax.axis_size("fsdp") // 2
    place = lax.axis_index("fsdp")
    spots = jnp.arange(2 * depth, dtype=jnp.int32)
    return ((spots % 2) ^ (place % 2)) * depth + (place // 2 - spots // 2) % depth


def absolute_places():
    depth = lax.axis_size("fsdp") // 2
    place = lax.axis_index("fsdp")
    blocks = jnp.arange(2 * depth, dtype=jnp.int32)
    return ((place // 2 - blocks % depth) % depth) * 2 + ((place % 2) ^ (blocks // depth))


def gather_pieces(shard):
    depth = lax.axis_size("fsdp") // 2
    if depth > MAX_DEPTH:
        gathered = jnp.take(lax.all_gather(shard, "fsdp"), absolute_places(), axis=0)
        return [gathered[i] for i in range(2 * depth)]
    near = [shard] + [shift_z(shard, k) for k in range(1, depth)]
    far = [swap_x(piece) for piece in near]
    return near + far


def scatter_sum(partial):
    depth = lax.axis_size("fsdp") // 2
    half = partial.shape[0] // 2
    block = half // depth
    if depth > MAX_DEPTH:
        blocks = round_low(partial).reshape(2 * depth, block, -1)
        blocks = jnp.take(blocks, relative_blocks(), axis=0).reshape(partial.shape)
        return lax.psum_scatter(blocks, "fsdp", scatter_dimension=0, tiled=True).astype(F32)
    arrived = swap_x(round_low(partial[half:]))
    both = partial[:half] + arrived.astype(F32)
    total = both[:block]
    for k in range(1, depth):
        total = total + shift_z(
            round_low(both[k * block : (k + 1) * block]), -k
        ).astype(F32)
    return total


def image_sum(partial):
    half = partial.shape[0] // 2
    own = partial[:half] + swap(round_low(partial[half:]), "ctx").astype(F32)
    low = round_low(own)
    return low.astype(F32) + swap(low, "tp").astype(F32)


def with_other(own):
    return jnp.concatenate([own, swap(own, "ctx")], axis=0)


def stats_of(values):
    mean = jnp.mean(values, axis=-1, keepdims=True)
    centered = values - mean
    scale = lax.rsqrt(jnp.mean(centered * centered, axis=-1, keepdims=True) + EPSILON)
    return centered * scale, scale


def norm_back(normal, scale, gain, grad):
    weighted = grad * gain
    grad_in = scale * (
        weighted
        - jnp.mean(weighted, axis=-1, keepdims=True)
        - normal * jnp.mean(weighted * normal, axis=-1, keepdims=True)
    )
    return grad_in, jnp.sum(grad * normal, axis=0), jnp.sum(grad, axis=0)


def body(
    inputs,
    lengths,
    grad_out,
    ln1_gain,
    ln1_shift,
    w_qkv,
    b_qv,
    w_proj,
    b_proj,
    ln2_gain,
    ln2_shift,
    w_up,
    b_up,
    w_down,
    b_down,
):
    n = lax.axis_size("fsdp")
    depth = n // 2
    core = lax.axis_index("ctx")
    place = lax.axis_index("fsdp")
    rows = w_up.shape[0]
    head_cols = w_proj.shape[1] // 2
    hidden = w_up.shape[1] // 2
    own_slots = inputs.shape[1]
    width = D // n

    qkv_halves = w_qkv.reshape(rows, 3, 2, head_cols)
    proj_halves = w_proj.reshape(rows, 2, head_cols)
    up_halves = w_up.reshape(rows, 2, hidden)
    down_halves = w_down.reshape(rows, 2, hidden)

    def half_of(which):
        first = jnp.concatenate(
            [
                lax.dynamic_index_in_dim(qkv_halves, which, 2, keepdims=False).reshape(
                    rows, 3 * head_cols
                ),
                lax.dynamic_index_in_dim(proj_halves, which, 1, keepdims=False),
            ],
            axis=1,
        )
        return (
            first,
            lax.dynamic_index_in_dim(up_halves, which, 1, keepdims=False),
            lax.dynamic_index_in_dim(down_halves, which, 1, keepdims=False),
        )

    def by_core(own, other, axis):
        return jnp.where(
            core == 0,
            jnp.concatenate([own, other], axis=axis),
            jnp.concatenate([other, own], axis=axis),
        )

    small = jnp.concatenate(
        [
            jnp.stack([ln1_gain, ln1_shift, b_proj, ln2_gain, ln2_shift, b_down, b_qv[:, 0]]),
            b_up.reshape(2, rows),
        ]
    )
    small_both = by_core(small, swap(small, "ctx"), 1)
    own_parts, other_parts = half_of(core), half_of(1 - core)
    shards = [by_core(own, swap(other, "ctx"), 0) for own, other in zip(own_parts, other_parts)]
    small_flat = jnp.zeros((16 * 2 * rows,), BF16)
    small_flat = small_flat.at[: 9 * 2 * rows].set(small_both.reshape(-1))
    cols = shards[0].shape[1]
    small_rows = -(-16 * 2 * rows // cols)
    small_rows_padded = -(-small_rows // 8) * 8
    small_block = jnp.zeros((small_rows_padded * cols,), BF16)
    small_block = small_block.at[: 16 * 2 * rows].set(small_flat).reshape(small_rows_padded, cols)

    first_pieces = gather_pieces(jnp.concatenate([shards[0], small_block], axis=0))
    up_pieces = gather_pieces(shards[1])
    down_pieces = gather_pieces(shards[2])
    first_full = jnp.concatenate([p[: 2 * rows] for p in first_pieces], axis=0)
    qkv_full = first_full[:, : 3 * head_cols]
    proj_full = first_full[:, 3 * head_cols :]
    up_full = jnp.concatenate(up_pieces, axis=0)
    down_full = jnp.concatenate(down_pieces, axis=0)
    small_all = jnp.stack([p[2 * rows :].reshape(-1)[: 16 * 2 * rows] for p in first_pieces])
    small_all = small_all.reshape(n, 16, 2 * rows)
    vectors = small_all.transpose(1, 0, 2).reshape(16, D).astype(F32)
    gain_one, shift_one, proj_bias, gain_two, shift_two, down_bias = (vectors[i] for i in range(6))
    absolute, relative = absolute_places(), relative_blocks()
    small_abs = jnp.take(small_all, relative, axis=0).astype(F32)
    qv_all = small_abs[:, 6].reshape(2, 2, head_cols)
    qv_bias = lax.dynamic_index_in_dim(qv_all, core, 1, keepdims=False)
    up_all = small_abs[:, 7:9].reshape(n, 2, 2, rows).transpose(0, 2, 1, 3).reshape(2, hidden)
    up_bias = lax.dynamic_index_in_dim(up_all, core, 0, keepdims=False)

    def to_relative(array):
        blocks = array.reshape(array.shape[0], n, width)
        return jnp.take(blocks, absolute, axis=1).reshape(array.shape)

    def to_absolute(array):
        blocks = array.reshape(array.shape[0], n, width)
        return jnp.take(blocks, relative, axis=1).reshape(array.shape)

    length = lengths[0]
    own_ids = core * own_slots + jnp.arange(own_slots, dtype=jnp.int32)
    other_ids = (1 - core) * own_slots + jnp.arange(own_slots, dtype=jnp.int32)
    slot_ids = jnp.concatenate([own_ids, other_ids])
    key_valid = slot_ids < length
    row_valid = key_valid.astype(F32)[:, None]
    own_valid = row_valid[:own_slots]

    entering_all = with_other(to_relative(inputs[0])).astype(F32) * row_valid
    grad_low = with_other(to_relative(grad_out[0]))
    grad_res = grad_low[:own_slots].astype(F32)
    normal_one, scale_one = stats_of(entering_all)
    normed = (normal_one * gain_one + shift_one).astype(BF16)
    packed = jnp.dot(normed, qkv_full, preferred_element_type=F32)
    slots = 2 * own_slots
    heads = head_cols // HD
    head_shape = (slots, heads, HD)
    query = (packed[:, :head_cols] + qv_bias[0]).astype(BF16).reshape(head_shape)
    key = packed[:, head_cols : 2 * head_cols].astype(BF16).reshape(head_shape)
    value = (packed[:, 2 * head_cols :] + qv_bias[1]).astype(BF16).reshape(head_shape)
    score_scale = HD ** (-0.5)
    scores = jnp.einsum("qhd,khd->hqk", query, key, preferred_element_type=F32) * score_scale
    scores = jnp.where(key_valid[None, None, :], scores, MASK_FILL)
    raised = jnp.exp(scores - jnp.max(scores, axis=-1, keepdims=True))
    prob = raised / jnp.sum(raised, axis=-1, keepdims=True)
    prob_low = prob.astype(BF16)
    context = jnp.einsum("hqk,khd->qhd", prob_low, value, preferred_element_type=F32)
    context = context.astype(BF16).reshape(slots, head_cols)
    attended = image_sum(contract(context, proj_full, 1, 1)) + proj_bias
    entering = entering_all[:own_slots]
    middle = entering + attended
    normal_two, scale_two = stats_of(middle)
    normed_two = with_other((normal_two * gain_two + shift_two).astype(BF16))
    pre_act = jnp.dot(normed_two, up_full, preferred_element_type=F32) + up_bias
    cumulative = 0.5 * (1.0 + lax.erf(pre_act * ROOT_HALF))
    active = (pre_act * cumulative).astype(BF16)
    slope = cumulative + pre_act * (INV_ROOT_TWO_PI * jnp.exp(-0.5 * pre_act * pre_act))
    branch = image_sum(contract(active, down_full, 1, 1)) + down_bias
    result = middle + branch
    output = to_absolute(result.astype(BF16))[None]
    square_sums = jnp.stack(
        [jnp.sum(own_valid * t * t) for t in (entering, attended, middle, branch, result)]
        + [jnp.sum(own_valid)]
    )

    sum_down_bias = jnp.sum(grad_res, axis=0)
    sum_down = scatter_sum(contract(grad_low, active, 0, 0))
    grad_active = jnp.dot(grad_low, down_full, preferred_element_type=F32)
    grad_pre = (grad_active * slope).astype(BF16)
    sum_up_bias = jnp.sum(grad_pre.astype(F32), axis=0)
    sum_up = scatter_sum(contract(normed_two, grad_pre, 0, 0))
    grad_normed_two = image_sum(contract(grad_pre, up_full, 1, 1))
    grad_mid_part, sum_gain_two, sum_shift_two = norm_back(
        normal_two, scale_two, gain_two, grad_normed_two
    )
    grad_middle = grad_res + grad_mid_part
    grad_att_own = grad_middle.astype(BF16)
    sum_proj_bias = jnp.sum(grad_att_own.astype(F32), axis=0)
    grad_att = with_other(grad_att_own)
    grad_proj = contract(grad_att, context, 0, 0)
    grad_context = (
        jnp.dot(grad_att, proj_full, preferred_element_type=F32).astype(BF16).reshape(head_shape)
    )
    grad_prob = jnp.einsum("qhd,khd->hqk", grad_context, value, preferred_element_type=F32)
    grad_scores = (
        prob * (grad_prob - jnp.sum(prob * grad_prob, axis=-1, keepdims=True))
    ).astype(BF16)
    grad_query = jnp.einsum("hqk,khd->qhd", grad_scores, key, preferred_element_type=F32)
    grad_key = jnp.einsum("hqk,qhd->khd", grad_scores, query, preferred_element_type=F32)
    grad_value = jnp.einsum("hqk,qhd->khd", prob_low, grad_context, preferred_element_type=F32)
    grad_query = (grad_query * score_scale).astype(BF16).reshape(slots, head_cols)
    grad_key = (grad_key * score_scale).astype(BF16).reshape(slots, head_cols)
    grad_value = grad_value.astype(BF16).reshape(slots, head_cols)
    sum_qv_bias = jnp.concatenate(
        [jnp.sum(grad_query.astype(F32), axis=0), jnp.sum(grad_value.astype(F32), axis=0)]
    )
    grad_packed = jnp.concatenate([grad_query, grad_key, grad_value], axis=1)
    sum_first = scatter_sum(
        jnp.concatenate([contract(normed, grad_packed, 0, 0), grad_proj], axis=1)
    )
    grad_normed = image_sum(contract(grad_packed, qkv_full, 1, 1))
    grad_enter, sum_gain_one, sum_shift_one = norm_back(
        normal_one[:own_slots], scale_one[:own_slots], gain_one, grad_normed
    )
    grad_inputs = to_absolute((grad_middle + grad_enter) * own_valid)[None]

    tail = jnp.concatenate(
        [sum_qv_bias, square_sums, jnp.zeros((D - 2 * head_cols - 6,), F32)]
    )
    per_core = jnp.stack(
        [
            sum_gain_one,
            sum_shift_one,
            sum_proj_bias,
            sum_gain_two,
            sum_shift_two,
            sum_down_bias,
            sum_up_bias.reshape(-1)[:D],
            tail,
        ]
    )
    if depth > MAX_DEPTH:
        vectors_sum = jnp.take(per_core[:6].reshape(6, n, width), relative, axis=1)
        vectors_sum = lax.psum(vectors_sum.reshape(6, D), "fsdp")
        vector_sum = lax.dynamic_slice_in_dim(vectors_sum, place * width, width, 1)
        rest_sum = lax.psum(per_core[6:], "fsdp")
    else:
        arrived = swap_x(per_core)
        turned = jnp.concatenate([arrived[:6, D // 2 :], arrived[:6, : D // 2]], axis=1)
        both = per_core + jnp.concatenate([turned, arrived[6:]], axis=0)
        vector_sum = both[:6, :width]
        rest_sum = both[6:]
        for k in range(1, depth):
            moved = shift_z(both, -k)
            vector_sum = vector_sum + moved[:6, k * width : (k + 1) * width]
            rest_sum = rest_sum + moved[6:]
    closing = jnp.zeros((8, D), F32).at[:6, :width].set(vector_sum).at[6:].set(rest_sum)
    other_closing = swap(closing, "ctx")
    vector_sum = vector_sum + other_closing[:6, :width]
    vector_own = lax.dynamic_slice_in_dim(vector_sum, core * rows, rows, 1)
    totals = (rest_sum[1] + other_closing[7])[2 * head_cols : 2 * head_cols + 6]
    rms = jnp.sqrt(totals[:5] / (totals[5] * D))
    qv_sum = by_core(
        rest_sum[1, : 2 * head_cols].reshape(2, 1, head_cols),
        other_closing[7, : 2 * head_cols].reshape(2, 1, head_cols),
        1,
    ).reshape(-1)
    qv_own = lax.dynamic_slice_in_dim(qv_sum, (2 * place + core) * rows, rows, 0)
    up_sum = by_core(rest_sum[0], other_closing[6], 0)
    up_own = lax.dynamic_slice_in_dim(up_sum, (2 * place + core) * 2 * rows, 2 * rows, 0)

    def owned(total):
        mine = lax.dynamic_slice_in_dim(total, core * rows, rows, 0)
        theirs = swap(lax.dynamic_slice_in_dim(total, (1 - core) * rows, rows, 0), "ctx")
        return mine, theirs

    mine, theirs = owned(sum_first)
    first_out = by_core(mine.reshape(rows, 4, 1, head_cols), theirs.reshape(rows, 4, 1, head_cols), 2)
    first_out = first_out.reshape(rows, 4, 2 * head_cols)
    grad_w_up = by_core(*owned(sum_up), 1)
    grad_w_down = by_core(*owned(sum_down), 1)
    return (
        output,
        grad_inputs,
        vector_own[0],
        vector_own[1],
        first_out[:, :3],
        qv_own[:, None],
        first_out[:, 3],
        vector_own[2],
        vector_own[3],
        vector_own[4],
        grad_w_up,
        up_own[:, None],
        grad_w_down,
        vector_own[5],
        rms,
    )


def solution(mesh):
    both = ("fsdp", "ctx")
    rows, vector, matrix = P("fsdp", "ctx", None), P(both), P(both, "tp")
    in_specs = (
        rows,
        P("fsdp"),
        rows,
        vector,
        vector,
        P(both, None, "tp"),
        matrix,
        matrix,
        vector,
        vector,
        vector,
        matrix,
        matrix,
        matrix,
        vector,
    )
    out_specs = (
        rows,
        rows,
        vector,
        vector,
        P(both, None, "tp"),
        matrix,
        matrix,
        vector,
        vector,
        vector,
        matrix,
        matrix,
        matrix,
        vector,
        P(),
    )
    return jax.shard_map(body, mesh=mesh, in_specs=in_specs, out_specs=out_specs, check_vma=False)
```

time: 854 us -> 335 us (0.39)
  waiting for transfers between devices: 566 us -> 118 us
  blocking collectives: 147 us -> 0 us
  starting transfers between devices: 1.13 us -> 82.8 us
  matrix products: 52.7 us -> 25.7 us
  other arithmetic: 15.9 us -> 39 us
  between operations: 17.2 us -> 3.53 us
  local copies, waits for them, and re-layouts: 52.8 us -> 64.2 us
    unnamed x21 -> x0, waiting for transfers between devices: 204 us -> none
    reduce_scatter x3 -> x0, waiting for transfers between devices: 187 us -> none  [the longest x1 107 us: body(): lax.psum_scatter(grad_up, ('fsdp', 'ctx'), scatter_dimension=0, tiled=True)]
    unnamed x2 -> x0, blocking collectives: 125 us -> none
    ppermute x0 -> x57, waiting for transfers between devices: none -> 118 us  [the longest x21 76.6 us: shift_z(): lax.ppermute(array, 'fsdp', [(i, (i + 2 * steps) % n) for i in range(n)])]
    all_gather x4 -> x0, waiting for transfers between devices: 94.7 us -> none  [the longest x1 50.9 us: body(): lax.all_gather(w_up, ('fsdp', 'ctx'), axis=0, tiled=True)]
    ppermute x0 -> x57, starting transfers between devices: none -> 82.8 us  [the longest x21 57.9 us: shift_z(): lax.ppermute(array, 'fsdp', [(i, (i + 2 * steps) % n) for i in range(n)])]
    psum x4 -> x0, waiting for transfers between devices: 80.5 us -> none  [the longest x1 33.8 us: body(): grad_normed_two = lax.psum(contract(grad_pre, up_full, 1, 1), 'tp')]
    all_gather x3 -> x0, blocking collectives: 22.1 us -> none  [the longest x1 17.4 us: body(): lax.all_gather(b_up, ('fsdp', 'ctx'), axis=0, tiled=True)]
  transfers between devices with their start and end apart: 16 -> 57, of which waited for: 12 -> 21; matrix products, arithmetic and copies ran while one was open for 11% -> 32% of each run, Pallas kernels for 0% -> 0%
where the time goes in v1:
time: 335 us; the launch traced here: 333 us
  waiting for transfers between devices  118 us (35%)
  starting transfers between devices  82.8 us (25%)
  local copies, waits for them, and re-layouts  64.2 us (19%)
  other arithmetic  39 us (12%)
  matrix products  25.7 us (8%)
  between operations  3.53 us (1%)
    ppermute x21, waiting for transfers between devices, shift_z(): lax.ppermute(array, 'fsdp', [(i, (i + 2 * steps) % n) for i in range(n)])  76.6 us
    ppermute x21, starting transfers between devices, shift_z(): lax.ppermute(array, 'fsdp', [(i, (i + 2 * steps) % n) for i in range(n)])  57.9 us
    unnamed x176, local copies, waits for them, and re-layouts  28.1 us
    ppermute x16, waiting for transfers between devices, swap_x(): return lax.ppermute(array, 'fsdp', [(i, i ^ 1) for i in range(n)])  21.7 us
    ppermute x20, waiting for transfers between devices, swap(): return lax.ppermute(array, axis, [(0, 1), (1, 0)])  19.9 us
    ppermute x16, starting transfers between devices, swap_x(): return lax.ppermute(array, 'fsdp', [(i, i ^ 1) for i in range(n)])  16.6 us
    dot_general x8, matrix products, contract(): lax.dot_general(left, right, (((left_dim,), (right_dim,)), ((), ())), pre...  11.5 us
    ppermute x20, starting transfers between devices, swap(): return lax.ppermute(array, axis, [(0, 1), (1, 0)])  8.28 us
  transfers between devices with their start and end apart: 57, of which 21 were waited for; matrix products, arithmetic and copies ran while one was open for 32% of the time, Pallas kernels for 0%

profile of v1, /device:TPU:0, one launch (start us, length us, event | category | flops | bytes accessed | tf_op | source)
XLA Modules:
  0.0 333.4 jit_solution(15274136535306187145)
XLA Ops:
  19.8 3.0 collective-permute-start.17
  22.8 3.6 %collective-permute-start.16 = (bf16[128,1024]{1,0:T(8,128)(2,1)S(1)}, bf16[128,1024]{1,0:T(8,128)(2,1)}, u32[]{:S(2)}, u32[]{:S(2)}) collective-permute-start(bf16[128,1024]{1,0:T(8,128)(2,1)S(1)} %get-tuple-element.90), channel_id=1, source_target_pairs={{0,24},{4,28},{8,0},{12,4},{16,8},{20,12},{24,16},{28,20},{1,25},{... | collective-permute-start | bytes 786440 | tf_op jit(solution)/shard_map/ppermute | solution.py:38
  36.7 8.7 %collective-permute-done.14 = bf16[128,1024]{1,0:T(8,128)(2,1)S(1)} collective-permute-done((bf16[128,1024]{1,0:T(8,128)(2,1)S(1)}, bf16[128,1024]{1,0:T(8,128)(2,1)S(1)}, u32[]{:S(2)}, u32[]{:S(2)}) %collective-permute-start.14) | collective-permute-done | bytes 262176 | tf_op jit(solution)/shard_map/ppermute | solution.py:38
  45.4 10.6 %collective-permute-start.22 = (bf16[128,1024]{1,0:T(8,128)(2,1)}, bf16[128,1024]{1,0:T(8,128)(2,1)S(1)}, u32[]{:S(2)}, u32[]{:S(2)}) collective-permute-start(bf16[128,1024]{1,0:T(8,128)(2,1)} %get-tuple-element.86), channel_id=1, source_target_pairs={{0,8},{4,12},{8,16},{12,20},{16,24},{20,28},{24,0},{28,4},{1,9},{5... | collective-permute-start | bytes 786440 | tf_op jit(solution)/shard_map/ppermute | solution.py:38
  55.9 4.6 %collective-permute-done.15 = bf16[128,1024]{1,0:T(8,128)(2,1)S(1)} collective-permute-done((bf16[128,1024]{1,0:T(8,128)(2,1)S(1)}, bf16[128,1024]{1,0:T(8,128)(2,1)S(1)}, u32[]{:S(2)}, u32[]{:S(2)}) %collective-permute-start.15) | collective-permute-done | bytes 262176 | tf_op jit(solution)/shard_map/ppermute | solution.py:38
  62.9 16.3 %collective-permute-start.3 = (bf16[136,1024]{1,0:T(8,128)(2,1)}, bf16[136,1024]{1,0:T(8,128)(2,1)}, u32[]{:S(2)}, u32[]{:S(2)}) collective-permute-start(bf16[136,1024]{1,0:T(8,128)(2,1)} %pad_maximum_fusion.9), channel_id=1, source_target_pairs={{0,8},{4,12},{8,16},{12,20},{16,24},{20,28},{24,0},{28,4},{1,9},{5... | collective-permute-start | bytes 835592 | tf_op jit(solution)/shard_map/ppermute | solution.py:38
  82.8 7.4 %collective-permute-done.4 = bf16[136,1024]{1,0:T(8,128)(2,1)} collective-permute-done((bf16[136,1024]{1,0:T(8,128)(2,1)}, bf16[136,1024]{1,0:T(8,128)(2,1)}, u32[]{:S(2)}, u32[]{:S(2)}) %collective-permute-start.4) | collective-permute-done | bytes 278560 | tf_op jit(solution)/shard_map/ppermute | solution.py:38
  102.7 5.0 %collective-permute-done.8 = bf16[136,1024]{1,0:T(8,128)(2,1)} collective-permute-done((bf16[136,1024]{1,0:T(8,128)(2,1)}, bf16[136,1024]{1,0:T(8,128)(2,1)}, u32[]{:S(2)}, u32[]{:S(2)}) %collective-permute-start.8) | collective-permute-done | bytes 278560 | tf_op jit(solution)/shard_map/ppermute | solution.py:33
  108.9 4.7 %collective-permute-done.7 = bf16[136,1024]{1,0:T(8,128)(2,1)} collective-permute-done((bf16[136,1024]{1,0:T(8,128)(2,1)}, bf16[136,1024]{1,0:T(8,128)(2,1)}, u32[]{:S(2)}, u32[]{:S(2)}) %collective-permute-start.7) | collective-permute-done | bytes 278560 | tf_op jit(solution)/shard_map/ppermute | solution.py:33
  143.7 8.1 %collective-permute-done.26 = bf16[128,1024]{1,0:T(8,128)(2,1)S(1)} collective-permute-done((bf16[128,1024]{1,0:T(8,128)(2,1)S(1)}, bf16[128,1024]{1,0:T(8,128)(2,1)S(1)}, u32[]{:S(2)}, u32[]{:S(2)}) %collective-permute-start.26) | collective-permute-done | bytes 262176 | tf_op jit(solution)/shard_map/ppermute | solution.py:33
  155.3 2.8 multiply_convert_fusion.1
  172.6 6.1 %collective-permute-done.30 = bf16[160,1024]{1,0:T(8,128)(2,1)S(1)} collective-permute-done((bf16[160,1024]{1,0:T(8,128)(2,1)S(1)}, bf16[160,1024]{1,0:T(8,128)(2,1)S(1)}, u32[]{:S(2)}, u32[]{:S(2)}) %collective-permute-start.30) | collective-permute-done | bytes 327712 | tf_op jit(solution)/shard_map/ppermute | solution.py:28
  178.7 6.2 %collective-permute-done.33 = bf16[160,1024]{1,0:T(8,128)(2,1)S(1)} collective-permute-done((bf16[160,1024]{1,0:T(8,128)(2,1)S(1)}, bf16[160,1024]{1,0:T(8,128)(2,1)S(1)}, u32[]{:S(2)}, u32[]{:S(2)}) %collective-permute-start.33) | collective-permute-done | bytes 327712 | tf_op jit(solution)/shard_map/ppermute | solution.py:28
  206.2 4.0 %concatenate.143 = f32[1024]{0:T(1024)S(1)} concatenate(f32[256]{0:T(256)S(1)} %reduce_sum.247, f32[256]{0:T(256)S(1)} %reduce_sum.249, f32[1]{0:T(128)} %bitcast.46, f32[1]{0:T(128)} %bitcast.47, f32[1]{0:T(128)} %bitcast.48, f32[1]{0:T(128)} %bitcast.49, f32[1]{0:T(128)} %bitcast.50, f32[1]{0:T(128)} %bitcast.51, f32[506]{0:T(512)S(1)} %broadcast_in_dim.79), dimensions={0} | concatenate | bytes 8192 | tf_op jit(solution)/shard_map/concatenate | solution.py:296
  212.6 8.6 %collective-permute-start.53 = (bf16[128,1024]{1,0:T(8,128)(2,1)S(1)}, bf16[128,1024]{1,0:T(8,128)(2,1)S(1)}, u32[]{:S(2)}, u32[]{:S(2)}) collective-permute-start(bf16[128,1024]{1,0:T(8,128)(2,1)S(1)} %get-tuple-element.99), channel_id=1, source_target_pairs={{0,24},{4,28},{8,0},{12,4},{16,8},{20,12},{24,16},{28,20},{1,25},{... | collective-permute-start | bytes 786440 | tf_op jit(solution)/shard_map/ppermute | solution.py:38
  227.9 4.3 %collective-permute-start.48 = (bf16[128,1024]{1,0:T(8,128)(2,1)S(1)}, bf16[128,1024]{1,0:T(8,128)(2,1)S(1)}, u32[]{:S(2)}, u32[]{:S(2)}) collective-permute-start(bf16[128,1024]{1,0:T(8,128)(2,1)S(1)} %get-tuple-element.102), channel_id=1, source_target_pairs={{0,24},{4,28},{8,0},{12,4},{16,8},{20,12},{24,16},{28,20},{1,25},{... | collective-permute-start | bytes 786440 | tf_op jit(solution)/shard_map/ppermute | solution.py:38
  236.0 8.8 %collective-permute-done.54 = bf16[128,1024]{1,0:T(8,128)(2,1)S(1)} collective-permute-done((bf16[128,1024]{1,0:T(8,128)(2,1)S(1)}, bf16[128,1024]{1,0:T(8,128)(2,1)S(1)}, u32[]{:S(2)}, u32[]{:S(2)}) %collective-permute-start.54) | collective-permute-done | bytes 262176 | tf_op jit(solution)/shard_map/ppermute | solution.py:38
  245.1 5.5 %collective-permute-done.50 = bf16[128,1024]{1,0:T(8,128)(2,1)S(1)} collective-permute-done((bf16[128,1024]{1,0:T(8,128)(2,1)S(1)}, bf16[128,1024]{1,0:T(8,128)(2,1)S(1)}, u32[]{:S(2)}, u32[]{:S(2)}) %collective-permute-start.50) | collective-permute-done | bytes 262176 | tf_op jit(solution)/shard_map/ppermute | solution.py:38
  250.6 15.5 %collective-permute-done.49 = bf16[128,1024]{1,0:T(8,128)(2,1)S(1)} collective-permute-done((bf16[128,1024]{1,0:T(8,128)(2,1)S(1)}, bf16[128,1024]{1,0:T(8,128)(2,1)S(1)}, u32[]{:S(2)}, u32[]{:S(2)}) %collective-permute-start.49) | collective-permute-done | bytes 262176 | tf_op jit(solution)/shard_map/ppermute | solution.py:38
  270.9 6.8 %collective-permute-done.36 = bf16[160,1024]{1,0:T(8,128)(2,1)S(1)} collective-permute-done((bf16[160,1024]{1,0:T(8,128)(2,1)S(1)}, bf16[160,1024]{1,0:T(8,128)(2,1)S(1)}, u32[]{:S(2)}, u32[]{:S(2)}) %collective-permute-start.36) | collective-permute-done | bytes 327712 | tf_op jit(solution)/shard_map/ppermute | solution.py:28
  279.7 3.4 %collective-permute-done.37 = f32[8,1024]{1,0:T(8,128)S(1)} collective-permute-done((f32[8,1024]{1,0:T(8,128)S(1)}, f32[8,1024]{1,0:T(8,128)S(1)}, u32[]{:S(2)}, u32[]{:S(2)}) %collective-permute-start.37) | collective-permute-done | bytes 32800 | tf_op jit(solution)/shard_map/ppermute | solution.py:33
  283.1 3.3 collective-permute-start.39
  310.9 7.7 %collective-permute-done.45 = bf16[128,1024]{0,1:T(8,128)(2,1)S(1)} collective-permute-done((bf16[128,1024]{0,1:T(8,128)(2,1)S(1)}, bf16[128,1024]{0,1:T(8,128)(2,1)S(1)}, u32[]{:S(2)}, u32[]{:S(2)}) %collective-permute-start.45) | collective-permute-done | bytes 262176 | tf_op jit(solution)/shard_map/ppermute | solution.py:38
  318.5 10.1 %collective-permute-done.44 = bf16[128,1024]{0,1:T(8,128)(2,1)S(1)} collective-permute-done((bf16[128,1024]{0,1:T(8,128)(2,1)S(1)}, bf16[128,1024]{0,1:T(8,128)(2,1)S(1)}, u32[]{:S(2)}, u32[]{:S(2)}) %collective-permute-start.44) | collective-permute-done | bytes 262176 | tf_op jit(solution)/shard_map/ppermute | solution.py:38
  (442 shorter events, 164.8 us)
Async XLA Ops:
  8.8 20.1 %collective-permute-start.21 = (bf16[64,1024]{1,0:T(8,128)(2,1)}, bf16[64,1024]{1,0:T(8,128)(2,1)}, u32[]{:S(2)}, u32[]{:S(2)}) collective-permute-start(bf16[64,1024]{1,0:T(8,128)(2,1)} %bitcast.178), channel_id=1, source_target_pairs={{0,2},{2,0},{1,3},{3,1},{4,6},{6,4},{5,7},{7,5},{8,10},{10,8},{9,1... | collective-permute-start | bytes 393224 | tf_op jit(solution)/shard_map/ppermute | solution.py:28
  13.2 20.5 %collective-permute-start.31 = (bf16[160,1024]{1,0:T(8,128)(2,1)}, bf16[160,1024]{1,0:T(8,128)(2,1)}, u32[]{:S(2)}, u32[]{:S(2)}) collective-permute-start(bf16[160,1024]{1,0:T(8,128)(2,1)} %bitcast.175), channel_id=1, source_target_pairs={{0,2},{2,0},{1,3},{3,1},{4,6},{6,4},{5,7},{7,5},{8,10},{10,8},{9,1... | collective-permute-start | bytes 983048 | tf_op jit(solution)/shard_map/ppermute | solution.py:28
  19.8 42.4 %collective-permute-start.17 = (bf16[128,1024]{1,0:T(8,128)(2,1)S(1)}, bf16[128,1024]{1,0:T(8,128)(2,1)S(1)}, u32[]{:S(2)}, u32[]{:S(2)}) collective-permute-start(bf16[128,1024]{1,0:T(8,128)(2,1)S(1)} %get-tuple-element.90), channel_id=1, source_target_pairs={{0,4},{4,0},{8,12},{12,8},{16,20},{20,16},{24,28},{28,24},{1,5},{5... | collective-permute-start | bytes 786440 | tf_op jit(solution)/shard_map/ppermute | solution.py:33
  22.8 38.3 %collective-permute-start.16 = (bf16[128,1024]{1,0:T(8,128)(2,1)S(1)}, bf16[128,1024]{1,0:T(8,128)(2,1)}, u32[]{:S(2)}, u32[]{:S(2)}) collective-permute-start(bf16[128,1024]{1,0:T(8,128)(2,1)S(1)} %get-tuple-element.90), channel_id=1, source_target_pairs={{0,24},{4,28},{8,0},{12,4},{16,8},{20,12},{24,16},{28,20},{1,25},{... | collective-permute-start | bytes 786440 | tf_op jit(solution)/shard_map/ppermute | solution.py:38
  28.9 31.6 %collective-permute-start.15 = (bf16[128,1024]{1,0:T(8,128)(2,1)S(1)}, bf16[128,1024]{1,0:T(8,128)(2,1)S(1)}, u32[]{:S(2)}, u32[]{:S(2)}) collective-permute-start(bf16[128,1024]{1,0:T(8,128)(2,1)S(1)} %get-tuple-element.90), channel_id=1, source_target_pairs={{0,16},{4,20},{8,24},{12,28},{16,0},{20,4},{24,8},{28,12},{1,17},{... | collective-permute-start | bytes 786440 | tf_op jit(solution)/shard_map/ppermute | solution.py:38
  33.7 45.6 %collective-permute-start.23 = (bf16[128,1024]{1,0:T(8,128)(2,1)}, bf16[128,1024]{1,0:T(8,128)(2,1)S(1)}, u32[]{:S(2)}, u32[]{:S(2)}) collective-permute-start(bf16[128,1024]{1,0:T(8,128)(2,1)} %get-tuple-element.86), channel_id=1, source_target_pairs={{0,16},{4,20},{8,24},{12,28},{16,0},{20,4},{24,8},{28,12},{1,17},{... | collective-permute-start | bytes 786440 | tf_op jit(solution)/shard_map/ppermute | solution.py:38
  61.1 20.9 %collective-permute-start.5 = (bf16[136,1024]{1,0:T(8,128)(2,1)}, bf16[136,1024]{1,0:T(8,128)(2,1)}, u32[]{:S(2)}, u32[]{:S(2)}) collective-permute-start(bf16[136,1024]{1,0:T(8,128)(2,1)} %pad_maximum_fusion.9), channel_id=1, source_target_pairs={{0,24},{4,28},{8,0},{12,4},{16,8},{20,12},{24,16},{28,20},{1,25},{... | collective-permute-start | bytes 835592 | tf_op jit(solution)/shard_map/ppermute | solution.py:38
  62.2 28.1 %collective-permute-start.4 = (bf16[136,1024]{1,0:T(8,128)(2,1)}, bf16[136,1024]{1,0:T(8,128)(2,1)}, u32[]{:S(2)}, u32[]{:S(2)}) collective-permute-start(bf16[136,1024]{1,0:T(8,128)(2,1)} %pad_maximum_fusion.9), channel_id=1, source_target_pairs={{0,16},{4,20},{8,24},{12,28},{16,0},{20,4},{24,8},{28,12},{1,17},{... | collective-permute-start | bytes 835592 | tf_op jit(solution)/shard_map/ppermute | solution.py:38
  62.9 28.0 %collective-permute-start.3 = (bf16[136,1024]{1,0:T(8,128)(2,1)}, bf16[136,1024]{1,0:T(8,128)(2,1)}, u32[]{:S(2)}, u32[]{:S(2)}) collective-permute-start(bf16[136,1024]{1,0:T(8,128)(2,1)} %pad_maximum_fusion.9), channel_id=1, source_target_pairs={{0,8},{4,12},{8,16},{12,20},{16,24},{20,28},{24,0},{28,4},{1,9},{5... | collective-permute-start | bytes 835592 | tf_op jit(solution)/shard_map/ppermute | solution.py:38
  79.3 52.3 %collective-permute-start.25 = (bf16[128,1024]{1,0:T(8,128)(2,1)}, bf16[128,1024]{1,0:T(8,128)(2,1)}, u32[]{:S(2)}, u32[]{:S(2)}) collective-permute-start(bf16[128,1024]{1,0:T(8,128)(2,1)} %get-tuple-element.86), channel_id=1, source_target_pairs={{0,4},{4,0},{8,12},{12,8},{16,20},{20,16},{24,28},{28,24},{1,5},{5... | collective-permute-start | bytes 786440 | tf_op jit(solution)/shard_map/ppermute | solution.py:33
  81.3 48.6 %collective-permute-start.24 = (bf16[128,1024]{1,0:T(8,128)(2,1)}, bf16[128,1024]{1,0:T(8,128)(2,1)}, u32[]{:S(2)}, u32[]{:S(2)}) collective-permute-start(bf16[128,1024]{1,0:T(8,128)(2,1)} %get-tuple-element.86), channel_id=1, source_target_pairs={{0,24},{4,28},{8,0},{12,4},{16,8},{20,12},{24,16},{28,20},{1,25},{... | collective-permute-start | bytes 786440 | tf_op jit(solution)/shard_map/ppermute | solution.py:38
  93.9 19.8 %collective-permute-start.7 = (bf16[136,1024]{1,0:T(8,128)(2,1)}, bf16[136,1024]{1,0:T(8,128)(2,1)}, u32[]{:S(2)}, u32[]{:S(2)}) collective-permute-start(bf16[136,1024]{1,0:T(8,128)(2,1)} %collective-permute-done.3), channel_id=1, source_target_pairs={{0,4},{4,0},{8,12},{12,8},{16,20},{20,16},{24,28},{28,24},{1,5},{5... | collective-permute-start | bytes 835592 | tf_op jit(solution)/shard_map/ppermute | solution.py:33
  101.6 40.5 %collective-permute-start.20 = (bf16[128,1024]{1,0:T(8,128)(2,1)}, bf16[128,1024]{1,0:T(8,128)(2,1)}, u32[]{:S(2)}, u32[]{:S(2)}) collective-permute-start(bf16[128,1024]{1,0:T(8,128)(2,1)} %collective-permute-done.16), channel_id=1, source_target_pairs={{0,4},{4,0},{8,12},{12,8},{16,20},{20,16},{24,28},{28,24},{1,5},{5... | collective-permute-start | bytes 786440 | tf_op jit(solution)/shard_map/ppermute | solution.py:33
  107.6 31.1 %collective-permute-start.19 = (bf16[128,1024]{1,0:T(8,128)(2,1)}, bf16[128,1024]{1,0:T(8,128)(2,1)}, u32[]{:S(2)}, u32[]{:S(2)}) collective-permute-start(bf16[128,1024]{1,0:T(8,128)(2,1)} %copy-done.28), channel_id=1, source_target_pairs={{0,4},{4,0},{8,12},{12,8},{16,20},{20,16},{24,28},{28,24},{1,5},{5... | collective-permute-start | bytes 786440 | tf_op jit(solution)/shard_map/ppermute | solution.py:33
  113.6 21.3 %collective-permute-start.18 = (bf16[128,1024]{1,0:T(8,128)(2,1)}, bf16[128,1024]{1,0:T(8,128)(2,1)}, u32[]{:S(2)}, u32[]{:S(2)}) collective-permute-start(bf16[128,1024]{1,0:T(8,128)(2,1)} %copy-done.31), channel_id=1, source_target_pairs={{0,4},{4,0},{8,12},{12,8},{16,20},{20,16},{24,28},{28,24},{1,5},{5... | collective-permute-start | bytes 786440 | tf_op jit(solution)/shard_map/ppermute | solution.py:33
  131.7 22.6 %collective-permute-start.28 = (bf16[128,1024]{1,0:T(8,128)(2,1)}, bf16[128,1024]{1,0:T(8,128)(2,1)S(1)}, u32[]{:S(2)}, u32[]{:S(2)}) collective-permute-start(bf16[128,1024]{1,0:T(8,128)(2,1)} %collective-permute-done.24), channel_id=1, source_target_pairs={{0,4},{4,0},{8,12},{12,8},{16,20},{20,16},{24,28},{28,24},{1,5},{5... | collective-permute-start | bytes 786440 | tf_op jit(solution)/shard_map/ppermute | solution.py:33
  166.4 43.7 %collective-permute-start.52 = (bf16[512,1024]{1,0:T(8,128)(2,1)}, bf16[512,1024]{1,0:T(8,128)(2,1)}, u32[]{:S(2)}, u32[]{:S(2)}) collective-permute-start(bf16[512,1024]{1,0:T(8,128)(2,1)} %fusion.3), channel_id=1, source_target_pairs={{0,4},{4,0},{8,12},{12,8},{16,20},{20,16},{24,28},{28,24},{1,5},{5... | collective-permute-start | bytes 3145736 | tf_op jit(solution)/shard_map/ppermute | solution.py:33
  189.3 31.8 %collective-permute-start.47 = (bf16[512,1024]{1,0:T(8,128)(2,1)}, bf16[512,1024]{1,0:T(8,128)(2,1)}, u32[]{:S(2)}, u32[]{:S(2)}) collective-permute-start(bf16[512,1024]{1,0:T(8,128)(2,1)} %fusion.4), channel_id=1, source_target_pairs={{0,4},{4,0},{8,12},{12,8},{16,20},{20,16},{24,28},{28,24},{1,5},{5... | collective-permute-start | bytes 3145736 | tf_op jit(solution)/shard_map/ppermute | solution.py:33
  199.4 67.1 %collective-permute-start.35 = (bf16[160,1024]{1,0:T(8,128)(2,1)}, bf16[160,1024]{1,0:T(8,128)(2,1)}, u32[]{:S(2)}, u32[]{:S(2)}) collective-permute-start(bf16[160,1024]{1,0:T(8,128)(2,1)} %fusion.28), channel_id=1, source_target_pairs={{0,2},{2,0},{1,3},{3,1},{4,6},{6,4},{5,7},{7,5},{8,10},{10,8},{9,1... | collective-permute-start | bytes 983048 | tf_op jit(solution)/shard_map/ppermute | solution.py:28
  204.6 95.8 %collective-permute-start.42 = (bf16[512,1024]{0,1:T(8,128)(2,1)}, bf16[512,1024]{0,1:T(8,128)(2,1)}, u32[]{:S(2)}, u32[]{:S(2)}) collective-permute-start(bf16[512,1024]{0,1:T(8,128)(2,1)} %fusion.6), channel_id=1, source_target_pairs={{0,4},{4,0},{8,12},{12,8},{16,20},{20,16},{24,28},{28,24},{1,5},{5... | collective-permute-start | bytes 3145736 | tf_op jit(solution)/shard_map/ppermute | solution.py:33
  221.2 23.6 %collective-permute-start.54 = (bf16[128,1024]{1,0:T(8,128)(2,1)S(1)}, bf16[128,1024]{1,0:T(8,128)(2,1)S(1)}, u32[]{:S(2)}, u32[]{:S(2)}) collective-permute-start(bf16[128,1024]{1,0:T(8,128)(2,1)S(1)} %get-tuple-element.101), channel_id=1, source_target_pairs={{0,16},{4,20},{8,24},{12,28},{16,0},{20,4},{24,8},{28,12},{1,17},{... | collective-permute-start | bytes 786440 | tf_op jit(solution)/shard_map/ppermute | solution.py:38
  244.8 21.4 %collective-permute-start.49 = (bf16[128,1024]{1,0:T(8,128)(2,1)S(1)}, bf16[128,1024]{1,0:T(8,128)(2,1)S(1)}, u32[]{:S(2)}, u32[]{:S(2)}) collective-permute-start(bf16[128,1024]{1,0:T(8,128)(2,1)S(1)} %get-tuple-element.104), channel_id=1, source_target_pairs={{0,16},{4,20},{8,24},{12,28},{16,0},{20,4},{24,8},{28,12},{1,17},{... | collective-permute-start | bytes 786440 | tf_op jit(solution)/shard_map/ppermute | solution.py:38
  245.0 24.2 %collective-permute-start.56 = (f32[64,1024]{1,0:T(8,128)S(1)}, f32[64,1024]{1,0:T(8,128)S(1)}, u32[]{:S(2)}, u32[]{:S(2)}) collective-permute-start(f32[64,1024]{1,0:T(8,128)S(1)} %get-tuple-element.114), channel_id=1, source_target_pairs={{0,2},{2,0},{1,3},{3,1},{4,6},{6,4},{5,7},{7,5},{8,10},{10,8},{9,1... | collective-permute-start | bytes 786440 | tf_op jit(solution)/shard_map/ppermute | solution.py:28
  304.2 24.4 %collective-permute-start.44 = (bf16[128,1024]{0,1:T(8,128)(2,1)S(1)}, bf16[128,1024]{0,1:T(8,128)(2,1)S(1)}, u32[]{:S(2)}, u32[]{:S(2)}) collective-permute-start(bf16[128,1024]{0,1:T(8,128)(2,1)S(1)} %get-tuple-element.107), channel_id=1, source_target_pairs={{0,16},{4,20},{8,24},{12,28},{16,0},{20,4},{24,8},{28,12},{1,17},{... | collective-permute-start | bytes 786440 | tf_op jit(solution)/shard_map/ppermute | solution.py:38
  (102 other events, 1337.7 us)

commit v2 on v1

--- a/solution.py
+++ b/solution.py
@@ -11,7 +11,6 @@
 INV_ROOT_TWO_PI = 0.3989422804014327
 F32 = jnp.float32
 BF16 = jnp.bfloat16
-MAX_DEPTH = 4
 
 
 def contract(left, right, left_dim, right_dim):
@@ -28,56 +27,63 @@
     return lax.ppermute(array, axis, [(0, 1), (1, 0)])
 
 
-def swap_x(array):
+def flip(array, bit):
     n = lax.axis_size("fsdp")
-    return lax.ppermute(array, "fsdp", [(i, i ^ 1) for i in range(n)])
-
-
-def shift_z(array, steps):
-    n = lax.axis_size("fsdp")
-    return lax.ppermute(array, "fsdp", [(i, (i + 2 * steps) % n) for i in range(n)])
+    return lax.ppermute(array, "fsdp", [(i, i ^ bit) for i in range(n)])
+
+
+X_BIT, NEAR_BIT, FAR_BIT = 1, 2, 4
+
+
+def is_cube():
+    return lax.axis_size("fsdp") == 8
+
+
+def turned_bits(blocks):
+    return (blocks % 2) * 4 + (blocks // 2 % 2) * 2 + blocks // 4
 
 
 def relative_blocks():
-    depth = lax.axis_size("fsdp") // 2
-    place = lax.axis_index("fsdp")
-    spots = jnp.arange(2 * depth, dtype=jnp.int32)
-    return ((spots % 2) ^ (place % 2)) * depth + (place // 2 - spots // 2) % depth
+    spots = jnp.arange(lax.axis_size("fsdp"), dtype=jnp.int32)
+    if not is_cube():
+        return spots
+    return turned_bits(spots ^ lax.axis_index("fsdp"))
 
 
 def absolute_places():
-    depth = lax.axis_size("fsdp") // 2
-    place = lax.axis_index("fsdp")
-    blocks = jnp.arange(2 * depth, dtype=jnp.int32)
-    return ((place // 2 - blocks % depth) % depth) * 2 + ((place % 2) ^ (blocks // depth))
-
-
-def gather_pieces(shard):
-    depth = lax.axis_size("fsdp") // 2
-    if depth > MAX_DEPTH:
-        gathered = jnp.take(lax.all_gather(shard, "fsdp"), absolute_places(), axis=0)
-        return [gathered[i] for i in range(2 * depth)]
-    near = [shard] + [shift_z(shard, k) for k in range(1, depth)]
-    far = [swap_x(piece) for piece in near]
-    return near + far
+    blocks = jnp.arange(lax.axis_size("fsdp"), dtype=jnp.int32)
+    if not is_cube():
+        return blocks
+    return turned_bits(blocks) ^ lax.axis_index("fsdp")
+
+
+def tie(*values):
+    return lax.optimization_barrier(values)
+
+
+def rows_of(*pieces):
+    return jnp.concatenate(pieces, axis=0)
+
+
+def sent_half(left, right):
+    return round_low(contract(left[:, left.shape[1] // 2 :], right, 0, 0))
+
+
+def kept_half(left, right, arrived):
+    return contract(left[:, : left.shape[1] // 2], right, 0, 0) + arrived.astype(F32)
+
+
+def upper(array):
+    return array[array.shape[0] // 2 :]
+
+
+def lower(array):
+    return array[: array.shape[0] // 2]
 
 
 def scatter_sum(partial):
-    depth = lax.axis_size("fsdp") // 2
-    half = partial.shape[0] // 2
-    block = half // depth
-    if depth > MAX_DEPTH:
-        blocks = round_low(partial).reshape(2 * depth, block, -1)
-        blocks = jnp.take(blocks, relative_blocks(), axis=0).reshape(partial.shape)
-        return lax.psum_scatter(blocks, "fsdp", scatter_dimension=0, tiled=True).astype(F32)
-    arrived = swap_x(round_low(partial[half:]))
-    both = partial[:half] + arrived.astype(F32)
-    total = both[:block]
-    for k in range(1, depth):
-        total = total + shift_z(
-            round_low(both[k * block : (k + 1) * block]), -k
-        ).astype(F32)
-    return total
+    low = round_low(partial)
+    return lax.psum_scatter(low, "fsdp", scatter_dimension=0, tiled=True).astype(F32)
 
 
 def image_sum(partial):
@@ -126,7 +132,7 @@
     b_down,
 ):
     n = lax.axis_size("fsdp")
-    depth = n // 2
+    cube = is_cube()
     core = lax.axis_index("ctx")
     place = lax.axis_index("fsdp")
     rows = w_up.shape[0]
@@ -140,8 +146,8 @@
     up_halves = w_up.reshape(rows, 2, hidden)
     down_halves = w_down.reshape(rows, 2, hidden)
 
-    def half_of(which):
-        first = jnp.concatenate(
+    def first_half(which):
+        return jnp.concatenate(
             [
                 lax.dynamic_index_in_dim(qkv_halves, which, 2, keepdims=False).reshape(
                     rows, 3 * head_cols
@@ -150,11 +156,9 @@
             ],
             axis=1,
         )
-        return (
-            first,
-            lax.dynamic_index_in_dim(up_halves, which, 1, keepdims=False),
-            lax.dynamic_index_in_dim(down_halves, which, 1, keepdims=False),
-        )
+
+    def half_of(halves, which):
+        return lax.dynamic_index_in_dim(halves, which, 1, keepdims=False)
 
     def by_core(own, other, axis):
         return jnp.where(
@@ -170,25 +174,46 @@
         ]
     )
     small_both = by_core(small, swap(small, "ctx"), 1)
-    own_parts, other_parts = half_of(core), half_of(1 - core)
-    shards = [by_core(own, swap(other, "ctx"), 0) for own, other in zip(own_parts, other_parts)]
+    first_own, first_other = first_half(core), first_half(1 - core)
+    first_mine = by_core(first_own, swap(first_other, "ctx"), 0)
     small_flat = jnp.zeros((16 * 2 * rows,), BF16)
     small_flat = small_flat.at[: 9 * 2 * rows].set(small_both.reshape(-1))
-    cols = shards[0].shape[1]
+    cols = first_mine.shape[1]
     small_rows = -(-16 * 2 * rows // cols)
     small_rows_padded = -(-small_rows // 8) * 8
     small_block = jnp.zeros((small_rows_padded * cols,), BF16)
     small_block = small_block.at[: 16 * 2 * rows].set(small_flat).reshape(small_rows_padded, cols)
 
-    first_pieces = gather_pieces(jnp.concatenate([shards[0], small_block], axis=0))
-    up_pieces = gather_pieces(shards[1])
-    down_pieces = gather_pieces(shards[2])
-    first_full = jnp.concatenate([p[: 2 * rows] for p in first_pieces], axis=0)
+    first_shard = jnp.concatenate([first_mine, small_block], axis=0)
+    first_shard, inputs, grad_out, up_halves, down_halves = tie(
+        first_shard, inputs, grad_out, up_halves, down_halves
+    )
+    u, d = (
+        by_core(half_of(t, core), swap(half_of(t, 1 - core), "ctx"), 0)
+        for t in (up_halves, down_halves)
+    )
+    f = first_shard
+    if cube:
+        f_far, f_x, u_x = flip(f, FAR_BIT), flip(f, X_BIT), flip(u, X_BIT)
+        f_far, f_x, u_x, u, d = tie(f_far, f_x, u_x, u, d)
+        f_near = flip(rows_of(f, f_far), NEAR_BIT)
+        u_far, f_far_x, d_x = flip(u, FAR_BIT), flip(f_far, X_BIT), flip(d, X_BIT)
+        f_near, u_far, f_far_x, d_x, u, d = tie(f_near, u_far, f_far_x, d_x, u, d)
+        u_near = flip(rows_of(u, u_far), NEAR_BIT)
+        d_far, f_near_x, u_far_x = flip(d, FAR_BIT), flip(f_near, X_BIT), flip(u_far, X_BIT)
+        d_far, f_near_x, u_far_x, u_near, d = tie(d_far, f_near_x, u_far_x, u_near, d)
+        d_near = flip(rows_of(d, d_far), NEAR_BIT)
+        u_near_x, d_far_x = flip(u_near, X_BIT), flip(d_far, X_BIT)
+        first_all = rows_of(f, f_far, f_near, f_x, f_far_x, f_near_x)
+    else:
+        first_all, up_full, down_full = (
+            lax.all_gather(t, "fsdp", tiled=True) for t in (f, u, d)
+        )
+    first_all = first_all.reshape(n, 2 * rows + small_rows_padded, cols)
+    first_full = first_all[:, : 2 * rows].reshape(D, cols)
     qkv_full = first_full[:, : 3 * head_cols]
     proj_full = first_full[:, 3 * head_cols :]
-    up_full = jnp.concatenate(up_pieces, axis=0)
-    down_full = jnp.concatenate(down_pieces, axis=0)
-    small_all = jnp.stack([p[2 * rows :].reshape(-1)[: 16 * 2 * rows] for p in first_pieces])
+    small_all = first_all[:, 2 * rows :].reshape(n, -1)[:, : 16 * 2 * rows]
     small_all = small_all.reshape(n, 16, 2 * rows)
     vectors = small_all.transpose(1, 0, 2).reshape(16, D).astype(F32)
     gain_one, shift_one, proj_bias, gain_two, shift_two, down_bias = (vectors[i] for i in range(6))
@@ -235,7 +260,12 @@
     prob_low = prob.astype(BF16)
     context = jnp.einsum("hqk,khd->qhd", prob_low, value, preferred_element_type=F32)
     context = context.astype(BF16).reshape(slots, head_cols)
-    attended = image_sum(contract(context, proj_full, 1, 1)) + proj_bias
+    att_part = contract(context, proj_full, 1, 1)
+    if cube:
+        d_near, u_near_x, d_far_x, att_part = tie(d_near, u_near_x, d_far_x, att_part)
+        d_near_x = flip(d_near, X_BIT)
+        up_full = rows_of(u, u_far, u_near, u_x, u_far_x, u_near_x)
+    attended = image_sum(att_part) + proj_bias
     entering = entering_all[:own_slots]
     middle = entering + attended
     normal_two, scale_two = stats_of(middle)
@@ -244,6 +274,31 @@
     cumulative = 0.5 * (1.0 + lax.erf(pre_act * ROOT_HALF))
     active = (pre_act * cumulative).astype(BF16)
     slope = cumulative + pre_act * (INV_ROOT_TWO_PI * jnp.exp(-0.5 * pre_act * pre_act))
+    sum_down_bias = jnp.sum(grad_res, axis=0)
+    if cube:
+        d_near_x, active, slope = tie(d_near_x, active, slope)
+        down_full = rows_of(d, d_far, d_near, d_x, d_far_x, d_near_x)
+    grad_active = jnp.dot(grad_low, down_full, preferred_element_type=F32)
+    grad_pre = (grad_active * slope).astype(BF16)
+    gn_part = contract(grad_pre, up_full, 1, 1)
+    if cube:
+        down_low = sent_half(grad_low, active)
+        gn_part, down_low, grad_pre = tie(gn_part, down_low, grad_pre)
+        down_x = flip(down_low, X_BIT)
+        up_low = sent_half(normed_two, grad_pre)
+    grad_normed_two = image_sum(gn_part)
+    grad_mid_part, sum_gain_two, sum_shift_two = norm_back(
+        normal_two, scale_two, gain_two, grad_normed_two
+    )
+    grad_middle = grad_res + grad_mid_part
+    grad_att_own = grad_middle.astype(BF16)
+    sum_proj_bias = jnp.sum(grad_att_own.astype(F32), axis=0)
+    grad_att = with_other(grad_att_own)
+    if cube:
+        down_x, up_low, grad_att, active = tie(down_x, up_low, grad_att, active)
+        up_x = flip(up_low, X_BIT)
+        down_two = kept_half(grad_low, active, down_x)
+        down_near = flip(round_low(upper(down_two)), NEAR_BIT)
     branch = image_sum(contract(active, down_full, 1, 1)) + down_bias
     result = middle + branch
     output = to_absolute(result.astype(BF16))[None]
@@ -251,22 +306,7 @@
         [jnp.sum(own_valid * t * t) for t in (entering, attended, middle, branch, result)]
         + [jnp.sum(own_valid)]
     )
-
-    sum_down_bias = jnp.sum(grad_res, axis=0)
-    sum_down = scatter_sum(contract(grad_low, active, 0, 0))
-    grad_active = jnp.dot(grad_low, down_full, preferred_element_type=F32)
-    grad_pre = (grad_active * slope).astype(BF16)
     sum_up_bias = jnp.sum(grad_pre.astype(F32), axis=0)
-    sum_up = scatter_sum(contract(normed_two, grad_pre, 0, 0))
-    grad_normed_two = image_sum(contract(grad_pre, up_full, 1, 1))
-    grad_mid_part, sum_gain_two, sum_shift_two = norm_back(
-        normal_two, scale_two, gain_two, grad_normed_two
-    )
-    grad_middle = grad_res + grad_mid_part
-    grad_att_own = grad_middle.astype(BF16)
-    sum_proj_bias = jnp.sum(grad_att_own.astype(F32), axis=0)
-    grad_att = with_other(grad_att_own)
-    grad_proj = contract(grad_att, context, 0, 0)
     grad_context = (
         jnp.dot(grad_att, proj_full, preferred_element_type=F32).astype(BF16).reshape(head_shape)
     )
@@ -284,10 +324,46 @@
         [jnp.sum(grad_query.astype(F32), axis=0), jnp.sum(grad_value.astype(F32), axis=0)]
     )
     grad_packed = jnp.concatenate([grad_query, grad_key, grad_value], axis=1)
-    sum_first = scatter_sum(
-        jnp.concatenate([contract(normed, grad_packed, 0, 0), grad_proj], axis=1)
-    )
-    grad_normed = image_sum(contract(grad_packed, qkv_full, 1, 1))
+    gn_one_part = contract(grad_packed, qkv_full, 1, 1)
+    if cube:
+        first_low = jnp.concatenate(
+            [sent_half(normed, grad_packed), sent_half(grad_att, context)], axis=1
+        )
+        up_x, down_near, first_low, gn_one_part = tie(up_x, down_near, first_low, gn_one_part)
+        first_x_high = flip(upper(first_low), X_BIT)
+        up_two = kept_half(normed_two, grad_pre, up_x)
+        up_near = flip(round_low(upper(up_two)), NEAR_BIT)
+        down_one = lower(down_two) + down_near.astype(F32)
+        down_far = flip(round_low(upper(down_one)), FAR_BIT)
+        first_two = jnp.concatenate(
+            [
+                contract(normed[:, : D // 2], grad_packed, 0, 0),
+                contract(grad_att[:, : D // 2], context, 0, 0),
+            ],
+            axis=1,
+        )
+        first_x_high, up_near, down_far, first_low = tie(
+            first_x_high, up_near, down_far, first_low
+        )
+        first_x_low = flip(lower(first_low), X_BIT)
+        first_near = flip(
+            round_low(upper(first_two) + first_x_high.astype(F32)), NEAR_BIT
+        )
+        up_one = lower(up_two) + up_near.astype(F32)
+        up_far = flip(round_low(upper(up_one)), FAR_BIT)
+        sum_down = lower(down_one) + down_far.astype(F32)
+        first_x_low, first_near, up_far = tie(first_x_low, first_near, up_far)
+        first_one = lower(first_two) + first_x_low.astype(F32) + first_near.astype(F32)
+        first_far = flip(round_low(upper(first_one)), FAR_BIT)
+        sum_up = lower(up_one) + up_far.astype(F32)
+        sum_first = lower(first_one) + first_far.astype(F32)
+    else:
+        sum_down = scatter_sum(contract(grad_low, active, 0, 0))
+        sum_up = scatter_sum(contract(normed_two, grad_pre, 0, 0))
+        sum_proj = scatter_sum(contract(grad_att, context, 0, 0))
+        sum_qkv = scatter_sum(contract(normed, grad_packed, 0, 0))
+        sum_first = jnp.concatenate([sum_qkv, sum_proj], axis=1)
+    grad_normed = image_sum(gn_one_part)
     grad_enter, sum_gain_one, sum_shift_one = norm_back(
         normal_one[:own_slots], scale_one[:own_slots], gain_one, grad_normed
     )
@@ -308,21 +384,17 @@
             tail,
         ]
     )
-    if depth > MAX_DEPTH:
-        vectors_sum = jnp.take(per_core[:6].reshape(6, n, width), relative, axis=1)
-        vectors_sum = lax.psum(vectors_sum.reshape(6, D), "fsdp")
+    if not is_cube():
+        vectors_sum = lax.psum(per_core[:6], "fsdp")
         vector_sum = lax.dynamic_slice_in_dim(vectors_sum, place * width, width, 1)
         rest_sum = lax.psum(per_core[6:], "fsdp")
     else:
-        arrived = swap_x(per_core)
-        turned = jnp.concatenate([arrived[:6, D // 2 :], arrived[:6, : D // 2]], axis=1)
-        both = per_core + jnp.concatenate([turned, arrived[6:]], axis=0)
-        vector_sum = both[:6, :width]
-        rest_sum = both[6:]
-        for k in range(1, depth):
-            moved = shift_z(both, -k)
-            vector_sum = vector_sum + moved[:6, k * width : (k + 1) * width]
-            rest_sum = rest_sum + moved[6:]
+        total = per_core
+        for bit, half in ((X_BIT, D // 2), (NEAR_BIT, D // 4), (FAR_BIT, D // 8)):
+            arrived = flip(total, bit)
+            vector_sum = total[:6, :half] + arrived[:6, half : 2 * half]
+            rest_sum = total[6:] + arrived[6:]
+            total = jnp.zeros((8, D), F32).at[:6, :half].set(vector_sum).at[6:].set(rest_sum)
     closing = jnp.zeros((8, D), F32).at[:6, :width].set(vector_sum).at[6:].set(rest_sum)
     other_closing = swap(closing, "ctx")
     vector_sum = vector_sum + other_closing[:6, :width]
@@ -334,9 +406,9 @@
         other_closing[7, : 2 * head_cols].reshape(2, 1, head_cols),
         1,
     ).reshape(-1)
-    qv_own = lax.dynamic_slice_in_dim(qv_sum, (2 * place + core) * rows, rows, 0)
+    qv_mine = lax.dynamic_slice_in_dim(qv_sum, (2 * place + core) * rows, rows, 0)
     up_sum = by_core(rest_sum[0], other_closing[6], 0)
-    up_own = lax.dynamic_slice_in_dim(up_sum, (2 * place + core) * 2 * rows, 2 * rows, 0)
+    up_mine = lax.dynamic_slice_in_dim(up_sum, (2 * place + core) * 2 * rows, 2 * rows, 0)
 
     def owned(total):
         mine = lax.dynamic_slice_in_dim(total, core * rows, rows, 0)
@@ -354,13 +426,13 @@
         vector_own[0],
         vector_own[1],
         first_out[:, :3],
-        qv_own[:, None],
+        qv_mine[:, None],
         first_out[:, 3],
         vector_own[2],
         vector_own[3],
         vector_own[4],
         grad_w_up,
-        up_own[:, None],
+        up_mine[:, None],
         grad_w_down,
         vector_own[5],
         rms,

time: 335 us -> 265 us (0.79)
  starting transfers between devices: 82.8 us -> 45.5 us
  local copies, waits for them, and re-layouts: 64.2 us -> 41.4 us
  other arithmetic: 39 us -> 30.4 us
  waiting for transfers between devices: 118 us -> 112 us
  matrix products: 25.7 us -> 30.5 us
    ppermute x37 -> x28, starting transfers between devices: 74.5 us -> 38.5 us  [flip(): return lax.ppermute(array, 'fsdp', [(i, i ^ bit) for i in range(n)])]
    unnamed x176 -> x181, local copies, waits for them, and re-layouts: 28.1 us -> 11.3 us
    ppermute x20, waiting for transfers between devices: 19.9 us -> 13.7 us  [swap(): return lax.ppermute(array, axis, [(0, 1), (1, 0)])]
    dot_general x8 -> x12, matrix products: 11.5 us -> 16.7 us  [contract(): lax.dot_general(left, right, (((left_dim,), (right_dim,)), ((), ())), pre...]
    unnamed x6 -> x3, other arithmetic: 6.05 us -> 1.46 us
    gather x4, local copies, waits for them, and re-layouts: 7.76 us -> 4.03 us  [to_absolute(): return jnp.take(blocks, relative, axis=1).reshape(array.shape)]
    add x8 -> x9, other arithmetic: 6.8 us -> 4.05 us  [the longest x1 1.5 us: body(): lower(first_two) + first_x_low.astype(F32) + first_near.astype(F32)]
    ppermute x37 -> x28, waiting for transfers between devices: 98.3 us -> 98.3 us  [flip(): return lax.ppermute(array, 'fsdp', [(i, i ^ bit) for i in range(n)])]
  transfers between devices with their start and end apart: 57 -> 48, of which waited for: 21 -> 20; matrix products, arithmetic and copies ran while one was open for 32% -> 29% of each run, Pallas kernels for 0% -> 0%
where the time goes in v2:
time: 265 us; the launch traced here: 263 us
  waiting for transfers between devices  112 us (42%)
  starting transfers between devices  45.5 us (17%)
  local copies, waits for them, and re-layouts  41.4 us (16%)
  matrix products  30.5 us (12%)
  other arithmetic  30.4 us (11%)
  between operations  3.72 us (1%)
    ppermute x28, waiting for transfers between devices, flip(): return lax.ppermute(array, 'fsdp', [(i, i ^ bit) for i in range(n)])  98.3 us
    ppermute x28, starting transfers between devices, flip(): return lax.ppermute(array, 'fsdp', [(i, i ^ bit) for i in range(n)])  38.5 us
    dot_general x12, matrix products, contract(): lax.dot_general(left, right, (((left_dim,), (right_dim,)), ((), ())), pre...  16.7 us
    ppermute x20, waiting for transfers between devices, swap(): return lax.ppermute(array, axis, [(0, 1), (1, 0)])  13.7 us
    unnamed x181, local copies, waits for them, and re-layouts  11.3 us
    ppermute x20, starting transfers between devices, swap(): return lax.ppermute(array, axis, [(0, 1), (1, 0)])  7.04 us
    convert_element_type x14, other arithmetic, round_low(): return lax.reduce_precision(values, 8, 7).astype(BF16)  6.99 us
  transfers between devices with their start and end apart: 48, of which 20 were waited for; matrix products, arithmetic and copies ran while one was open for 29% of the time, Pallas kernels for 0%

profile of v2, /device:TPU:0, one launch (start us, length us, event | category | flops | bytes accessed | tf_op | source)
XLA Modules:
  0.0 263.5 jit_solution(353758367456685029)
XLA Ops:
  9.0 3.0 %collective-permute-start.4 = (bf16[136,1024]{1,0:T(8,128)(2,1)S(1)}, bf16[136,1024]{1,0:T(8,128)(2,1)S(1)}, u32[]{:S(2)}, u32[]{:S(2)}) collective-permute-start(bf16[136,1024]{1,0:T(8,128)(2,1)S(1)} %pad_maximum_fusion.10), channel_id=1, source_target_pairs={{0,4},{4,0},{8,12},{12,8},{16,20},{20,16},{24,28},{28,24},{1,5},{5... | collective-permute-start | bytes 835592 | tf_op jit(solution)/shard_map/ppermute | solution.py:32
  12.0 2.6 collective-permute-start.3
  20.5 6.7 %collective-permute-done.3 = bf16[136,1024]{1,0:T(8,128)(2,1)S(1)} collective-permute-done((bf16[136,1024]{1,0:T(8,128)(2,1)S(1)}, bf16[136,1024]{1,0:T(8,128)(2,1)S(1)}, u32[]{:S(2)}, u32[]{:S(2)}) %collective-permute-start.3) | collective-permute-done | bytes 278560 | tf_op jit(solution)/shard_map/ppermute | solution.py:32
  33.9 12.8 %collective-permute-done.9 = bf16[128,1024]{1,0:T(8,128)(2,1)S(1)} collective-permute-done((bf16[128,1024]{1,0:T(8,128)(2,1)S(1)}, bf16[128,1024]{1,0:T(8,128)(2,1)S(1)}, u32[]{:S(2)}, u32[]{:S(2)}) %collective-permute-start.9) | collective-permute-done | bytes 262176 | tf_op jit(solution)/shard_map/ppermute | solution.py:32
  48.2 3.0 %collective-permute-start.15 = (bf16[256,1024]{1,0:T(8,128)(2,1)S(1)}, bf16[256,1024]{1,0:T(8,128)(2,1)}, u32[]{:S(2)}, u32[]{:S(2)}) collective-permute-start(bf16[256,1024]{1,0:T(8,128)(2,1)S(1)} %pad_maximum_fusion.8), channel_id=1, source_target_pairs={{0,8},{4,12},{8,0},{12,4},{16,24},{20,28},{24,16},{28,20},{1,9},{5... | collective-permute-start | bytes 1572872 | tf_op jit(solution)/shard_map/ppermute | solution.py:32
  55.2 12.1 %collective-permute-done.12 = bf16[128,1024]{1,0:T(8,128)(2,1)S(1)} collective-permute-done((bf16[128,1024]{1,0:T(8,128)(2,1)S(1)}, bf16[128,1024]{1,0:T(8,128)(2,1)S(1)}, u32[]{:S(2)}, u32[]{:S(2)}) %collective-permute-start.12) | collective-permute-done | bytes 262176 | tf_op jit(solution)/shard_map/ppermute | solution.py:32
  80.3 2.2 fusion.98
  82.5 2.0 convolution_convert_fusion.1
  93.5 5.8 %collective-permute-done.20 = bf16[160,1024]{1,0:T(8,128)(2,1)S(1)} collective-permute-done((bf16[160,1024]{1,0:T(8,128)(2,1)S(1)}, bf16[160,1024]{1,0:T(8,128)(2,1)S(1)}, u32[]{:S(2)}, u32[]{:S(2)}) %collective-permute-start.20) | collective-permute-done | bytes 327712 | tf_op jit(solution)/shard_map/ppermute | solution.py:27
  115.8 6.9 %collective-permute-done.26 = bf16[160,1024]{1,0:T(8,128)(2,1)S(1)} collective-permute-done((bf16[160,1024]{1,0:T(8,128)(2,1)S(1)}, bf16[160,1024]{1,0:T(8,128)(2,1)S(1)}, u32[]{:S(2)}, u32[]{:S(2)}) %collective-permute-start.26) | collective-permute-done | bytes 327712 | tf_op jit(solution)/shard_map/ppermute | solution.py:27
  126.7 12.9 %collective-permute-done.24 = bf16[512,1024]{1,0:T(8,128)(2,1)} collective-permute-done((bf16[512,1024]{1,0:T(8,128)(2,1)}, bf16[512,1024]{1,0:T(8,128)(2,1)}, u32[]{:S(2)}, u32[]{:S(2)}) %collective-permute-start.24) | collective-permute-done | bytes 1048608 | tf_op jit(solution)/shard_map/ppermute | solution.py:32
  139.6 2.0 convolution_convert_fusion.2
  143.4 2.1 convert_reduce_fusion.3
  153.1 2.3 convert_add_fusion.1
  164.6 6.0 %collective-permute-done.31 = bf16[256,1024]{1,0:T(8,128)(2,1)} collective-permute-done((bf16[256,1024]{1,0:T(8,128)(2,1)}, bf16[256,1024]{1,0:T(8,128)(2,1)}, u32[]{:S(2)}, u32[]{:S(2)}) %collective-permute-start.31) | collective-permute-done | bytes 524320 | tf_op jit(solution)/shard_map/ppermute | solution.py:32
  170.6 6.9 %collective-permute-done.30 = bf16[512,1024]{1,0:T(8,128)(2,1)} collective-permute-done((bf16[512,1024]{1,0:T(8,128)(2,1)}, bf16[512,1024]{1,0:T(8,128)(2,1)}, u32[]{:S(2)}, u32[]{:S(2)}) %collective-permute-start.30) | collective-permute-done | bytes 1048608 | tf_op jit(solution)/shard_map/ppermute | solution.py:32
  188.3 11.8 %collective-permute-done.40 = bf16[128,1024]{1,0:T(8,128)(2,1)S(1)} collective-permute-done((bf16[128,1024]{1,0:T(8,128)(2,1)S(1)}, bf16[128,1024]{1,0:T(8,128)(2,1)S(1)}, u32[]{:S(2)}, u32[]{:S(2)}) %collective-permute-start.40) | collective-permute-done | bytes 262176 | tf_op jit(solution)/shard_map/ppermute | solution.py:32
  204.0 2.2 collective-permute-start.43
  207.8 2.2 fusion.30
  210.0 4.0 %concatenate.162 = f32[1024]{0:T(1024)S(1)} concatenate(f32[256]{0:T(256)S(1)} %copy-done.67, f32[256]{0:T(256)S(1)} %copy-done.66, f32[1]{0:T(128)} %bitcast.48, f32[1]{0:T(128)} %bitcast.49, f32[1]{0:T(128)} %bitcast.50, f32[1]{0:T(128)} %bitcast.51, f32[1]{0:T(128)} %bitcast.52, f32[1]{0:T(128)} %bitcast.53, f32[506]{0:T(512)S(1)} %broadcast_in_dim.78), dimensions={0} | concatenate | bytes 8192 | tf_op jit(solution)/shard_map/concatenate | solution.py:372
  215.6 2.0 fusion.19
  225.4 7.2 %collective-permute-done.35 = f32[8,1024]{1,0:T(8,128)S(1)} collective-permute-done((f32[8,1024]{1,0:T(8,128)S(1)}, f32[8,1024]{1,0:T(8,128)S(1)}, u32[]{:S(2)}, u32[]{:S(2)}) %collective-permute-start.35) | collective-permute-done | bytes 32800 | tf_op jit(solution)/shard_map/ppermute | solution.py:32
  234.4 3.1 %collective-permute-done.36 = f32[8,1024]{1,0:T(8,128)S(1)} collective-permute-done((f32[8,1024]{1,0:T(8,128)S(1)}, f32[8,1024]{1,0:T(8,128)S(1)}, u32[]{:S(2)}, u32[]{:S(2)}) %collective-permute-start.36) | collective-permute-done | bytes 32800 | tf_op jit(solution)/shard_map/ppermute | solution.py:32
  246.2 13.0 %collective-permute-done.44 = bf16[128,1024]{1,0:T(8,128)(2,1)S(1)} collective-permute-done((bf16[128,1024]{1,0:T(8,128)(2,1)S(1)}, bf16[128,1024]{1,0:T(8,128)(2,1)S(1)}, u32[]{:S(2)}, u32[]{:S(2)}) %collective-permute-start.44) | collective-permute-done | bytes 262176 | tf_op jit(solution)/shard_map/ppermute | solution.py:32
  (433 shorter events, 125.1 us)
Async XLA Ops:
  12.0 15.2 %collective-permute-start.3 = (bf16[136,1024]{1,0:T(8,128)(2,1)S(1)}, bf16[136,1024]{1,0:T(8,128)(2,1)S(1)}, u32[]{:S(2)}, u32[]{:S(2)}) collective-permute-start(bf16[136,1024]{1,0:T(8,128)(2,1)S(1)} %pad_maximum_fusion.10), channel_id=1, source_target_pairs={{0,16},{4,20},{8,24},{12,28},{16,0},{20,4},{24,8},{28,12},{1,17},{... | collective-permute-start | bytes 835592 | tf_op jit(solution)/shard_map/ppermute | solution.py:32
  18.6 15.3 %collective-permute-start.21 = (bf16[160,1024]{1,0:T(8,128)(2,1)S(1)}, bf16[160,1024]{1,0:T(8,128)(2,1)S(1)}, u32[]{:S(2)}, u32[]{:S(2)}) collective-permute-start(bf16[160,1024]{1,0:T(8,128)(2,1)S(1)} %bitcast.226), channel_id=1, source_target_pairs={{0,2},{2,0},{1,3},{3,1},{4,6},{6,4},{5,7},{7,5},{8,10},{10,8},{9,1... | collective-permute-start | bytes 983048 | tf_op jit(solution)/shard_map/ppermute | solution.py:27
  28.1 19.5 %collective-permute-start.8 = (bf16[272,1024]{1,0:T(8,128)(2,1)S(1)}, bf16[272,1024]{1,0:T(8,128)(2,1)S(1)}, u32[]{:S(2)}, u32[]{:S(2)}) collective-permute-start(bf16[272,1024]{1,0:T(8,128)(2,1)S(1)} %pad_maximum_fusion.7), channel_id=1, source_target_pairs={{0,8},{4,12},{8,0},{12,4},{16,24},{20,28},{24,16},{28,20},{1,9},{5... | collective-permute-start | bytes 1671176 | tf_op jit(solution)/shard_map/ppermute | solution.py:32
  30.1 16.6 %collective-permute-start.10 = (bf16[136,1024]{1,0:T(8,128)(2,1)S(1)}, bf16[136,1024]{1,0:T(8,128)(2,1)S(1)}, u32[]{:S(2)}, u32[]{:S(2)}) collective-permute-start(bf16[136,1024]{1,0:T(8,128)(2,1)S(1)} %collective-permute-done.3), channel_id=1, source_target_pairs={{0,4},{4,0},{8,12},{12,8},{16,20},{20,16},{24,28},{28,24},{1,5},{5... | collective-permute-start | bytes 835592 | tf_op jit(solution)/shard_map/ppermute | solution.py:32
  30.7 16.0 %collective-permute-start.9 = (bf16[128,1024]{1,0:T(8,128)(2,1)S(1)}, bf16[128,1024]{1,0:T(8,128)(2,1)S(1)}, u32[]{:S(2)}, u32[]{:S(2)}) collective-permute-start(bf16[128,1024]{1,0:T(8,128)(2,1)S(1)} %maximum_select_fusion.4), channel_id=1, source_target_pairs={{0,16},{4,20},{8,24},{12,28},{16,0},{20,4},{24,8},{28,12},{1,17},{... | collective-permute-start | bytes 786440 | tf_op jit(solution)/shard_map/ppermute | solution.py:32
  32.3 14.4 %collective-permute-start.11 = (bf16[128,1024]{1,0:T(8,128)(2,1)S(1)}, bf16[128,1024]{1,0:T(8,128)(2,1)S(1)}, u32[]{:S(2)}, u32[]{:S(2)}) collective-permute-start(bf16[128,1024]{1,0:T(8,128)(2,1)S(1)} %maximum_select_fusion.5), channel_id=1, source_target_pairs={{0,4},{4,0},{8,12},{12,8},{16,20},{20,16},{24,28},{28,24},{1,5},{5... | collective-permute-start | bytes 786440 | tf_op jit(solution)/shard_map/ppermute | solution.py:32
  47.6 19.7 %collective-permute-start.14 = (bf16[128,1024]{1,0:T(8,128)(2,1)S(1)}, bf16[128,1024]{1,0:T(8,128)(2,1)S(1)}, u32[]{:S(2)}, u32[]{:S(2)}) collective-permute-start(bf16[128,1024]{1,0:T(8,128)(2,1)S(1)} %collective-permute-done.9), channel_id=1, source_target_pairs={{0,4},{4,0},{8,12},{12,8},{16,20},{20,16},{24,28},{28,24},{1,5},{5... | collective-permute-start | bytes 786440 | tf_op jit(solution)/shard_map/ppermute | solution.py:32
  48.2 19.9 %collective-permute-start.15 = (bf16[256,1024]{1,0:T(8,128)(2,1)S(1)}, bf16[256,1024]{1,0:T(8,128)(2,1)}, u32[]{:S(2)}, u32[]{:S(2)}) collective-permute-start(bf16[256,1024]{1,0:T(8,128)(2,1)S(1)} %pad_maximum_fusion.8), channel_id=1, source_target_pairs={{0,8},{4,12},{8,0},{12,4},{16,24},{20,28},{24,16},{28,20},{1,9},{5... | collective-permute-start | bytes 1572872 | tf_op jit(solution)/shard_map/ppermute | solution.py:32
  51.1 17.0 %collective-permute-start.13 = (bf16[272,1024]{1,0:T(8,128)(2,1)S(1)}, bf16[272,1024]{1,0:T(8,128)(2,1)S(1)}, u32[]{:S(2)}, u32[]{:S(2)}) collective-permute-start(bf16[272,1024]{1,0:T(8,128)(2,1)S(1)} %collective-permute-done.8), channel_id=1, source_target_pairs={{0,4},{4,0},{8,12},{12,8},{16,20},{20,16},{24,28},{28,24},{1,5},{5... | collective-permute-start | bytes 1671176 | tf_op jit(solution)/shard_map/ppermute | solution.py:32
  68.1 18.1 %collective-permute-start.18 = (bf16[128,1024]{1,0:T(8,128)(2,1)S(1)}, bf16[128,1024]{1,0:T(8,128)(2,1)}, u32[]{:S(2)}, u32[]{:S(2)}) collective-permute-start(bf16[128,1024]{1,0:T(8,128)(2,1)S(1)} %collective-permute-done.12), channel_id=1, source_target_pairs={{0,4},{4,0},{8,12},{12,8},{16,20},{20,16},{24,28},{28,24},{1,5},{5... | collective-permute-start | bytes 786440 | tf_op jit(solution)/shard_map/ppermute | solution.py:32
  90.8 14.3 %collective-permute-start.22 = (bf16[256,1024]{1,0:T(8,128)(2,1)}, bf16[256,1024]{1,0:T(8,128)(2,1)S(1)}, u32[]{:S(2)}, u32[]{:S(2)}) collective-permute-start(bf16[256,1024]{1,0:T(8,128)(2,1)} %collective-permute-done.16), channel_id=1, source_target_pairs={{0,4},{4,0},{8,12},{12,8},{16,20},{20,16},{24,28},{28,24},{1,5},{5... | collective-permute-start | bytes 1572872 | tf_op jit(solution)/shard_map/ppermute | solution.py:32
  114.3 25.3 %collective-permute-start.24 = (bf16[512,1024]{1,0:T(8,128)(2,1)}, bf16[512,1024]{1,0:T(8,128)(2,1)}, u32[]{:S(2)}, u32[]{:S(2)}) collective-permute-start(bf16[512,1024]{1,0:T(8,128)(2,1)} %reduce-precision_convert_fusion.1), channel_id=1, source_target_pairs={{0,4},{4,0},{8,12},{12,8},{16,20},{20,16},{24,28},{28,24},{1,5},{5... | collective-permute-start | bytes 3145736 | tf_op jit(solution)/shard_map/ppermute | solution.py:32
  151.5 33.5 %collective-permute-start.28 = (bf16[160,1024]{1,0:T(8,128)(2,1)}, bf16[160,1024]{1,0:T(8,128)(2,1)}, u32[]{:S(2)}, u32[]{:S(2)}) collective-permute-start(bf16[160,1024]{1,0:T(8,128)(2,1)} %fusion.31), channel_id=1, source_target_pairs={{0,2},{2,0},{1,3},{3,1},{4,6},{6,4},{5,7},{7,5},{8,10},{10,8},{9,1... | collective-permute-start | bytes 983048 | tf_op jit(solution)/shard_map/ppermute | solution.py:27
  151.6 25.9 %collective-permute-start.30 = (bf16[512,1024]{1,0:T(8,128)(2,1)}, bf16[512,1024]{1,0:T(8,128)(2,1)}, u32[]{:S(2)}, u32[]{:S(2)}) collective-permute-start(bf16[512,1024]{1,0:T(8,128)(2,1)} %reduce-precision_convert_fusion), channel_id=1, source_target_pairs={{0,4},{4,0},{8,12},{12,8},{16,20},{20,16},{24,28},{28,24},{1,5},{5... | collective-permute-start | bytes 3145736 | tf_op jit(solution)/shard_map/ppermute | solution.py:32
  181.0 19.2 %collective-permute-start.38 = (bf16[256,1024]{1,0:T(8,128)(2,1)S(1)}, bf16[256,1024]{1,0:T(8,128)(2,1)S(1)}, u32[]{:S(2)}, u32[]{:S(2)}) collective-permute-start(bf16[256,1024]{1,0:T(8,128)(2,1)S(1)} %slice.439), channel_id=1, source_target_pairs={{0,4},{4,0},{8,12},{12,8},{16,20},{20,16},{24,28},{28,24},{1,5},{5... | collective-permute-start | bytes 1572872 | tf_op jit(solution)/shard_map/ppermute | solution.py:32
  182.5 19.6 %collective-permute-start.39 = (bf16[256,1024]{1,0:T(8,128)(2,1)S(1)}, bf16[256,1024]{1,0:T(8,128)(2,1)S(1)}, u32[]{:S(2)}, u32[]{:S(2)}) collective-permute-start(bf16[256,1024]{1,0:T(8,128)(2,1)S(1)} %fusion.20), channel_id=1, source_target_pairs={{0,8},{4,12},{8,0},{12,4},{16,24},{20,28},{24,16},{28,20},{1,9},{5... | collective-permute-start | bytes 1572872 | tf_op jit(solution)/shard_map/ppermute | solution.py:32
  183.0 17.1 %collective-permute-start.40 = (bf16[128,1024]{1,0:T(8,128)(2,1)S(1)}, bf16[128,1024]{1,0:T(8,128)(2,1)S(1)}, u32[]{:S(2)}, u32[]{:S(2)}) collective-permute-start(bf16[128,1024]{1,0:T(8,128)(2,1)S(1)} %fusion.41), channel_id=1, source_target_pairs={{0,16},{4,20},{8,24},{12,28},{16,0},{20,4},{24,8},{28,12},{1,17},{... | collective-permute-start | bytes 786440 | tf_op jit(solution)/shard_map/ppermute | solution.py:32
  186.1 21.7 %collective-permute-start.29 = (bf16[160,1024]{1,0:T(8,128)(2,1)S(1)}, bf16[160,1024]{1,0:T(8,128)(2,1)S(1)}, u32[]{:S(2)}, u32[]{:S(2)}) collective-permute-start(bf16[160,1024]{1,0:T(8,128)(2,1)S(1)} %fusion.33), channel_id=1, source_target_pairs={{0,1},{1,0},{2,3},{3,2},{4,5},{5,4},{6,7},{7,6},{8,9},{9,8},{10,11... | collective-permute-start | bytes 983048 | tf_op jit(solution)/shard_map/ppermute | solution.py:27
  187.7 19.5 %collective-permute-start.33 = (bf16[160,1024]{1,0:T(8,128)(2,1)S(1)}, bf16[160,1024]{1,0:T(8,128)(2,1)S(1)}, u32[]{:S(2)}, u32[]{:S(2)}) collective-permute-start(bf16[160,1024]{1,0:T(8,128)(2,1)S(1)} %reduce-precision_convert_fusion.3), channel_id=1, source_target_pairs={{0,1},{1,0},{2,3},{3,2},{4,5},{5,4},{6,7},{7,6},{8,9},{9,8},{10,11... | collective-permute-start | bytes 983048 | tf_op jit(solution)/shard_map/ppermute | solution.py:27
  204.0 38.6 %collective-permute-start.43 = (bf16[128,1024]{1,0:T(8,128)(2,1)}, bf16[128,1024]{1,0:T(8,128)(2,1)}, u32[]{:S(2)}, u32[]{:S(2)}) collective-permute-start(bf16[128,1024]{1,0:T(8,128)(2,1)} %fusion.40), channel_id=1, source_target_pairs={{0,16},{4,20},{8,24},{12,28},{16,0},{20,4},{24,8},{28,12},{1,17},{... | collective-permute-start | bytes 786440 | tf_op jit(solution)/shard_map/ppermute | solution.py:32
  207.3 30.4 %collective-permute-start.47 = (f32[64,1024]{1,0:T(8,128)}, f32[64,1024]{1,0:T(8,128)}, u32[]{:S(2)}, u32[]{:S(2)}) collective-permute-start(f32[64,1024]{1,0:T(8,128)} %get-tuple-element.235), channel_id=1, source_target_pairs={{0,2},{2,0},{1,3},{3,1},{4,6},{6,4},{5,7},{7,5},{8,10},{10,8},{9,1... | collective-permute-start | bytes 786440 | tf_op jit(solution)/shard_map/ppermute | solution.py:27
  217.6 25.0 %collective-permute-start.42 = (bf16[256,1024]{1,0:T(8,128)(2,1)}, bf16[256,1024]{1,0:T(8,128)(2,1)}, u32[]{:S(2)}, u32[]{:S(2)}) collective-permute-start(bf16[256,1024]{1,0:T(8,128)(2,1)} %fusion.19), channel_id=1, source_target_pairs={{0,8},{4,12},{8,0},{12,4},{16,24},{20,28},{24,16},{28,20},{1,9},{5... | collective-permute-start | bytes 1572872 | tf_op jit(solution)/shard_map/ppermute | solution.py:32
  217.8 24.8 %collective-permute-start.41 = (bf16[256,1024]{1,0:T(8,128)(2,1)}, bf16[256,1024]{1,0:T(8,128)(2,1)}, u32[]{:S(2)}, u32[]{:S(2)}) collective-permute-start(bf16[256,1024]{1,0:T(8,128)(2,1)} %slice.444), channel_id=1, source_target_pairs={{0,4},{4,0},{8,12},{12,8},{16,20},{20,16},{24,28},{28,24},{1,5},{5... | collective-permute-start | bytes 1572872 | tf_op jit(solution)/shard_map/ppermute | solution.py:32
  244.2 14.9 %collective-permute-start.44 = (bf16[128,1024]{1,0:T(8,128)(2,1)S(1)}, bf16[128,1024]{1,0:T(8,128)(2,1)S(1)}, u32[]{:S(2)}, u32[]{:S(2)}) collective-permute-start(bf16[128,1024]{1,0:T(8,128)(2,1)S(1)} %fusion.39), channel_id=1, source_target_pairs={{0,16},{4,20},{8,24},{12,28},{16,0},{20,4},{24,8},{28,12},{1,17},{... | collective-permute-start | bytes 786440 | tf_op jit(solution)/shard_map/ppermute | solution.py:32
  (99 other events, 883.8 us)

commit v3 on v2

v3 whole, which is shorter than its diff:
```python
import jax
import jax.numpy as jnp
from jax import lax
from jax.experimental import pallas as pl
from jax.experimental.pallas import tpu as pltpu
from jax.sharding import PartitionSpec as P

D = 1024
HD = 64
EPSILON = 1e-06
MASK_FILL = -1e30
ROOT_HALF = 0.7071067811865476
INV_ROOT_TWO_PI = 0.3989422804014327
F32 = jnp.float32
BF16 = jnp.bfloat16


def contract(left, right, left_dim, right_dim):
    return lax.dot_general(
        left, right, (((left_dim,), (right_dim,)), ((), ())), preferred_element_type=F32
    )


def round_low(values):
    return lax.reduce_precision(values, 8, 7).astype(BF16)


def swap(array, axis):
    return lax.ppermute(array, axis, [(0, 1), (1, 0)])


def flip(array, bit):
    n = lax.axis_size("fsdp")
    return lax.ppermute(array, "fsdp", [(i, i ^ bit) for i in range(n)])


X_BIT, NEAR_BIT, FAR_BIT = 1, 2, 4


def is_cube():
    return lax.axis_size("fsdp") == 8


def turned_bits(blocks):
    return (blocks % 2) * 4 + (blocks // 2 % 2) * 2 + blocks // 4


def relative_blocks():
    spots = jnp.arange(lax.axis_size("fsdp"), dtype=jnp.int32)
    if not is_cube():
        return spots
    return turned_bits(spots ^ lax.axis_index("fsdp"))


def absolute_places():
    blocks = jnp.arange(lax.axis_size("fsdp"), dtype=jnp.int32)
    if not is_cube():
        return blocks
    return turned_bits(blocks) ^ lax.axis_index("fsdp")


def tie(*values):
    return lax.optimization_barrier(values)


def rows_of(*pieces):
    return jnp.concatenate(pieces, axis=0)


def upper(array):
    return array[array.shape[0] // 2 :]


def lower(array):
    return array[: array.shape[0] // 2]


def scatter_sum(partial):
    low = round_low(partial)
    return lax.psum_scatter(low, "fsdp", scatter_dimension=0, tiled=True).astype(F32)


def low_cost():
    return pl.CostEstimate(flops=1000, transcendentals=0, bytes_accessed=1000)


def probabilities(query, key, mask):
    scores = contract(query, key, 1, 1) * (HD ** (-0.5))
    scores = jnp.where(mask > 0, scores, MASK_FILL)
    raised = jnp.exp(scores - jnp.max(scores, axis=-1, keepdims=True))
    return raised / jnp.sum(raised, axis=-1, keepdims=True)


def spans_of(pieces, block, pitch):
    spans, row = [], 0
    for index, piece in enumerate(pieces):
        for start in range(0, piece.shape[0], pitch):
            spans.append((index, start, row))
            row += block
    return spans


def merged(spans, block, pitch):
    if block != pitch:
        return [(index, start, row, block) for index, start, row in spans]
    joined = []
    for index, start, row in spans:
        if joined and joined[-1][0] == index:
            last = joined[-1]
            joined[-1] = (index, last[1], last[2], last[3] + block)
        else:
            joined.append((index, start, row, block))
    return joined


def times_pieces(left, pieces, spans, columns):
    total = None
    for index, start, row, size in spans:
        part = jnp.dot(
            left[:, row : row + size],
            pieces[index][start : start + size, columns],
            preferred_element_type=F32,
        )
        total = part if total is None else total + part
    return total


def times_pieces_back(left, pieces, spans, columns, own, other):
    half = own.shape[0]
    for index, start, row, size in spans:
        weight = pieces[index][start : start + size, columns]
        own[:, row : row + size] = contract(left[:half, :], weight, 1, 1)
        other[:, row : row + size] = contract(left[half:, :], weight, 1, 1).astype(BF16)


def shape_of(rows, columns, dtype):
    return jax.ShapeDtypeStruct((rows, columns), dtype)


def stacked(refs):
    return jnp.concatenate([ref[...] for ref in refs], axis=0)


def read_small(blocks, block, width, places_ref, relative, absolute):
    for index, (ref, start) in enumerate(blocks):
        lines = [
            ref[
                start + block + vector // 8 : start + block + vector // 8 + 1,
                vector % 8 * width : (vector % 8 + 1) * width,
            ]
            for vector in range(16)
        ]
        values = jnp.concatenate(lines, axis=0).astype(F32)
        relative[:, index * width : (index + 1) * width] = values
        to = pl.ds(pl.multiple_of(places_ref[index] * width, 128), width)
        absolute[:, to] = values


def attention(normal, vectors, bias, mask, pieces, block, pitch, places):
    slots, model = normal.shape
    width = pieces[0].shape[1] // 4
    half = slots // 2
    all_spans = spans_of(pieces, block, pitch)
    spans = merged(all_spans, block, pitch)
    given = [] if vectors is None else [vectors, bias]

    def kernel(places_ref, normal_ref, mask_ref, *refs):
        weights = refs[: len(pieces)]
        query, key, value, context, own, other, normed = refs[len(pieces) + len(given) :][:7]
        if given:
            small, own_bias = refs[len(pieces) : len(pieces) + 2]
            query_bias, value_bias = own_bias[0:1, :], own_bias[1:2, :]
        else:
            small, absolute = refs[-2:]
            blocks = [(weights[index], start) for index, start, _ in all_spans]
            read_small(blocks, block, model // len(blocks), places_ref, small, absolute)
            at = pl.multiple_of(places_ref[len(blocks)] * width, 128)
            query_bias = absolute[6:7, pl.ds(at, width)]
            value_bias = absolute[6:7, pl.ds(at + 2 * width, width)]
        normed[...] = (normal_ref[...] * small[0:1, :] + small[1:2, :]).astype(BF16)
        packed = times_pieces(normed, weights, spans, slice(0, 3 * width))
        query[...] = (packed[:, :width] + query_bias).astype(BF16)
        key[...] = packed[:, width : 2 * width].astype(BF16)
        value[...] = (packed[:, 2 * width :] + value_bias).astype(BF16)
        valid = mask_ref[...]
        parts = []
        for head in range(width // HD):
            at = slice(head * HD, (head + 1) * HD)
            prob = probabilities(query[:, at], key[:, at], valid)
            parts.append(jnp.dot(prob.astype(BF16), value[:, at], preferred_element_type=F32))
        context[...] = jnp.concatenate(parts, axis=1).astype(BF16)
        times_pieces_back(context, weights, spans, slice(3 * width, 4 * width), own, other)

    in_vmem = pl.BlockSpec(memory_space=pltpu.VMEM)
    small_shape = [] if given else [shape_of(16, model, F32)] * 2
    out_shape = (
        [shape_of(slots, width, BF16)] * 4
        + [shape_of(half, model, F32), shape_of(half, model, BF16), shape_of(slots, model, BF16)]
        + small_shape
    )
    return pl.pallas_call(
        kernel,
        name="attention",
        in_specs=[pl.BlockSpec(memory_space=pltpu.SMEM)]
        + [in_vmem] * (2 + len(pieces) + len(given)),
        out_specs=[in_vmem] * len(out_shape),
        out_shape=out_shape,
        cost_estimate=low_cost(),
    )(places, normal, mask, *pieces, *given)


def attention_back(grad_att, context, mask, query, key, value, pieces, block, pitch):
    slots, width = context.shape
    model = grad_att[0].shape[1]
    half = slots // 2
    scale = HD ** (-0.5)
    spans = merged(spans_of(pieces, block, pitch), block, pitch)

    def kernel(grad_own, grad_other, context_ref, mask_ref, query_ref, key_ref, value_ref, *refs):
        weights = refs[: len(pieces)]
        packed_own, packed_other, own, other, bias_sum, packed = refs[len(pieces) :]
        grad_ref = stacked((grad_own, grad_other))
        valid = mask_ref[...]
        grad_context = times_pieces(
            grad_ref, weights, spans, slice(3 * width, 4 * width)
        ).astype(BF16)
        queries, keys, values = [], [], []
        for head in range(width // HD):
            at = slice(head * HD, (head + 1) * HD)
            q, k, v, g = query_ref[:, at], key_ref[:, at], value_ref[:, at], grad_context[:, at]
            prob = probabilities(q, k, valid)
            grad_prob = contract(g, v, 1, 1)
            dots = jnp.sum(prob * grad_prob, axis=-1, keepdims=True)
            grad_scores = (prob * (grad_prob - dots)).astype(BF16)
            queries.append(jnp.dot(grad_scores, k, preferred_element_type=F32) * scale)
            keys.append(contract(grad_scores, q, 0, 0) * scale)
            values.append(contract(prob.astype(BF16), g, 0, 0))
        for kind, parts in enumerate((queries, keys, values)):
            joined = jnp.concatenate(parts, axis=1).astype(BF16)
            packed[:, kind * width : (kind + 1) * width] = joined
            if kind != 1:
                at = (kind // 2) * width
                bias_sum[:, at : at + width] = jnp.sum(joined.astype(F32), axis=0, keepdims=True)
        packed[:, 3 * width :] = context_ref[...]
        packed_own[...] = packed[:half, :]
        packed_other[...] = packed[half:, :]
        grads = packed.at[:, : 3 * width]
        times_pieces_back(grads, weights, spans, slice(0, 3 * width), own, other)

    return pl.pallas_call(
        kernel,
        name="attention_back",
        out_shape=[
            shape_of(half, 4 * width, BF16),
            shape_of(half, 4 * width, BF16),
            shape_of(half, model, F32),
            shape_of(half, model, BF16),
            shape_of(1, 2 * width, F32),
        ],
        scratch_shapes=[pltpu.VMEM((slots, 4 * width), BF16)],
        cost_estimate=low_cost(),
    )(*grad_att, context, mask, query, key, value, *pieces)


def hidden_layer(own, other, normed, bias, pieces, block):
    half, model = own.shape
    slots, hidden = 2 * half, bias.shape[1]
    spans = merged(spans_of(pieces, block, block), block, block)

    def kernel(own_ref, other_ref, normed_ref, bias_ref, *refs):
        message, slope = refs[len(pieces) :]
        left = stacked((own_ref, other_ref))
        pre_act = times_pieces(left, refs[: len(pieces)], spans, slice(0, hidden))
        pre_act = pre_act + bias_ref[...]
        cumulative = 0.5 * (1.0 + lax.erf(pre_act * ROOT_HALF))
        message[:slots, :] = (pre_act * cumulative).astype(BF16)
        message[slots:, : model // 2] = normed_ref[:half, model // 2 :]
        message[slots:, model // 2 :] = own_ref[:, model // 2 :]
        slope[...] = cumulative + pre_act * (
            INV_ROOT_TWO_PI * jnp.exp(-0.5 * pre_act * pre_act)
        )

    return pl.pallas_call(
        kernel,
        name="hidden_layer",
        out_shape=[shape_of(slots + half, hidden, BF16), shape_of(slots, hidden, F32)],
        cost_estimate=low_cost(),
    )(own, other, normed, bias, *pieces)


def hidden_back(grads, slope, up_pieces, down_pieces, block):
    model = grads[0].shape[1]
    slots, hidden = slope.shape
    half = slots // 2
    spans = merged(spans_of(up_pieces, block, block), block, block)
    down_spans = merged(spans_of(down_pieces, block, block), block, block)
    count = len(up_pieces)
    total = count + len(down_pieces)

    def kernel(grad_own, grad_other, slope_ref, *refs):
        grad_ref = stacked((grad_own, grad_other))
        up, down = refs[:count], refs[count:total]
        grad_pre, own, other, bias_sum = refs[total:]
        grad_active = times_pieces(grad_ref, down, down_spans, slice(0, hidden))
        low = (grad_active * slope_ref[...]).astype(BF16)
        grad_pre[...] = low
        bias_sum[...] = jnp.sum(low.astype(F32), axis=0, keepdims=True)
        times_pieces_back(grad_pre, up, spans, slice(0, hidden), own, other)

    return pl.pallas_call(
        kernel,
        name="hidden_back",
        out_shape=[
            shape_of(slots, hidden, BF16),
            shape_of(half, model, F32),
            shape_of(half, model, BF16),
            shape_of(1, hidden, F32),
        ],
        cost_estimate=low_cost(),
    )(*grads, slope, *up_pieces, *down_pieces)


def project_back(values, slots, pieces, block):
    columns = values.shape[1]
    spans = merged(spans_of(pieces, block, block), block, block)
    half = slots // 2

    def kernel(values_ref, *refs):
        left = values_ref.at[:slots, :]
        times_pieces_back(left, refs[: len(pieces)], spans, slice(0, columns), refs[-2], refs[-1])

    return pl.pallas_call(
        kernel,
        name="project_back",
        out_shape=[shape_of(half, D, F32), shape_of(half, D, BF16)],
        cost_estimate=low_cost(),
    )(values, *pieces)


def weight_grad(groups, rights, parts):
    columns = rights[0][0].shape[1]
    cut = D // 4
    arrays, index_of = [], {}

    def index(array):
        if id(array) not in index_of:
            index_of[id(array)] = len(arrays)
            arrays.append(array)
        return index_of[id(array)]

    right_rows = [(index(array), row, count) for array, row, count in rights]
    left_rows = [
        ([(index(array), row, count, column) for array, row, count, column in lefts], lo, hi)
        for lefts, lo, hi in groups
    ]
    size = cut // parts

    def kernel(*refs):
        outs = refs[len(arrays) :]
        targets = [(outs[part], cut + part * size) for part in range(parts)] + [(outs[-1], 0)]
        for lefts, lo, hi in left_rows:
            right = jnp.concatenate(
                [refs[at][row : row + count, lo:hi] for at, row, count in right_rows], axis=0
            )
            for target, first in targets:
                left = jnp.concatenate(
                    [
                        refs[at][row : row + count, column + first : column + first + target.shape[0]]
                        for at, row, count, column in lefts
                    ],
                    axis=0,
                )
                target[:, lo:hi] = contract(left, right, 0, 0).astype(target.dtype)

    return pl.pallas_call(
        kernel,
        name="weight_grad",
        out_shape=[shape_of(size, columns, BF16)] * parts + [shape_of(cut, columns, F32)],
        cost_estimate=low_cost(),
    )(*arrays)


def norm_of(values):
    mean = jnp.mean(values, axis=-1, keepdims=True)
    centered = values - mean
    scale = lax.rsqrt(jnp.mean(centered * centered, axis=-1, keepdims=True) + EPSILON)
    return centered * scale, scale


def valid_rows(rows, places_ref):
    slot = lax.broadcasted_iota(jnp.int32, (rows, 1), 0) + places_ref[places_ref.shape[0] - 2]
    return (slot < places_ref[places_ref.shape[0] - 1]).astype(F32)


def assemble(mine, theirs, places):
    rows, columns = mine.shape
    width = columns // 4
    last = places.shape[0] - 3

    def kernel(places_ref, mine_ref, theirs_ref, three, fourth):
        core = places_ref[last]
        for source, half in ((mine_ref, core), (theirs_ref, 1 - core)):
            to = pl.ds(pl.multiple_of(half * width, 128), width)
            for kind in range(3):
                three[:, kind, to] = source[:, kind * width : (kind + 1) * width]
            fourth[:, to] = source[:, 3 * width :]

    in_vmem = pl.BlockSpec(memory_space=pltpu.VMEM)
    return pl.pallas_call(
        kernel,
        name="assemble",
        in_specs=[pl.BlockSpec(memory_space=pltpu.SMEM)] + [in_vmem] * 2,
        out_specs=[in_vmem] * 2,
        out_shape=[
            jax.ShapeDtypeStruct((rows, 3, 2 * width), F32),
            shape_of(rows, 2 * width, F32),
        ],
        cost_estimate=low_cost(),
    )(places, mine, theirs)


def norm_grad(normal, scale, gain, grad):
    weighted = grad * gain
    return scale * (
        weighted
        - jnp.mean(weighted, axis=-1, keepdims=True)
        - normal * jnp.mean(weighted * normal, axis=-1, keepdims=True)
    )


def column_sum(values):
    return jnp.sum(values, axis=0, keepdims=True)


def second_norm_back(middle, gain, low, other_low, grad_res):
    rows, model = middle.shape

    def kernel(middle_ref, gain_ref, low_ref, other_ref, res_ref, *outs):
        grad_middle, grad_att, sums = outs
        grad = low_ref[...].astype(F32) + other_ref[...].astype(F32)
        res = res_ref[...].astype(F32)
        n, scale = norm_of(middle_ref[...])
        total = res + norm_grad(n, scale, gain_ref[...], grad)
        grad_middle[...] = total
        rounded = total.astype(BF16)
        grad_att[...] = rounded
        sums[0:1, :] = column_sum(rounded.astype(F32))
        sums[1:2, :] = column_sum(grad * n)
        sums[2:3, :] = column_sum(grad)
        sums[3:4, :] = column_sum(res)

    return pl.pallas_call(
        kernel,
        name="second_norm_back",
        out_shape=[
            shape_of(rows, model, F32),
            shape_of(rows, model, BF16),
            shape_of(4, model, F32),
        ],
        cost_estimate=low_cost(),
    )(middle, gain, low, other_low, grad_res)


def place_blocks(target, rows, values, places_ref):
    count = places_ref.shape[0] - 3
    width = values.shape[1] // count
    if width % 128:
        target[rows, :] = values
        return
    for block in range(count):
        to = pl.ds(pl.multiple_of(places_ref[block] * width, 128), width)
        target[rows, to] = values[:, block * width : (block + 1) * width]


def finish(middle, entering, attended, low, other_low, bias, places):
    rows, model = middle.shape

    def kernel(
        places_ref, middle_ref, entering_ref, attended_ref, low_ref, other_ref, bias_ref,
        output, stats
    ):
        branch = low_ref[...].astype(F32) + other_ref[...].astype(F32) + bias_ref[...]
        result = middle_ref[...] + branch
        place_blocks(output, slice(None), result.astype(BF16), places_ref)
        good = valid_rows(rows, places_ref)
        lane = lax.broadcasted_iota(jnp.int32, (1, 128), 1)
        row = jnp.where(lane == 5, column_sum(good), 0.0)
        terms = (entering_ref[...], attended_ref[...], middle_ref[...], branch, result)
        for index, term in enumerate(terms):
            total = jnp.sum(column_sum(term * term * good), axis=1, keepdims=True)
            row = jnp.where(lane == index, total, row)
        stats[...] = row

    in_vmem = pl.BlockSpec(memory_space=pltpu.VMEM)
    return pl.pallas_call(
        kernel,
        name="finish",
        in_specs=[pl.BlockSpec(memory_space=pltpu.SMEM)] + [in_vmem] * 6,
        out_specs=[in_vmem] * 2,
        out_shape=[shape_of(rows, model, BF16), shape_of(1, 128, F32)],
        cost_estimate=low_cost(),
    )(places, middle, entering, attended, low, other_low, bias)


def first_norm_back(
    inputs, gain, low, other_low, grad_middle, sums, up_sum, qv_sum, stats, places
):
    rows, model = inputs.shape

    def kernel(
        places_ref, inputs_ref, gain_ref, low_ref, other_ref, middle_ref,
        sums_ref, up_ref, qv_ref, stats_ref, grad_inputs, message
    ):
        grad = low_ref[...].astype(F32) + other_ref[...].astype(F32)
        valid = valid_rows(rows, places_ref)
        n, scale = norm_of(inputs_ref[...].astype(F32) * valid)
        total = middle_ref[...] + norm_grad(n, scale, gain_ref[...], grad)
        total = total * valid
        vectors = jnp.concatenate(
            [column_sum(grad * n), column_sum(grad), sums_ref[...]], axis=0
        )
        message[6:7, :] = up_ref[...]
        message[7:8, :] = jnp.zeros((1, model), F32)
        message[7:8, : qv_ref.shape[1]] = qv_ref[...]
        message[7:8, model - 128 :] = stats_ref[...]
        place_blocks(grad_inputs, slice(None), total, places_ref)
        place_blocks(message, slice(0, 6), vectors, places_ref)

    in_vmem = pl.BlockSpec(memory_space=pltpu.VMEM)
    return pl.pallas_call(
        kernel,
        name="first_norm_back",
        in_specs=[pl.BlockSpec(memory_space=pltpu.SMEM)] + [in_vmem] * 9,
        out_specs=[in_vmem] * 2,
        out_shape=[shape_of(rows, model, F32), shape_of(8, model, F32)],
        cost_estimate=low_cost(),
    )(
        places, inputs, gain, low, other_low, grad_middle, sums, up_sum, qv_sum, stats
    )


def halves_low(own, other):
    low = round_low(own + swap(other, "ctx").astype(F32))
    return low, swap(low, "tp")


def halves_sum(own, other):
    low = round_low(own + swap(other, "ctx").astype(F32))
    return low.astype(F32) + swap(low, "tp").astype(F32)


def coded(values):
    high = lax.reduce_precision(values, 8, 7)
    return rows_of(high.astype(BF16), round_low(values - high))


def decoded(rows):
    return lower(rows).astype(F32) + upper(rows).astype(F32)


def with_other(own):
    return jnp.concatenate([own, swap(own, "ctx")], axis=0)


def body(
    inputs,
    lengths,
    grad_out,
    ln1_gain,
    ln1_shift,
    w_qkv,
    b_qv,
    w_proj,
    b_proj,
    ln2_gain,
    ln2_shift,
    w_up,
    b_up,
    w_down,
    b_down,
):
    n = lax.axis_size("fsdp")
    cube = is_cube()
    core = lax.axis_index("ctx")
    place = lax.axis_index("fsdp")
    rows = w_up.shape[0]
    head_cols = w_proj.shape[1] // 2
    hidden = w_up.shape[1] // 2
    own_slots = inputs.shape[1]
    width = D // n

    qkv_halves = w_qkv.reshape(rows, 3, 2, head_cols)
    proj_halves = w_proj.reshape(rows, 2, head_cols)
    up_halves = w_up.reshape(rows, 2, hidden)
    down_halves = w_down.reshape(rows, 2, hidden)

    def first_half(which):
        return jnp.concatenate(
            [
                lax.dynamic_index_in_dim(qkv_halves, which, 2, keepdims=False).reshape(
                    rows, 3 * head_cols
                ),
                lax.dynamic_index_in_dim(proj_halves, which, 1, keepdims=False),
            ],
            axis=1,
        )

    def half_of(halves, which):
        return lax.dynamic_index_in_dim(halves, which, 1, keepdims=False)

    def by_core(own, other, axis):
        return jnp.where(
            core == 0,
            jnp.concatenate([own, other], axis=axis),
            jnp.concatenate([other, own], axis=axis),
        )

    small = jnp.concatenate(
        [
            jnp.stack([ln1_gain, ln1_shift, b_proj, ln2_gain, ln2_shift, b_down, b_qv[:, 0]]),
            b_up.reshape(2, rows),
        ]
    )
    small_both = by_core(small, swap(small, "ctx"), 1)
    first_own, first_other = first_half(core), first_half(1 - core)
    first_mine = by_core(first_own, swap(first_other, "ctx"), 0)
    small_flat = jnp.zeros((16 * 2 * rows,), BF16)
    small_flat = small_flat.at[: 9 * 2 * rows].set(small_both.reshape(-1))
    cols = first_mine.shape[1]
    small_rows = -(-16 * 2 * rows // cols)
    small_rows_padded = -(-small_rows // 8) * 8
    small_block = jnp.zeros((small_rows_padded * cols,), BF16)
    small_block = small_block.at[: 16 * 2 * rows].set(small_flat).reshape(small_rows_padded, cols)

    first_shard = jnp.concatenate([first_mine, small_block], axis=0)
    first_shard, inputs, grad_out, up_halves, down_halves = tie(
        first_shard, inputs, grad_out, up_halves, down_halves
    )
    u, d = (
        by_core(half_of(t, core), swap(half_of(t, 1 - core), "ctx"), 0)
        for t in (up_halves, down_halves)
    )
    absolute, relative = absolute_places(), relative_blocks()

    def to_relative(array):
        blocks = array.reshape(array.shape[0], n, width)
        return jnp.take(blocks, absolute, axis=1).reshape(array.shape)

    grad_own = to_relative(grad_out[0])
    f = first_shard
    if cube:
        f_far, f_x = flip(f, FAR_BIT), flip(f, X_BIT)
        grad_far = flip(grad_own[:, D // 2 :], X_BIT)
        f_far, f_x, grad_far, u, d = tie(f_far, f_x, grad_far, u, d)
        u_x = flip(u, X_BIT)
        f_near = flip(rows_of(f, f_far), NEAR_BIT)
        u_far, f_far_x, d_x = flip(u, FAR_BIT), flip(f_far, X_BIT), flip(d, X_BIT)
        f_near, u_far, f_far_x, u_x, d_x, u, d = tie(f_near, u_far, f_far_x, u_x, d_x, u, d)
        u_near = flip(rows_of(u, u_far), NEAR_BIT)
        d_far, f_near_x, u_far_x = flip(d, FAR_BIT), flip(f_near, X_BIT), flip(u_far, X_BIT)
        d_far, f_near_x, u_far_x, u_near, d = tie(d_far, f_near_x, u_far_x, u_near, d)
        d_near = flip(rows_of(d, d_far), NEAR_BIT)
        u_near_x, d_far_x = flip(u_near, X_BIT), flip(d_far, X_BIT)
        first_pieces = [f, f_far, f_near, f_x, f_far_x, f_near_x]
    else:
        first_pieces, up_pieces, down_pieces = (
            [lax.all_gather(t, "fsdp", tiled=True)] for t in (f, u, d)
        )
    block, pitch = 2 * rows, 2 * rows + small_rows_padded
    vectors = qv_bias = None
    if not cube:
        whole = first_pieces[0].reshape(n, pitch, cols)
        first_pieces, pitch = [whole[:, :block].reshape(D, cols)], block
        small_abs = whole[:, block:].reshape(n, -1)[:, : 16 * 2 * rows]
        small_abs = small_abs.reshape(n, 16, 2 * rows).astype(F32)
        vectors = small_abs.transpose(1, 0, 2).reshape(16, D)
        qv_all = small_abs[:, 6].reshape(2, 2, head_cols)
        qv_bias = lax.dynamic_index_in_dim(qv_all, core, 1, keepdims=False)

    length = lengths[0]
    own_ids = core * own_slots + jnp.arange(own_slots, dtype=jnp.int32)
    other_ids = (1 - core) * own_slots + jnp.arange(own_slots, dtype=jnp.int32)
    slot_ids = jnp.concatenate([own_ids, other_ids])
    key_valid = slot_ids < length
    row_valid = key_valid.astype(F32)[:, None]
    places = jnp.concatenate([absolute, jnp.stack([core, core * own_slots, length])])

    inputs_own = to_relative(inputs[0])
    entering_all = with_other(inputs_own).astype(F32) * row_valid
    grads = (grad_own, swap(grad_own, "ctx"))
    normal_one, _ = norm_of(entering_all)
    slots = 2 * own_slots
    key_mask = row_valid.reshape(1, slots)
    query, key, value, context, att_own, att_other, normed, *found = attention(
        normal_one, vectors, qv_bias, key_mask, first_pieces, block, pitch, places
    )
    if cube:
        vectors, vectors_abs = found
        small_abs = vectors_abs.reshape(16, n, 2 * rows).transpose(1, 0, 2)
    gain_one, _, proj_bias, gain_two, shift_two, down_bias = (vectors[i] for i in range(6))
    up_all = small_abs[:, 7:9].reshape(n, 2, 2, rows).transpose(0, 2, 1, 3).reshape(2, hidden)
    up_bias = lax.dynamic_index_in_dim(up_all, core, 0, keepdims=False)
    if cube:
        d_near, u_near_x, d_far_x, att_own, att_other = tie(
            d_near, u_near_x, d_far_x, att_own, att_other
        )
        d_near_x = flip(lower(d_near), X_BIT)
        up_pieces = [u, u_far, u_near, u_x, u_far_x, u_near_x]
    att_low, att_tp = halves_low(att_own, att_other)
    if cube:
        att_low, att_tp, d_near_x, d_near = tie(att_low, att_tp, d_near_x, d_near)
        d_last_x = flip(upper(d_near), X_BIT)
    attended = att_low.astype(F32) + att_tp.astype(F32) + proj_bias
    entering = entering_all[:own_slots]
    middle = entering + attended
    normal_two, _ = norm_of(middle)
    normed_two_own = (normal_two * gain_two + shift_two).astype(BF16)
    normed_two_other = swap(normed_two_own, "ctx")
    active, slope = hidden_layer(
        normed_two_own, normed_two_other, normed, up_bias[None], up_pieces, block
    )
    if cube:
        active, slope, d_last_x = tie(active, slope, d_last_x)
        active_far = flip(active, X_BIT)
        down_pieces = [d, d_far, d_near, d_x, d_far_x, d_near_x, d_last_x]
    grad_pre, gn_own, gn_other, sum_up_bias = hidden_back(
        grads, slope, up_pieces, down_pieces, block
    )
    gn_low = round_low(gn_own + swap(gn_other, "ctx").astype(F32))
    if cube:
        gn_low, active = tie(gn_low, active)
    gn_tp = swap(gn_low, "tp")
    branch_own, branch_other = project_back(active, slots, down_pieces, block)
    if cube:
        gn_low, gn_tp, active_far, grad_pre, branch_own, branch_other = tie(
            gn_low, gn_tp, active_far, grad_pre, branch_own, branch_other
        )
        pre_far = flip(grad_pre, X_BIT)
        size, half = own_slots, D // 2
    grad_middle, grad_att_own, sums = second_norm_back(
        middle, gain_two[None], gn_low, gn_tp, grad_own
    )
    if cube:
        grad_att_own, active_far, branch_own, branch_other = tie(
            grad_att_own, active_far, branch_own, branch_other
        )
        att_far = flip(grad_att_own[:, half:], X_BIT)
        down_high, down_two = weight_grad(
            [
                (
                    [(t, 0, size, 0) for t in (*grads, grad_far, swap(grad_far, "ctx"))],
                    0,
                    hidden,
                )
            ],
            [(active, 0, slots), (active_far, 0, slots)],
            1,
        )
    grad_att_other = swap(grad_att_own, "ctx")
    if cube:
        down_high, grad_att_other = tie(down_high, grad_att_other)
        down_near = flip(down_high, NEAR_BIT)
    branch_low, branch_tp = halves_low(branch_own, branch_other)
    packed, packed_other, gn_one_own, gn_one_other, sum_qv_bias = attention_back(
        (grad_att_own, grad_att_other), context, key_mask, query, key, value, first_pieces, block, pitch
    )
    if cube:
        pre_far, att_far, down_near, packed, gn_one_own, gn_one_other, branch_low, branch_tp = tie(
            pre_far, att_far, down_near, packed, gn_one_own, gn_one_other, branch_low, branch_tp
        )
        packed_one = flip(packed, X_BIT)
        down_far = flip(round_low(upper(down_two) + upper(down_near).astype(F32)), FAR_BIT)
        normed_swapped = swap(active_far[slots:], "ctx")
        up_high, up_two = weight_grad(
            [
                (
                    [
                        (normed_two_own, 0, size, 0),
                        (normed_two_other, 0, size, 0),
                        (active_far, slots, size, half),
                        (normed_swapped, 0, size, half),
                    ],
                    0,
                    hidden,
                )
            ],
            [(grad_pre, 0, slots), (pre_far, 0, slots)],
            1,
        )
    gn_one_low = round_low(gn_one_own + swap(gn_one_other, "ctx").astype(F32))
    if cube:
        gn_one_low, packed_one, up_high, packed_other, down_far = tie(
            gn_one_low, packed_one, up_high, packed_other, down_far
        )
        packed_two = flip(packed_other, X_BIT)
        up_near = flip(up_high, NEAR_BIT)
    gn_one_tp = swap(gn_one_low, "tp")
    if cube:
        att_swapped = swap(att_far, "ctx")
        packed_two, gn_one_tp, att_swapped = tie(packed_two, gn_one_tp, att_swapped)
        *first_high, first_two = weight_grad(
            [
                (
                    [
                        (normed, 0, slots, 0),
                        (active_far, slots, size, 0),
                        (normed_swapped, 0, size, 0),
                    ],
                    0,
                    3 * head_cols,
                ),
                (
                    [
                        (t, 0, size, 0)
                        for t in (grad_att_own, grad_att_other, att_far, att_swapped)
                    ],
                    3 * head_cols,
                    4 * head_cols,
                ),
            ],
            [(t, 0, size) for t in (packed, packed_other, packed_one, packed_two)],
            2,
        )
    else:
        packed = rows_of(packed, packed_other)
        sum_down = scatter_sum(contract(rows_of(*grads), active[:slots], 0, 0))
        sum_up = scatter_sum(contract(rows_of(normed_two_own, normed_two_other), grad_pre, 0, 0))
        sum_first = jnp.concatenate(
            [
                scatter_sum(contract(normed, packed[:, : 3 * head_cols], 0, 0)),
                scatter_sum(
                    contract(rows_of(grad_att_own, grad_att_other), context, 0, 0)
                ),
            ],
            axis=1,
        )
    output, stats = finish(
        middle, entering, attended, branch_low, branch_tp, down_bias[None], places
    )
    output = output[None]
    grad_inputs, message = first_norm_back(
        inputs_own,
        gain_one[None],
        gn_one_low,
        gn_one_tp,
        grad_middle,
        sums,
        sum_up_bias,
        sum_qv_bias,
        stats,
        places,
    )
    grad_inputs = grad_inputs[None]

    if cube:
        message = message + flip(message, X_BIT)
        first_high, up_near, message = tie(first_high, up_near, message)
        first_near = [flip(rows_of(first_high[1], coded(message)), NEAR_BIT)]
        up_far = flip(round_low(upper(up_two) + upper(up_near).astype(F32)), FAR_BIT)
        sum_down = lower(down_two) + lower(down_near).astype(F32) + down_far.astype(F32)
        first_near[0], first_high, up_far = tie(first_near[0], first_high, up_far)
        first_near.append(flip(first_high[0], NEAR_BIT))
        message = message + decoded(first_near[0][block:])
        first_low = round_low(upper(first_two) + first_near[0][:block].astype(F32))
        first_far = flip(rows_of(first_low, coded(message)), FAR_BIT)
        first_near[1], first_far = tie(first_near[1], first_far)
        sum_first = (
            lower(first_two) + first_near[1].astype(F32) + first_far[:block].astype(F32)
        )
        sum_up = lower(up_two) + lower(up_near).astype(F32) + up_far.astype(F32)
        message = message + decoded(first_far[block:])
    else:
        message = lax.psum(message, "fsdp")
    other_message = swap(message, "ctx")
    at = 2 * place + core
    vector_own = lax.dynamic_slice_in_dim(
        message[:6] + other_message[:6], at * rows, rows, 1
    )
    totals = (message[7] + other_message[7])[D - 128 : D - 122]
    rms = jnp.sqrt(totals[:5] / (totals[5] * D))
    qv_sum = by_core(
        message[7, : 2 * head_cols].reshape(2, 1, head_cols),
        other_message[7, : 2 * head_cols].reshape(2, 1, head_cols),
        1,
    ).reshape(-1)
    qv_mine = lax.dynamic_slice_in_dim(qv_sum, at * rows, rows, 0)
    up_sum = by_core(message[6], other_message[6], 0)
    up_mine = lax.dynamic_slice_in_dim(up_sum, at * 2 * rows, 2 * rows, 0)

    def owned(total):
        mine = lax.dynamic_slice_in_dim(total, core * rows, rows, 0)
        theirs = swap(lax.dynamic_slice_in_dim(total, (1 - core) * rows, rows, 0), "ctx")
        return mine, theirs

    grad_w_qkv, grad_w_proj = assemble(*owned(sum_first), places)
    grad_w_up = by_core(*owned(sum_up), 1)
    grad_w_down = by_core(*owned(sum_down), 1)
    return (
        output,
        grad_inputs,
        vector_own[0],
        vector_own[1],
        grad_w_qkv,
        qv_mine[:, None],
        grad_w_proj,
        vector_own[2],
        vector_own[3],
        vector_own[4],
        grad_w_up,
        up_mine[:, None],
        grad_w_down,
        vector_own[5],
        rms,
    )


def solution(mesh):
    both = ("fsdp", "ctx")
    rows, vector, matrix = P("fsdp", "ctx", None), P(both), P(both, "tp")
    in_specs = (
        rows,
        P("fsdp"),
        rows,
        vector,
        vector,
        P(both, None, "tp"),
        matrix,
        matrix,
        vector,
        vector,
        vector,
        matrix,
        matrix,
        matrix,
        vector,
    )
    out_specs = (
        rows,
        rows,
        vector,
        vector,
        P(both, None, "tp"),
        matrix,
        matrix,
        vector,
        vector,
        vector,
        matrix,
        matrix,
        matrix,
        vector,
        P(),
    )
    return jax.shard_map(body, mesh=mesh, in_specs=in_specs, out_specs=out_specs, check_vma=False)
```

time: 265 us -> 243 us (0.917)
  Pallas kernels: 0 us -> 54.5 us
  matrix products: 30.5 us -> 0 us
  local copies, waits for them, and re-layouts: 41.4 us -> 20 us
  other arithmetic: 30.4 us -> 16.9 us
  waiting for transfers between devices: 112 us -> 99.7 us
    pallas_call x0 -> x12, Pallas kernels: none -> 54.5 us  [the longest x3 12 us: weight_grad(): pl.pallas_call(kernel, name='weight_grad', out_shape=[shape_of(size, colu...]
    dot_general x21 -> x0, matrix products: 28.3 us -> none  [the longest x12 16.7 us: contract(): lax.dot_general(left, right, (((left_dim,), (right_dim,)), ((), ())), pre...]
    ppermute x28 -> x30, waiting for transfers between devices: 98.3 us -> 89.6 us  [flip(): return lax.ppermute(array, 'fsdp', [(i, i ^ bit) for i in range(n)])]
    concatenate x5 -> x0, local copies, waits for them, and re-layouts: 5.14 us -> none  [the longest x1 3.96 us: body(): jnp.concatenate([sum_qv_bias, square_sums, jnp.zeros((D - 2 * head_cols -...]
    reduce_sum x11 -> x4, other arithmetic: 7.23 us -> 2.1 us  [the longest x2 1.51 us: norm_of(): mean = jnp.mean(values, axis=-1, keepdims=True)]
    gather x5 -> x0, local copies, waits for them, and re-layouts: 4.6 us -> none  [the longest x4 4.03 us: to_absolute(): return jnp.take(blocks, relative, axis=1).reshape(array.shape)]
    add x12 -> x7, other arithmetic: 4.07 us -> 0.39 us  [the longest x1 0.1 us: body(): lower(down_two) + lower(down_near).astype(F32) + down_far.astype(F32)]
    ppermute x20 -> x23, waiting for transfers between devices: 13.7 us -> 10.1 us  [swap(): return lax.ppermute(array, axis, [(0, 1), (1, 0)])]
  transfers between devices with their start and end apart: 48 -> 53, of which waited for: 20 -> 24; matrix products, arithmetic and copies ran while one was open for 29% -> 9% of each run, Pallas kernels for 0% -> 20%
where the time goes in v3:
time: 243 us; the launch traced here: 242 us
  waiting for transfers between devices  99.7 us (41%)
  Pallas kernels  54.5 us (22%)
  starting transfers between devices  47.8 us (20%)
  local copies, waits for them, and re-layouts  20 us (8%)
  other arithmetic  16.9 us (7%)
  between operations  2.9 us (1%)
    ppermute x30, waiting for transfers between devices, flip(): return lax.ppermute(array, 'fsdp', [(i, i ^ bit) for i in range(n)])  89.6 us
    ppermute x30, starting transfers between devices, flip(): return lax.ppermute(array, 'fsdp', [(i, i ^ bit) for i in range(n)])  40.4 us
    pallas_call x3, Pallas kernels, weight_grad(): pl.pallas_call(kernel, name='weight_grad', out_shape=[shape_of(size, colu...  12 us
    ppermute x23, waiting for transfers between devices, swap(): return lax.ppermute(array, axis, [(0, 1), (1, 0)])  10.1 us
    unnamed x118, local copies, waits for them, and re-layouts  8.67 us
    pallas_call x1, Pallas kernels, attention_back(): pl.pallas_call(kernel, name='attention_back', out_shape=[shape_of(half, 4...  7.96 us
    ppermute x23, starting transfers between devices, swap(): return lax.ppermute(array, axis, [(0, 1), (1, 0)])  7.46 us
    pallas_call x1, Pallas kernels, attention(): pl.pallas_call(kernel, name='attention', in_specs=[pl.BlockSpec(memory_sp...  7.26 us
  transfers between devices with their start and end apart: 53, of which 24 were waited for; matrix products, arithmetic and copies ran while one was open for 9% of the time, Pallas kernels for 20%

profile of v3, /device:TPU:0, one launch (start us, length us, event | category | flops | bytes accessed | tf_op | source)
XLA Modules:
  0.0 241.7 jit_solution(8350178269708580457)
XLA Ops:
  8.2 3.8 %collective-permute-start.3 = (bf16[136,1024]{1,0:T(8,128)(2,1)S(1)}, bf16[136,1024]{1,0:T(8,128)(2,1)S(1)}, u32[]{:S(2)}, u32[]{:S(2)}) collective-permute-start(bf16[136,1024]{1,0:T(8,128)(2,1)S(1)} %pad_maximum_fusion.6.refs_0_), channel_id=1, source_target_pairs={{0,16},{4,20},{8,24},{12,28},{16,0},{20,4},{24,8},{28,12},{1,17},{... | collective-permute-start | bytes 835592 | tf_op jit(solution)/shard_map/ppermute | solution.py:34
  16.8 7.3 %collective-permute-done.5.refs_4_ = bf16[160,512]{1,0:T(8,128)(2,1)S(1)} collective-permute-done((bf16[160,512]{1,0:T(8,128)(2,1)S(1)}, bf16[160,512]{1,0:T(8,128)(2,1)S(1)}, u32[]{:S(2)}, u32[]{:S(2)}) %collective-permute-start.5) | collective-permute-done | bytes 163872 | tf_op jit(solution)/shard_map/ppermute | solution.py:34
  27.5 3.4 %collective-permute-start.9 = (bf16[128,1024]{1,0:T(8,128)(2,1)S(1)}, bf16[128,1024]{1,0:T(8,128)(2,1)S(1)}, u32[]{:S(2)}, u32[]{:S(2)}) collective-permute-start(bf16[128,1024]{1,0:T(8,128)(2,1)S(1)} %maximum_select_fusion.3.refs_0_), channel_id=1, source_target_pairs={{0,16},{4,20},{8,24},{12,28},{16,0},{20,4},{24,8},{28,12},{1,17},{... | collective-permute-start | bytes 786440 | tf_op jit(solution)/shard_map/ppermute | solution.py:34
  34.8 8.9 %collective-permute-done.9.refs_1_ = bf16[128,1024]{1,0:T(8,128)(2,1)S(1)} collective-permute-done((bf16[128,1024]{1,0:T(8,128)(2,1)S(1)}, bf16[128,1024]{1,0:T(8,128)(2,1)S(1)}, u32[]{:S(2)}, u32[]{:S(2)}) %collective-permute-start.9) | collective-permute-done | bytes 262176 | tf_op jit(solution)/shard_map/ppermute | solution.py:34
  52.7 14.0 %collective-permute-done.13.refs_7_.refs_1_ = bf16[128,1024]{1,0:T(8,128)(2,1)S(1)} collective-permute-done((bf16[128,1024]{1,0:T(8,128)(2,1)S(1)}, bf16[128,1024]{1,0:T(8,128)(2,1)S(1)}, u32[]{:S(2)}, u32[]{:S(2)}) %collective-permute-start.13) | collective-permute-done | bytes 262176 | tf_op jit(solution)/shard_map/ppermute | solution.py:34
  73.7 7.3 %attention.1 = (bf16[320,256]{1,0:T(8,128)(2,1)}, bf16[320,256]{1,0:T(8,128)(2,1)}, bf16[320,256]{1,0:T(8,128)(2,1)}, bf16[320,256]{1,0:T(8,128)(2,1)}, f32[160,...) custom-call(s32[11]{0:T(128)} %pad_add_fusion.places_ref, ...), custom_call_target="tpu_custom_call" | custom-call | flops 1000 | bytes 1000 | tf_op jit(solution)/shard_map/attention/pallas_call | solution.py:201
  81.0 7.8 %collective-permute-done.19.refs_10_.refs_4_ = bf16[128,1024]{1,0:T(8,128)(2,1)} collective-permute-done((bf16[128,1024]{1,0:T(8,128)(2,1)S(1)}, bf16[128,1024]{1,0:T(8,128)(2,1)}, u32[]{:S(2)}, u32[]{:S(2)}) %collective-permute-start.19) | collective-permute-done | bytes 262176 | tf_op jit(solution)/shard_map/ppermute | solution.py:34
  96.6 5.0 %collective-permute-done.22.refs_11_.refs_5_ = bf16[128,1024]{1,0:T(8,128)(2,1)S(1)} collective-permute-done((bf16[128,1024]{1,0:T(8,128)(2,1)S(1)}, bf16[128,1024]{1,0:T(8,128)(2,1)S(1)}, u32[]{:S(2)}, u32[]{:S(2)}) %collective-permute-start.22) | collective-permute-done | bytes 262176 | tf_op jit(solution)/shard_map/ppermute | solution.py:34
  107.4 4.9 %hidden_layer.1 = (bf16[480,1024]{1,0:T(8,128)(2,1)}, f32[320,1024]{1,0:T(8,128)}) custom-call(bf16[160,1024]{1,0:T(8,128)(2,1)} %copy-done.8, bf16[160,1024]{1,0:T(8,128)(2,1)} %copy-done.21, bf16[320,1024]{1,0:T(8,128)(2,1)} %get-tuple-element.177.normed_ref.refs_4_, f32[1,1024]{1,0:T(1,128)} %constant_dynamic-slice_fusion.8.bias_ref, ...), custom_call_target="tpu_custom_call" | custom-call | flops 1000 | bytes 1000 | tf_op jit(solution)/shard_map/hidden_layer/pallas_call | solution.py:283
  115.1 6.6 %hidden_back.1 = (bf16[320,1024]{1,0:T(8,128)(2,1)}, f32[160,1024]{1,0:T(8,128)}, bf16[160,1024]{1,0:T(8,128)(2,1)}, f32[1,1024]{1,0:T(1,128)}) custom-call(bf16[160,1024]{1,0:T(8,128)(2,1)} %bitcast.106, bf16[160,1024]{1,0:T(8,128)(2,1)} %copy-done.18, f32[320,1024]{1,0:T(8,128)} %get-tuple-element.185.slope_ref, bf16[128,1024]{1,0:T(8,128)(2,1)} %copy-done.7, ...), custom_call_target="tpu_custom_call" | custom-call | flops 1000 | bytes 1000 | tf_op jit(solution)/shard_map/hidden_back/pallas_call | solution.py:310
  125.7 4.3 %project_back.1 = (f32[160,1024]{1,0:T(8,128)}, bf16[160,1024]{1,0:T(8,128)(2,1)}) custom-call(bf16[480,1024]{1,0:T(8,128)(2,1)} %get-tuple-element.195.values_ref.refs_0_, bf16[128,1024]{1,0:T(8,128)(2,1)} %copy-done.6, bf16[128,1024]{1,0:T(8,128)(2,1)} %copy-done.10, bf16[256,1024]{1,0:T(8,128)(2,1)} %copy-done.4, ...), custom_call_target="tpu_custom_call" | custom-call | flops 1000 | bytes 1000 | tf_op jit(solution)/shard_map/project_back/pallas_call | solution.py:332
  130.0 4.6 %collective-permute-done.27.other_ref = bf16[160,1024]{1,0:T(8,128)(2,1)S(1)} collective-permute-done((bf16[160,1024]{1,0:T(8,128)(2,1)S(1)}, bf16[160,1024]{1,0:T(8,128)(2,1)S(1)}, u32[]{:S(2)}, u32[]{:S(2)}) %collective-permute-start.27) | collective-permute-done | bytes 327712 | tf_op jit(solution)/shard_map/ppermute | solution.py:29
  136.6 3.3 %second_norm_back.1 = (f32[160,1024]{1,0:T(8,128)}, bf16[160,1024]{1,0:T(8,128)(2,1)}, f32[4,1024]{1,0:T(4,128)}) custom-call(f32[160,1024]{1,0:T(8,128)} %copy-done, f32[1,1024]{1,0:T(1,128)} %copy-done.48, bf16[160,1024]{1,0:T(8,128)(2,1)} %copy-done.20, bf16[160,1024]{1,0:T(8,128)(2,1)} %copy-done.38, bf16[160,1024]{1,0:T(8,128)(2,1)} %bitcast.107), custom_call_target="tpu_custom_call" | custom-call | flops 1000 | bytes 1000 | tf_op jit(solution)/shard_map/second_norm_back/pallas_call | solution.py:452
  143.1 3.8 %weight_grad.3 = (bf16[256,1024]{1,0:T(8,128)(2,1)}, f32[256,1024]{1,0:T(8,128)}) custom-call(bf16[480,1024]{1,0:T(8,128)(2,1)} %get-tuple-element.195.values_ref.refs_0_, bf16[480,1024]{1,0:T(8,128)(2,1)} %copy-done.1, bf16[160,1024]{1,0:T(8,128)(2,1)} %bitcast.108, bf16[160,1024]{1,0:T(8,128)(2,1)} %copy-done.18, bf16[160,512]{1,0:T(8,128)(2,1)} %copy-done.45, ...), custom_call_target="tpu_custom_call" | custom-call | flops 1000 | bytes 1000 | tf_op jit(solution)/shard_map/weight_grad/pallas_call | solution.py:375
  150.9 8.0 %attention_back.1 = (bf16[160,1024]{1,0:T(8,128)(2,1)}, bf16[160,1024]{1,0:T(8,128)(2,1)}, f32[160,1024]{1,0:T(8,128)}, bf16[160,1024]{1,0:T(8,128)(2,1)}, f32[1,512]{1,0:T(1,128)}) custom-call(bf16[160,1024]{1,0:T(8,128)(2,1)} %get-tuple-element.205.grad_own.refs_7_, bf16[160,1024]{1,0:T(8,128)(2,1)} %copy-done.17, ...), custom_call_target="tpu_custom_call" | custom-call | flops 1000 | bytes 1000 | tf_op jit(solution)/shard_map/attention_back/pallas_call | solution.py:250
  165.2 3.9 %weight_grad.4 = (bf16[256,1024]{1,0:T(8,128)(2,1)}, f32[256,1024]{1,0:T(8,128)}) custom-call(bf16[320,1024]{1,0:T(8,128)(2,1)} %get-tuple-element.198.refs_0_, bf16[320,1024]{1,0:T(8,128)(2,1)} %collective-permute-done.29.refs_1_, bf16[160,1024]{1,0:T(8,128)(2,1)} %copy-done.8, bf16[160,1024]{1,0:T(8,128)(2,1)} %copy-done.21, bf16[480,1024]{1,0:T(8,128)(2,1)} %copy-done.1, ...), custom_call_target="tpu_custom_call" | custom-call | flops 1000 | bytes 1000 | tf_op jit(solution)/shard_map/weight_grad/pallas_call | solution.py:375
  170.2 8.3 %collective-permute-done.39 = bf16[128,1024]{1,0:T(8,128)(2,1)S(1)} collective-permute-done((bf16[128,1024]{1,0:T(8,128)(2,1)}, bf16[128,1024]{1,0:T(8,128)(2,1)S(1)}, u32[]{:S(2)}, u32[]{:S(2)}) %collective-permute-start.39) | collective-permute-done | bytes 262176 | tf_op jit(solution)/shard_map/ppermute | solution.py:34
  181.1 3.2 %finish.1 = (bf16[160,1024]{1,0:T(8,128)(2,1)}, f32[1,128]{1,0:T(1,128)}) custom-call(s32[11]{0:T(128)} %pad_add_fusion.places_ref, f32[160,1024]{1,0:T(8,128)} %copy-done, f32[160,1024]{1,0:T(8,128)} %get-tuple-element.310.entering_ref, f32[160,1024]{1,0:T(8,128)} %get-tuple-element.309.attended_ref, bf16[160,1024]{1,0:T(8,128)(2,1)} %copy-done.22, ...), custom_call_target="tpu_custom_call" | custom-call | flops 1000 | bytes 1000 | tf_op jit(solution)/shard_map/finish/pallas_call | solution.py:495
  184.3 4.6 %collective-permute-done.40.refs_3_ = bf16[160,1024]{1,0:T(8,128)(2,1)S(1)} collective-permute-done((bf16[160,1024]{1,0:T(8,128)(2,1)S(1)}, bf16[160,1024]{1,0:T(8,128)(2,1)S(1)}, u32[]{:S(2)}, u32[]{:S(2)}) %collective-permute-start.40) | collective-permute-done | bytes 327712 | tf_op jit(solution)/shard_map/ppermute | solution.py:34
  190.0 2.9 %first_norm_back.1 = (f32[160,1024]{1,0:T(8,128)}, f32[8,1024]{1,0:T(8,128)}) custom-call(s32[11]{0:T(128)} %pad_add_fusion.places_ref, bf16[160,1024]{1,0:T(8,128)(2,1)} %bitcast.103, f32[1,1024]{1,0:T(1,128)} %get-tuple-element.327.gain_ref, bf16[160,1024]{1,0:T(8,128)(2,1)} %copy-done.19, bf16[160,1024]{1,0:T(8,128)(2,1)} %copy-done.37, ...), custom_call_target="tpu_custom_call" | custom-call | flops 1000 | bytes 1000 | tf_op jit(solution)/shard_map/first_norm_back/pallas_call | solution.py:530
  194.3 4.3 %weight_grad.5 = (bf16[128,1024]{1,0:T(8,128)(2,1)}, bf16[128,1024]{1,0:T(8,128)(2,1)}, f32[256,1024]{1,0:T(8,128)}) custom-call(bf16[160,1024]{1,0:T(8,128)(2,1)} %get-tuple-element.225.refs_0_, bf16[160,1024]{1,0:T(8,128)(2,1)} %get-tuple-element.232.refs_1_, bf16[160,1024]{1,0:T(8,128)(2,1)} %collective-permute-done.37.refs_2_, ...), custom_call_target="tpu_custom_call" | custom-call | flops 1000 | bytes 1000 | tf_op jit(solution)/shard_map/weight_grad/pallas_call | solution.py:375
  202.7 11.9 %collective-permute-done.46 = bf16[128,1024]{1,0:T(8,128)(2,1)S(1)} collective-permute-done((bf16[128,1024]{1,0:T(8,128)(2,1)S(1)}, bf16[128,1024]{1,0:T(8,128)(2,1)S(1)}, u32[]{:S(2)}, u32[]{:S(2)}) %collective-permute-start.46) | collective-permute-done | bytes 262176 | tf_op jit(solution)/shard_map/ppermute | solution.py:34
  219.2 3.6 %collective-permute-done.47 = bf16[128,1024]{1,0:T(8,128)(2,1)S(1)} collective-permute-done((bf16[128,1024]{1,0:T(8,128)(2,1)S(1)}, bf16[128,1024]{1,0:T(8,128)(2,1)S(1)}, u32[]{:S(2)}, u32[]{:S(2)}) %collective-permute-start.47) | collective-permute-done | bytes 262176 | tf_op jit(solution)/shard_map/ppermute | solution.py:34
  222.8 9.2 %collective-permute-done.48 = bf16[144,1024]{1,0:T(8,128)(2,1)S(1)} collective-permute-done((bf16[144,1024]{1,0:T(8,128)(2,1)S(1)}, bf16[144,1024]{1,0:T(8,128)(2,1)S(1)}, u32[]{:S(2)}, u32[]{:S(2)}) %collective-permute-start.48) | collective-permute-done | bytes 294944 | tf_op jit(solution)/shard_map/ppermute | solution.py:34
  (303 shorter events, 93.9 us)
Async XLA Ops:
  8.2 16.9 %collective-permute-start.3 = (bf16[136,1024]{1,0:T(8,128)(2,1)S(1)}, bf16[136,1024]{1,0:T(8,128)(2,1)S(1)}, u32[]{:S(2)}, u32[]{:S(2)}) collective-permute-start(bf16[136,1024]{1,0:T(8,128)(2,1)S(1)} %pad_maximum_fusion.6.refs_0_), channel_id=1, source_target_pairs={{0,16},{4,20},{8,24},{12,28},{16,0},{20,4},{24,8},{28,12},{1,17},{... | collective-permute-start | bytes 835592 | tf_op jit(solution)/shard_map/ppermute | solution.py:34
  12.0 13.2 %collective-permute-start.4 = (bf16[136,1024]{1,0:T(8,128)(2,1)S(1)}, bf16[136,1024]{1,0:T(8,128)(2,1)S(1)}, u32[]{:S(2)}, u32[]{:S(2)}) collective-permute-start(bf16[136,1024]{1,0:T(8,128)(2,1)S(1)} %pad_maximum_fusion.6.refs_0_), channel_id=1, source_target_pairs={{0,4},{4,0},{8,12},{12,8},{16,20},{20,16},{24,28},{28,24},{1,5},{5... | collective-permute-start | bytes 835592 | tf_op jit(solution)/shard_map/ppermute | solution.py:34
  25.2 20.5 %collective-permute-start.8 = (bf16[272,1024]{1,0:T(8,128)(2,1)S(1)}, bf16[272,1024]{1,0:T(8,128)(2,1)S(1)}, u32[]{:S(2)}, u32[]{:S(2)}) collective-permute-start(bf16[272,1024]{1,0:T(8,128)(2,1)S(1)} %pad_maximum_fusion.1), channel_id=1, source_target_pairs={{0,8},{4,12},{8,0},{12,4},{16,24},{20,28},{24,16},{28,20},{1,9},{5... | collective-permute-start | bytes 1671176 | tf_op jit(solution)/shard_map/ppermute | solution.py:34
  26.0 19.7 %collective-permute-start.10 = (bf16[136,1024]{1,0:T(8,128)(2,1)S(1)}, bf16[136,1024]{1,0:T(8,128)(2,1)S(1)}, u32[]{:S(2)}, u32[]{:S(2)}) collective-permute-start(bf16[136,1024]{1,0:T(8,128)(2,1)S(1)} %collective-permute-done.3.refs_1_), channel_id=1, source_target_pairs={{0,4},{4,0},{8,12},{12,8},{16,20},{20,16},{24,28},{28,24},{1,5},{5... | collective-permute-start | bytes 835592 | tf_op jit(solution)/shard_map/ppermute | solution.py:34
  27.5 16.2 %collective-permute-start.9 = (bf16[128,1024]{1,0:T(8,128)(2,1)S(1)}, bf16[128,1024]{1,0:T(8,128)(2,1)S(1)}, u32[]{:S(2)}, u32[]{:S(2)}) collective-permute-start(bf16[128,1024]{1,0:T(8,128)(2,1)S(1)} %maximum_select_fusion.3.refs_0_), channel_id=1, source_target_pairs={{0,16},{4,20},{8,24},{12,28},{16,0},{20,4},{24,8},{28,12},{1,17},{... | collective-permute-start | bytes 786440 | tf_op jit(solution)/shard_map/ppermute | solution.py:34
  31.4 14.3 %collective-permute-start.12 = (bf16[128,1024]{1,0:T(8,128)(2,1)S(1)}, bf16[128,1024]{1,0:T(8,128)(2,1)}, u32[]{:S(2)}, u32[]{:S(2)}) collective-permute-start(bf16[128,1024]{1,0:T(8,128)(2,1)S(1)} %maximum_select_fusion.4.refs_6_.refs_0_), channel_id=1, source_target_pairs={{0,4},{4,0},{8,12},{12,8},{16,20},{20,16},{24,28},{28,24},{1,5},{5... | collective-permute-start | bytes 786440 | tf_op jit(solution)/shard_map/ppermute | solution.py:34
  45.7 21.9 %collective-permute-start.14 = (bf16[272,1024]{1,0:T(8,128)(2,1)S(1)}, bf16[272,1024]{1,0:T(8,128)(2,1)S(1)}, u32[]{:S(2)}, u32[]{:S(2)}) collective-permute-start(bf16[272,1024]{1,0:T(8,128)(2,1)S(1)} %collective-permute-done.8.refs_2_), channel_id=1, source_target_pairs={{0,4},{4,0},{8,12},{12,8},{16,20},{20,16},{24,28},{28,24},{1,5},{5... | collective-permute-start | bytes 1671176 | tf_op jit(solution)/shard_map/ppermute | solution.py:34
  47.3 20.3 %collective-permute-start.16 = (bf16[256,1024]{1,0:T(8,128)(2,1)S(1)}, bf16[256,1024]{1,0:T(8,128)(2,1)}, u32[]{:S(2)}, u32[]{:S(2)}) collective-permute-start(bf16[256,1024]{1,0:T(8,128)(2,1)S(1)} %pad_maximum_fusion.2), channel_id=1, source_target_pairs={{0,8},{4,12},{8,0},{12,4},{16,24},{20,28},{24,16},{28,20},{1,9},{5... | collective-permute-start | bytes 1572872 | tf_op jit(solution)/shard_map/ppermute | solution.py:34
  50.3 16.5 %collective-permute-start.15 = (bf16[128,1024]{1,0:T(8,128)(2,1)S(1)}, bf16[128,1024]{1,0:T(8,128)(2,1)S(1)}, u32[]{:S(2)}, u32[]{:S(2)}) collective-permute-start(bf16[128,1024]{1,0:T(8,128)(2,1)S(1)} %collective-permute-done.9.refs_1_), channel_id=1, source_target_pairs={{0,4},{4,0},{8,12},{12,8},{16,20},{20,16},{24,28},{28,24},{1,5},{5... | collective-permute-start | bytes 786440 | tf_op jit(solution)/shard_map/ppermute | solution.py:34
  50.8 16.0 %collective-permute-start.13 = (bf16[128,1024]{1,0:T(8,128)(2,1)S(1)}, bf16[128,1024]{1,0:T(8,128)(2,1)S(1)}, u32[]{:S(2)}, u32[]{:S(2)}) collective-permute-start(bf16[128,1024]{1,0:T(8,128)(2,1)S(1)} %maximum_select_fusion.4.refs_6_.refs_0_), channel_id=1, source_target_pairs={{0,16},{4,20},{8,24},{12,28},{16,0},{20,4},{24,8},{28,12},{1,17},{... | collective-permute-start | bytes 786440 | tf_op jit(solution)/shard_map/ppermute | solution.py:34
  68.5 20.2 %collective-permute-start.17 = (bf16[256,1024]{1,0:T(8,128)(2,1)}, bf16[256,1024]{1,0:T(8,128)(2,1)S(1)}, u32[]{:S(2)}, u32[]{:S(2)}) collective-permute-start(bf16[256,1024]{1,0:T(8,128)(2,1)} %pad_maximum_fusion.3), channel_id=1, source_target_pairs={{0,8},{4,12},{8,0},{12,4},{16,24},{20,28},{24,16},{28,20},{1,9},{5... | collective-permute-start | bytes 1572872 | tf_op jit(solution)/shard_map/ppermute | solution.py:34
  69.9 18.9 %collective-permute-start.18 = (bf16[256,1024]{1,0:T(8,128)(2,1)}, bf16[256,1024]{1,0:T(8,128)(2,1)S(1)}, u32[]{:S(2)}, u32[]{:S(2)}) collective-permute-start(bf16[256,1024]{1,0:T(8,128)(2,1)} %collective-permute-done.16.refs_2_), channel_id=1, source_target_pairs={{0,4},{4,0},{8,12},{12,8},{16,20},{20,16},{24,28},{28,24},{1,5},{5... | collective-permute-start | bytes 1572872 | tf_op jit(solution)/shard_map/ppermute | solution.py:34
  71.5 17.2 %collective-permute-start.19 = (bf16[128,1024]{1,0:T(8,128)(2,1)S(1)}, bf16[128,1024]{1,0:T(8,128)(2,1)}, u32[]{:S(2)}, u32[]{:S(2)}) collective-permute-start(bf16[128,1024]{1,0:T(8,128)(2,1)S(1)} %collective-permute-done.13.refs_7_.refs_1_), channel_id=1, source_target_pairs={{0,4},{4,0},{8,12},{12,8},{16,20},{20,16},{24,28},{28,24},{1,5},{5... | collective-permute-start | bytes 786440 | tf_op jit(solution)/shard_map/ppermute | solution.py:34
  112.9 23.7 %collective-permute-start.28 = (bf16[480,1024]{1,0:T(8,128)(2,1)}, bf16[480,1024]{1,0:T(8,128)(2,1)S(1)}, u32[]{:S(2)}, u32[]{:S(2)}) collective-permute-start(bf16[480,1024]{1,0:T(8,128)(2,1)} %get-tuple-element.195.values_ref.refs_0_), channel_id=1, source_target_pairs={{0,4},{4,0},{8,12},{12,8},{16,20},{20,16},{24,28},{28,24},{1,5},{5... | collective-permute-start | bytes 2949128 | tf_op jit(solution)/shard_map/ppermute | solution.py:34
  140.5 20.9 %collective-permute-start.29 = (bf16[320,1024]{1,0:T(8,128)(2,1)}, bf16[320,1024]{1,0:T(8,128)(2,1)}, u32[]{:S(2)}, u32[]{:S(2)}) collective-permute-start(bf16[320,1024]{1,0:T(8,128)(2,1)} %get-tuple-element.198.refs_0_), channel_id=1, source_target_pairs={{0,4},{4,0},{8,12},{12,8},{16,20},{20,16},{24,28},{28,24},{1,5},{5... | collective-permute-start | bytes 1966088 | tf_op jit(solution)/shard_map/ppermute | solution.py:34
  146.9 14.5 %collective-permute-start.33 = (bf16[256,1024]{1,0:T(8,128)(2,1)}, bf16[256,1024]{1,0:T(8,128)(2,1)S(1)}, u32[]{:S(2)}, u32[]{:S(2)}) collective-permute-start(bf16[256,1024]{1,0:T(8,128)(2,1)} %get-tuple-element.209), channel_id=1, source_target_pairs={{0,8},{4,12},{8,0},{12,4},{16,24},{20,28},{24,16},{28,20},{1,9},{5... | collective-permute-start | bytes 1572872 | tf_op jit(solution)/shard_map/ppermute | solution.py:34
  147.9 13.5 %collective-permute-start.35 = (bf16[160,1024]{1,0:T(8,128)(2,1)S(1)}, bf16[160,1024]{1,0:T(8,128)(2,1)S(1)}, u32[]{:S(2)}, u32[]{:S(2)}) collective-permute-start(bf16[160,1024]{1,0:T(8,128)(2,1)S(1)} %reduce-precision_convert_fusion.1.low_ref), channel_id=1, source_target_pairs={{0,1},{1,0},{2,3},{3,2},{4,5},{5,4},{6,7},{7,6},{8,9},{9,8},{10,11... | collective-permute-start | bytes 983048 | tf_op jit(solution)/shard_map/ppermute | solution.py:29
  150.8 13.7 %collective-permute-start.38 = (bf16[160,1024]{1,0:T(8,128)(2,1)S(1)}, bf16[160,1024]{1,0:T(8,128)(2,1)S(1)}, u32[]{:S(2)}, u32[]{:S(2)}) collective-permute-start(bf16[160,1024]{1,0:T(8,128)(2,1)S(1)} %slice.176), channel_id=1, source_target_pairs={{0,2},{2,0},{1,3},{3,1},{4,6},{6,4},{5,7},{7,5},{8,10},{10,8},{9,1... | collective-permute-start | bytes 983048 | tf_op jit(solution)/shard_map/ppermute | solution.py:29
  161.5 17.0 %collective-permute-start.37 = (bf16[160,1024]{1,0:T(8,128)(2,1)}, bf16[160,1024]{1,0:T(8,128)(2,1)}, u32[]{:S(2)}, u32[]{:S(2)}) collective-permute-start(bf16[160,1024]{1,0:T(8,128)(2,1)} %get-tuple-element.225.refs_0_), channel_id=1, source_target_pairs={{0,4},{4,0},{8,12},{12,8},{16,20},{20,16},{24,28},{28,24},{1,5},{5... | collective-permute-start | bytes 983048 | tf_op jit(solution)/shard_map/ppermute | solution.py:34
  163.6 14.9 %collective-permute-start.39 = (bf16[128,1024]{1,0:T(8,128)(2,1)}, bf16[128,1024]{1,0:T(8,128)(2,1)S(1)}, u32[]{:S(2)}, u32[]{:S(2)}) collective-permute-start(bf16[128,1024]{1,0:T(8,128)(2,1)} %reduce-precision_convert_fusion.6), channel_id=1, source_target_pairs={{0,16},{4,20},{8,24},{12,28},{16,0},{20,4},{24,8},{28,12},{1,17},{... | collective-permute-start | bytes 786440 | tf_op jit(solution)/shard_map/ppermute | solution.py:34
  179.2 19.4 %collective-permute-start.43 = (bf16[256,1024]{1,0:T(8,128)(2,1)}, bf16[256,1024]{1,0:T(8,128)(2,1)S(1)}, u32[]{:S(2)}, u32[]{:S(2)}) collective-permute-start(bf16[256,1024]{1,0:T(8,128)(2,1)} %get-tuple-element.246), channel_id=1, source_target_pairs={{0,8},{4,12},{8,0},{12,4},{16,24},{20,28},{24,16},{28,20},{1,9},{5... | collective-permute-start | bytes 1572872 | tf_op jit(solution)/shard_map/ppermute | solution.py:34
  199.7 14.9 %collective-permute-start.45 = (bf16[144,1024]{1,0:T(8,128)(2,1)S(1)}, bf16[144,1024]{1,0:T(8,128)(2,1)S(1)}, u32[]{:S(2)}, u32[]{:S(2)}) collective-permute-start(bf16[144,1024]{1,0:T(8,128)(2,1)S(1)} %pad_maximum_fusion.4), channel_id=1, source_target_pairs={{0,8},{4,12},{8,0},{12,4},{16,24},{20,28},{24,16},{28,20},{1,9},{5... | collective-permute-start | bytes 884744 | tf_op jit(solution)/shard_map/ppermute | solution.py:34
  202.6 14.9 %collective-permute-start.52 = (f32[64,1024]{1,0:T(8,128)S(1)}, f32[64,1024]{1,0:T(8,128)S(1)}, u32[]{:S(2)}, u32[]{:S(2)}) collective-permute-start(f32[64,1024]{1,0:T(8,128)S(1)} %get-tuple-element.314), channel_id=1, source_target_pairs={{0,2},{2,0},{1,3},{3,1},{4,6},{6,4},{5,7},{7,5},{8,10},{10,8},{9,1... | collective-permute-start | bytes 786440 | tf_op jit(solution)/shard_map/ppermute | solution.py:29
  215.3 16.7 %collective-permute-start.48 = (bf16[144,1024]{1,0:T(8,128)(2,1)S(1)}, bf16[144,1024]{1,0:T(8,128)(2,1)S(1)}, u32[]{:S(2)}, u32[]{:S(2)}) collective-permute-start(bf16[144,1024]{1,0:T(8,128)(2,1)S(1)} %pad_maximum_fusion.5), channel_id=1, source_target_pairs={{0,16},{4,20},{8,24},{12,28},{16,0},{20,4},{24,8},{28,12},{1,17},{... | collective-permute-start | bytes 884744 | tf_op jit(solution)/shard_map/ppermute | solution.py:34
  (82 other events, 887.7 us)

commit v4 on v3

--- a/solution.py
+++ b/solution.py
@@ -218,7 +218,7 @@
 
     def kernel(grad_own, grad_other, context_ref, mask_ref, query_ref, key_ref, value_ref, *refs):
         weights = refs[: len(pieces)]
-        packed_own, packed_other, own, other, bias_sum, packed = refs[len(pieces) :]
+        packed, own, other, bias_sum = refs[len(pieces) :]
         grad_ref = stacked((grad_own, grad_other))
         valid = mask_ref[...]
         grad_context = times_pieces(
@@ -242,8 +242,6 @@
                 at = (kind // 2) * width
                 bias_sum[:, at : at + width] = jnp.sum(joined.astype(F32), axis=0, keepdims=True)
         packed[:, 3 * width :] = context_ref[...]
-        packed_own[...] = packed[:half, :]
-        packed_other[...] = packed[half:, :]
         grads = packed.at[:, : 3 * width]
         times_pieces_back(grads, weights, spans, slice(0, 3 * width), own, other)
 
@@ -251,13 +249,11 @@
         kernel,
         name="attention_back",
         out_shape=[
-            shape_of(half, 4 * width, BF16),
-            shape_of(half, 4 * width, BF16),
+            shape_of(slots, 4 * width, BF16),
             shape_of(half, model, F32),
             shape_of(half, model, BF16),
             shape_of(1, 2 * width, F32),
         ],
-        scratch_shapes=[pltpu.VMEM((slots, 4 * width), BF16)],
         cost_estimate=low_cost(),
     )(*grad_att, context, mask, query, key, value, *pieces)
 
@@ -390,33 +386,6 @@
 def valid_rows(rows, places_ref):
     slot = lax.broadcasted_iota(jnp.int32, (rows, 1), 0) + places_ref[places_ref.shape[0] - 2]
     return (slot < places_ref[places_ref.shape[0] - 1]).astype(F32)
-
-
-def assemble(mine, theirs, places):
-    rows, columns = mine.shape
-    width = columns // 4
-    last = places.shape[0] - 3
-
-    def kernel(places_ref, mine_ref, theirs_ref, three, fourth):
-        core = places_ref[last]
-        for source, half in ((mine_ref, core), (theirs_ref, 1 - core)):
-            to = pl.ds(pl.multiple_of(half * width, 128), width)
-            for kind in range(3):
-                three[:, kind, to] = source[:, kind * width : (kind + 1) * width]
-            fourth[:, to] = source[:, 3 * width :]
-
-    in_vmem = pl.BlockSpec(memory_space=pltpu.VMEM)
-    return pl.pallas_call(
-        kernel,
-        name="assemble",
-        in_specs=[pl.BlockSpec(memory_space=pltpu.SMEM)] + [in_vmem] * 2,
-        out_specs=[in_vmem] * 2,
-        out_shape=[
-            jax.ShapeDtypeStruct((rows, 3, 2 * width), F32),
-            shape_of(rows, 2 * width, F32),
-        ],
-        cost_estimate=low_cost(),
-    )(places, mine, theirs)
 
 
 def norm_grad(normal, scale, gain, grad):
@@ -647,6 +616,19 @@
         return jnp.take(blocks, absolute, axis=1).reshape(array.shape)
 
     grad_own = to_relative(grad_out[0])
+    length = lengths[0]
+    own_ids = core * own_slots + jnp.arange(own_slots, dtype=jnp.int32)
+    other_ids = (1 - core) * own_slots + jnp.arange(own_slots, dtype=jnp.int32)
+    slot_ids = jnp.concatenate([own_ids, other_ids])
+    key_valid = slot_ids < length
+    row_valid = key_valid.astype(F32)[:, None]
+    places = jnp.concatenate([absolute, jnp.stack([core, core * own_slots, length])])
+
+    inputs_own = to_relative(inputs[0])
+    entering_all = with_other(inputs_own).astype(F32) * row_valid
+    grads = (grad_own, swap(grad_own, "ctx"))
+    normal_one, _ = norm_of(entering_all)
+    slots = 2 * own_slots
     f = first_shard
     if cube:
         f_far, f_x = flip(f, FAR_BIT), flip(f, X_BIT)
@@ -658,9 +640,11 @@
         f_near, u_far, f_far_x, u_x, d_x, u, d = tie(f_near, u_far, f_far_x, u_x, d_x, u, d)
         u_near = flip(rows_of(u, u_far), NEAR_BIT)
         d_far, f_near_x, u_far_x = flip(d, FAR_BIT), flip(f_near, X_BIT), flip(u_far, X_BIT)
-        d_far, f_near_x, u_far_x, u_near, d = tie(d_far, f_near_x, u_far_x, u_near, d)
+        d_far, f_near_x, u_far_x, u_near, d, normal_one = tie(
+            d_far, f_near_x, u_far_x, u_near, d, normal_one
+        )
         d_near = flip(rows_of(d, d_far), NEAR_BIT)
-        u_near_x, d_far_x = flip(u_near, X_BIT), flip(d_far, X_BIT)
+        u_near_x = flip(u_near, X_BIT)
         first_pieces = [f, f_far, f_near, f_x, f_far_x, f_near_x]
     else:
         first_pieces, up_pieces, down_pieces = (
@@ -677,19 +661,6 @@
         qv_all = small_abs[:, 6].reshape(2, 2, head_cols)
         qv_bias = lax.dynamic_index_in_dim(qv_all, core, 1, keepdims=False)
 
-    length = lengths[0]
-    own_ids = core * own_slots + jnp.arange(own_slots, dtype=jnp.int32)
-    other_ids = (1 - core) * own_slots + jnp.arange(own_slots, dtype=jnp.int32)
-    slot_ids = jnp.concatenate([own_ids, other_ids])
-    key_valid = slot_ids < length
-    row_valid = key_valid.astype(F32)[:, None]
-    places = jnp.concatenate([absolute, jnp.stack([core, core * own_slots, length])])
-
-    inputs_own = to_relative(inputs[0])
-    entering_all = with_other(inputs_own).astype(F32) * row_valid
-    grads = (grad_own, swap(grad_own, "ctx"))
-    normal_one, _ = norm_of(entering_all)
-    slots = 2 * own_slots
     key_mask = row_valid.reshape(1, slots)
     query, key, value, context, att_own, att_other, normed, *found = attention(
         normal_one, vectors, qv_bias, key_mask, first_pieces, block, pitch, places
@@ -701,15 +672,12 @@
     up_all = small_abs[:, 7:9].reshape(n, 2, 2, rows).transpose(0, 2, 1, 3).reshape(2, hidden)
     up_bias = lax.dynamic_index_in_dim(up_all, core, 0, keepdims=False)
     if cube:
-        d_near, u_near_x, d_far_x, att_own, att_other = tie(
-            d_near, u_near_x, d_far_x, att_own, att_other
-        )
-        d_near_x = flip(lower(d_near), X_BIT)
+        d_near, u_near_x, d_far, att_own, att_other = tie(
+            d_near, u_near_x, d_far, att_own, att_other
+        )
+        d_rest_x = flip(rows_of(d_far, d_near), X_BIT)
         up_pieces = [u, u_far, u_near, u_x, u_far_x, u_near_x]
     att_low, att_tp = halves_low(att_own, att_other)
-    if cube:
-        att_low, att_tp, d_near_x, d_near = tie(att_low, att_tp, d_near_x, d_near)
-        d_last_x = flip(upper(d_near), X_BIT)
     attended = att_low.astype(F32) + att_tp.astype(F32) + proj_bias
     entering = entering_all[:own_slots]
     middle = entering + attended
@@ -720,9 +688,9 @@
         normed_two_own, normed_two_other, normed, up_bias[None], up_pieces, block
     )
     if cube:
-        active, slope, d_last_x = tie(active, slope, d_last_x)
+        active, slope, d_rest_x = tie(active, slope, d_rest_x)
         active_far = flip(active, X_BIT)
-        down_pieces = [d, d_far, d_near, d_x, d_far_x, d_near_x, d_last_x]
+        down_pieces = [d, d_far, d_near, d_x, d_rest_x]
     grad_pre, gn_own, gn_other, sum_up_bias = hidden_back(
         grads, slope, up_pieces, down_pieces, block
     )
@@ -761,14 +729,14 @@
         down_high, grad_att_other = tie(down_high, grad_att_other)
         down_near = flip(down_high, NEAR_BIT)
     branch_low, branch_tp = halves_low(branch_own, branch_other)
-    packed, packed_other, gn_one_own, gn_one_other, sum_qv_bias = attention_back(
+    packed, gn_one_own, gn_one_other, sum_qv_bias = attention_back(
         (grad_att_own, grad_att_other), context, key_mask, query, key, value, first_pieces, block, pitch
     )
     if cube:
         pre_far, att_far, down_near, packed, gn_one_own, gn_one_other, branch_low, branch_tp = tie(
             pre_far, att_far, down_near, packed, gn_one_own, gn_one_other, branch_low, branch_tp
         )
-        packed_one = flip(packed, X_BIT)
+        packed_far = flip(packed, X_BIT)
         down_far = flip(round_low(upper(down_two) + upper(down_near).astype(F32)), FAR_BIT)
         normed_swapped = swap(active_far[slots:], "ctx")
         up_high, up_two = weight_grad(
@@ -789,15 +757,11 @@
         )
     gn_one_low = round_low(gn_one_own + swap(gn_one_other, "ctx").astype(F32))
     if cube:
-        gn_one_low, packed_one, up_high, packed_other, down_far = tie(
-            gn_one_low, packed_one, up_high, packed_other, down_far
-        )
-        packed_two = flip(packed_other, X_BIT)
+        gn_one_low, down_far = tie(gn_one_low, down_far)
+    gn_one_tp = swap(gn_one_low, "tp")
+    if cube:
+        att_swapped = swap(att_far, "ctx")
         up_near = flip(up_high, NEAR_BIT)
-    gn_one_tp = swap(gn_one_low, "tp")
-    if cube:
-        att_swapped = swap(att_far, "ctx")
-        packed_two, gn_one_tp, att_swapped = tie(packed_two, gn_one_tp, att_swapped)
         *first_high, first_two = weight_grad(
             [
                 (
@@ -818,11 +782,14 @@
                     4 * head_cols,
                 ),
             ],
-            [(t, 0, size) for t in (packed, packed_other, packed_one, packed_two)],
+            [(packed, 0, slots), (packed_far, 0, slots)],
             2,
         )
+        first_high, gn_one_low, gn_one_tp, up_near = tie(
+            first_high, gn_one_low, gn_one_tp, up_near
+        )
+        up_far = flip(round_low(upper(up_two) + upper(up_near).astype(F32)), FAR_BIT)
     else:
-        packed = rows_of(packed, packed_other)
         sum_down = scatter_sum(contract(rows_of(*grads), active[:slots], 0, 0))
         sum_up = scatter_sum(contract(rows_of(normed_two_own, normed_two_other), grad_pre, 0, 0))
         sum_first = jnp.concatenate(
@@ -854,19 +821,18 @@
 
     if cube:
         message = message + flip(message, X_BIT)
-        first_high, up_near, message = tie(first_high, up_near, message)
         first_near = [flip(rows_of(first_high[1], coded(message)), NEAR_BIT)]
-        up_far = flip(round_low(upper(up_two) + upper(up_near).astype(F32)), FAR_BIT)
-        sum_down = lower(down_two) + lower(down_near).astype(F32) + down_far.astype(F32)
         first_near[0], first_high, up_far = tie(first_near[0], first_high, up_far)
-        first_near.append(flip(first_high[0], NEAR_BIT))
         message = message + decoded(first_near[0][block:])
         first_low = round_low(upper(first_two) + first_near[0][:block].astype(F32))
-        first_far = flip(rows_of(first_low, coded(message)), FAR_BIT)
-        first_near[1], first_far = tie(first_near[1], first_far)
+        far_rows, first_rest = tie(rows_of(first_low, coded(message)), first_high[0])
+        first_far = flip(far_rows, FAR_BIT)
+        first_near.append(flip(first_rest, NEAR_BIT))
+        first_near[1], up_far = tie(first_near[1], up_far)
         sum_first = (
             lower(first_two) + first_near[1].astype(F32) + first_far[:block].astype(F32)
         )
+        sum_down = lower(down_two) + lower(down_near).astype(F32) + down_far.astype(F32)
         sum_up = lower(up_two) + lower(up_near).astype(F32) + up_far.astype(F32)
         message = message + decoded(first_far[block:])
     else:
@@ -892,7 +858,12 @@
         theirs = swap(lax.dynamic_slice_in_dim(total, (1 - core) * rows, rows, 0), "ctx")
         return mine, theirs
 
-    grad_w_qkv, grad_w_proj = assemble(*owned(sum_first), places)
+    mine, theirs = owned(sum_first)
+    parts = [
+        by_core(mine[:, at : at + head_cols], theirs[:, at : at + head_cols], 1)
+        for at in range(0, 4 * head_cols, head_cols)
+    ]
+    grad_w_qkv, grad_w_proj = jnp.stack(parts[:3], axis=1), parts[3]
     grad_w_up = by_core(*owned(sum_up), 1)
     grad_w_down = by_core(*owned(sum_down), 1)
     return (

time: 243 us -> 230 us (0.947)
  waiting for transfers between devices: 99.7 us -> 91.4 us
  starting transfers between devices: 47.8 us -> 41.7 us
  other arithmetic: 16.9 us -> 21 us
  Pallas kernels: 54.5 us -> 51.9 us
    ppermute x30 -> x27, waiting for transfers between devices: 89.6 us -> 75.9 us  [flip(): return lax.ppermute(array, 'fsdp', [(i, i ^ bit) for i in range(n)])]
    ppermute x30 -> x27, starting transfers between devices: 40.4 us -> 35 us  [flip(): return lax.ppermute(array, 'fsdp', [(i, i ^ bit) for i in range(n)])]
    ppermute x23, waiting for transfers between devices: 10.1 us -> 15.5 us  [swap(): return lax.ppermute(array, axis, [(0, 1), (1, 0)])]
    pallas_call x2 -> x1, Pallas kernels: 9.95 us -> 7.89 us  [attention_back(): pl.pallas_call(kernel, name='attention_back', out_shape=[shape_of(slots,...]
    unnamed x118 -> x121, local copies, waits for them, and re-layouts: 8.67 us -> 6.98 us
    convert_element_type x7 -> x8, other arithmetic: 4.36 us -> 5.28 us  [round_low(): return lax.reduce_precision(values, 8, 7).astype(BF16)]
  transfers between devices with their start and end apart: 53 -> 50, of which waited for: 24 -> 26; matrix products, arithmetic and copies ran while one was open for 9% -> 13% of each run, Pallas kernels for 20% -> 20%
where the time goes in v4:
time: 230 us; the launch traced here: 229 us
  waiting for transfers between devices  91.4 us (40%)
  Pallas kernels  51.9 us (23%)
  starting transfers between devices  41.7 us (18%)
  other arithmetic  21 us (9%)
  local copies, waits for them, and re-layouts  19.7 us (9%)
  between operations  2.91 us (1%)
    ppermute x27, waiting for transfers between devices, flip(): return lax.ppermute(array, 'fsdp', [(i, i ^ bit) for i in range(n)])  75.9 us
    ppermute x27, starting transfers between devices, flip(): return lax.ppermute(array, 'fsdp', [(i, i ^ bit) for i in range(n)])  35 us
    ppermute x23, waiting for transfers between devices, swap(): return lax.ppermute(array, axis, [(0, 1), (1, 0)])  15.5 us
    pallas_call x3, Pallas kernels, weight_grad(): pl.pallas_call(kernel, name='weight_grad', out_shape=[shape_of(size, colu...  11.8 us
    pallas_call x1, Pallas kernels, attention_back(): pl.pallas_call(kernel, name='attention_back', out_shape=[shape_of(slots,...  7.89 us
    pallas_call x1, Pallas kernels, attention(): pl.pallas_call(kernel, name='attention', in_specs=[pl.BlockSpec(memory_sp...  7.26 us
    unnamed x121, local copies, waits for them, and re-layouts  6.98 us
    ppermute x23, starting transfers between devices, swap(): return lax.ppermute(array, axis, [(0, 1), (1, 0)])  6.77 us
  transfers between devices with their start and end apart: 50, of which 26 were waited for; matrix products, arithmetic and copies ran while one was open for 13% of the time, Pallas kernels for 20%

profile of v4, /device:TPU:0, one launch (start us, length us, event | category | flops | bytes accessed | tf_op | source)
XLA Modules:
  0.0 228.7 jit_solution(8392768264900853865)
XLA Ops:
  8.3 4.1 %collective-permute-start.3 = (bf16[136,1024]{1,0:T(8,128)(2,1)S(1)}, bf16[136,1024]{1,0:T(8,128)(2,1)S(1)}, u32[]{:S(2)}, u32[]{:S(2)}) collective-permute-start(bf16[136,1024]{1,0:T(8,128)(2,1)S(1)} %pad_maximum_fusion.8.refs_0_), channel_id=1, source_target_pairs={{0,16},{4,20},{8,24},{12,28},{16,0},{20,4},{24,8},{28,12},{1,17},{... | collective-permute-start | bytes 835592 | tf_op jit(solution)/shard_map/ppermute | solution.py:34
  17.6 6.7 %collective-permute-done.5.refs_4_ = bf16[160,512]{1,0:T(8,128)(2,1)S(1)} collective-permute-done((bf16[160,512]{1,0:T(8,128)(2,1)S(1)}, bf16[160,512]{1,0:T(8,128)(2,1)S(1)}, u32[]{:S(2)}, u32[]{:S(2)}) %collective-permute-start.5) | collective-permute-done | bytes 163872 | tf_op jit(solution)/shard_map/ppermute | solution.py:34
  27.6 3.4 %collective-permute-start.9 = (bf16[128,1024]{1,0:T(8,128)(2,1)S(1)}, bf16[128,1024]{1,0:T(8,128)(2,1)S(1)}, u32[]{:S(2)}, u32[]{:S(2)}) collective-permute-start(bf16[128,1024]{1,0:T(8,128)(2,1)S(1)} %maximum_select_fusion.3.refs_0_), channel_id=1, source_target_pairs={{0,16},{4,20},{8,24},{12,28},{16,0},{20,4},{24,8},{28,12},{1,17},{... | collective-permute-start | bytes 786440 | tf_op jit(solution)/shard_map/ppermute | solution.py:34
  33.4 10.4 %collective-permute-done.9.refs_1_ = bf16[128,1024]{1,0:T(8,128)(2,1)S(1)} collective-permute-done((bf16[128,1024]{1,0:T(8,128)(2,1)S(1)}, bf16[128,1024]{1,0:T(8,128)(2,1)S(1)}, u32[]{:S(2)}, u32[]{:S(2)}) %collective-permute-start.9) | collective-permute-done | bytes 262176 | tf_op jit(solution)/shard_map/ppermute | solution.py:34
  54.0 11.8 %collective-permute-done.13.refs_7_.refs_1_ = bf16[128,1024]{1,0:T(8,128)(2,1)S(1)} collective-permute-done((bf16[128,1024]{1,0:T(8,128)(2,1)S(1)}, bf16[128,1024]{1,0:T(8,128)(2,1)S(1)}, u32[]{:S(2)}, u32[]{:S(2)}) %collective-permute-start.13) | collective-permute-done | bytes 262176 | tf_op jit(solution)/shard_map/ppermute | solution.py:34
  71.6 7.3 %attention.1 = (bf16[320,256]{1,0:T(8,128)(2,1)}, bf16[320,256]{1,0:T(8,128)(2,1)}, bf16[320,256]{1,0:T(8,128)(2,1)}, bf16[320,256]{1,0:T(8,128)(2,1)}, f32[160,...) custom-call(s32[11]{0:T(128)} %pad_add_fusion.places_ref, ...), custom_call_target="tpu_custom_call" | custom-call | flops 1000 | bytes 1000 | tf_op jit(solution)/shard_map/attention/pallas_call | solution.py:201
  89.5 4.7 %collective-permute-done.20 = bf16[160,1024]{1,0:T(8,128)(2,1)S(1)} collective-permute-done((bf16[160,1024]{1,0:T(8,128)(2,1)S(1)}, bf16[160,1024]{1,0:T(8,128)(2,1)S(1)}, u32[]{:S(2)}, u32[]{:S(2)}) %collective-permute-start.20) | collective-permute-done | bytes 327712 | tf_op jit(solution)/shard_map/ppermute | solution.py:29
  98.3 4.9 %hidden_layer.1 = (bf16[480,1024]{1,0:T(8,128)(2,1)}, f32[320,1024]{1,0:T(8,128)}) custom-call(bf16[160,1024]{1,0:T(8,128)(2,1)} %copy-done.11, bf16[160,1024]{1,0:T(8,128)(2,1)} %copy-done.23, bf16[320,1024]{1,0:T(8,128)(2,1)} %get-tuple-element.166.normed_ref.refs_2_, f32[1,1024]{1,0:T(1,128)} %constant_dynamic-slice_fusion.7.bias_ref, ...), custom_call_target="tpu_custom_call" | custom-call | flops 1000 | bytes 1000 | tf_op jit(solution)/shard_map/hidden_layer/pallas_call | solution.py:279
  103.2 4.7 %collective-permute-done.23.refs_10_.refs_4_ = bf16[384,1024]{1,0:T(8,128)(2,1)S(1)} collective-permute-done((bf16[384,1024]{1,0:T(8,128)(2,1)}, bf16[384,1024]{1,0:T(8,128)(2,1)S(1)}, u32[]{:S(2)}, u32[]{:S(2)}) %collective-permute-start.23) | collective-permute-done | bytes 786464 | tf_op jit(solution)/shard_map/ppermute | solution.py:34
  109.7 6.4 %hidden_back.1 = (bf16[320,1024]{1,0:T(8,128)(2,1)}, f32[160,1024]{1,0:T(8,128)}, bf16[160,1024]{1,0:T(8,128)(2,1)}, f32[1,1024]{1,0:T(1,128)}) custom-call(bf16[160,1024]{1,0:T(8,128)(2,1)} %bitcast.118, bf16[160,1024]{1,0:T(8,128)(2,1)} %copy-done.20, f32[320,1024]{1,0:T(8,128)} %get-tuple-element.175.slope_ref, bf16[128,1024]{1,0:T(8,128)(2,1)} %copy-done.8, ...), custom_call_target="tpu_custom_call" | custom-call | flops 1000 | bytes 1000 | tf_op jit(solution)/shard_map/hidden_back/pallas_call | solution.py:306
  119.8 4.1 %project_back.1 = (f32[160,1024]{1,0:T(8,128)}, bf16[160,1024]{1,0:T(8,128)(2,1)}) custom-call(bf16[480,1024]{1,0:T(8,128)(2,1)} %get-tuple-element.183.values_ref.refs_0_, bf16[128,1024]{1,0:T(8,128)(2,1)} %copy-done.6, bf16[128,1024]{1,0:T(8,128)(2,1)} %copy-done.7, bf16[256,1024]{1,0:T(8,128)(2,1)} %copy-done.4, bf16[128,1024]{1,0:T(8,128)(2,1)} %copy-done.27, ...), custom_call_target="tpu_custom_call" | custom-call | flops 1000 | bytes 1000 | tf_op jit(solution)/shard_map/project_back/pallas_call | solution.py:328
  123.8 5.2 %collective-permute-done.25.other_ref = bf16[160,1024]{1,0:T(8,128)(2,1)S(1)} collective-permute-done((bf16[160,1024]{1,0:T(8,128)(2,1)S(1)}, bf16[160,1024]{1,0:T(8,128)(2,1)S(1)}, u32[]{:S(2)}, u32[]{:S(2)}) %collective-permute-start.25) | collective-permute-done | bytes 327712 | tf_op jit(solution)/shard_map/ppermute | solution.py:29
  130.8 3.3 %second_norm_back.1 = (f32[160,1024]{1,0:T(8,128)}, bf16[160,1024]{1,0:T(8,128)(2,1)}, f32[4,1024]{1,0:T(4,128)}) custom-call(f32[160,1024]{1,0:T(8,128)} %copy-done, f32[1,1024]{1,0:T(1,128)} %copy-done.54, bf16[160,1024]{1,0:T(8,128)(2,1)} %copy-done.22, bf16[160,1024]{1,0:T(8,128)(2,1)} %copy-done.42, bf16[160,1024]{1,0:T(8,128)(2,1)} %bitcast.119), custom_call_target="tpu_custom_call" | custom-call | flops 1000 | bytes 1000 | tf_op jit(solution)/shard_map/second_norm_back/pallas_call | solution.py:421
  137.4 3.8 %weight_grad.3 = (bf16[256,1024]{1,0:T(8,128)(2,1)}, f32[256,1024]{1,0:T(8,128)}) custom-call(bf16[480,1024]{1,0:T(8,128)(2,1)} %get-tuple-element.183.values_ref.refs_0_, bf16[480,1024]{1,0:T(8,128)(2,1)} %copy-done.1, bf16[160,1024]{1,0:T(8,128)(2,1)} %bitcast.120, bf16[160,1024]{1,0:T(8,128)(2,1)} %copy-done.20, bf16[160,512]{1,0:T(8,128)(2,1)} %copy-done.50, ...), custom_call_target="tpu_custom_call" | custom-call | flops 1000 | bytes 1000 | tf_op jit(solution)/shard_map/weight_grad/pallas_call | solution.py:371
  145.7 7.9 %attention_back.1 = (bf16[320,1024]{1,0:T(8,128)(2,1)}, f32[160,1024]{1,0:T(8,128)}, bf16[160,1024]{1,0:T(8,128)(2,1)}, f32[1,512]{1,0:T(1,128)}) custom-call(bf16[160,1024]{1,0:T(8,128)(2,1)} %get-tuple-element.193.grad_own.refs_5_, bf16[160,1024]{1,0:T(8,128)(2,1)} %copy-done.19, bf16[320,256]{1,0:T(8,128)(2,1)} %get-tuple-element.199.context_ref, ...), custom_call_target="tpu_custom_call" | custom-call | flops 1000 | bytes 1000 | tf_op jit(solution)/shard_map/attention_back/pallas_call | solution.py:248
  159.4 3.9 %weight_grad.5 = (bf16[256,1024]{1,0:T(8,128)(2,1)}, f32[256,1024]{1,0:T(8,128)}) custom-call(bf16[320,1024]{1,0:T(8,128)(2,1)} %get-tuple-element.186.refs_0_, bf16[320,1024]{1,0:T(8,128)(2,1)} %collective-permute-done.27.refs_1_, bf16[160,1024]{1,0:T(8,128)(2,1)} %copy-done.11, bf16[160,1024]{1,0:T(8,128)(2,1)} %copy-done.23, bf16[480,1024]{1,0:T(8,128)(2,1)} %copy-done.1, ...), custom_call_target="tpu_custom_call" | custom-call | flops 1000 | bytes 1000 | tf_op jit(solution)/shard_map/weight_grad/pallas_call | solution.py:371
  165.7 6.7 %collective-permute-done.38 = bf16[128,1024]{1,0:T(8,128)(2,1)S(1)} collective-permute-done((bf16[128,1024]{1,0:T(8,128)(2,1)}, bf16[128,1024]{1,0:T(8,128)(2,1)S(1)}, u32[]{:S(2)}, u32[]{:S(2)}) %collective-permute-start.38) | collective-permute-done | bytes 262176 | tf_op jit(solution)/shard_map/ppermute | solution.py:34
  173.2 3.2 %finish.1 = (bf16[160,1024]{1,0:T(8,128)(2,1)}, f32[1,128]{1,0:T(1,128)}) custom-call(s32[11]{0:T(128)} %pad_add_fusion.places_ref, f32[160,1024]{1,0:T(8,128)} %copy-done, f32[160,1024]{1,0:T(8,128)} %get-tuple-element.249.entering_ref, f32[160,1024]{1,0:T(8,128)} %get-tuple-element.248.attended_ref, bf16[160,1024]{1,0:T(8,128)(2,1)} %copy-done.24, ...), custom_call_target="tpu_custom_call" | custom-call | flops 1000 | bytes 1000 | tf_op jit(solution)/shard_map/finish/pallas_call | solution.py:464
  177.9 4.2 %weight_grad.4 = (bf16[128,1024]{1,0:T(8,128)(2,1)}, bf16[128,1024]{1,0:T(8,128)(2,1)}, f32[256,1024]{1,0:T(8,128)}) custom-call(bf16[320,1024]{1,0:T(8,128)(2,1)} %get-tuple-element.211.refs_0_, bf16[320,1024]{1,0:T(8,128)(2,1)} %copy-done.36, bf16[320,1024]{1,0:T(8,128)(2,1)} %get-tuple-element.166.normed_ref.refs_2_, bf16[480,1024]{1,0:T(8,128)(2,1)} %copy-done.1, ...), custom_call_target="tpu_custom_call" | custom-call | flops 1000 | bytes 1000 | tf_op jit(solution)/shard_map/weight_grad/pallas_call | solution.py:371
  183.5 3.0 %first_norm_back.1 = (f32[160,1024]{1,0:T(8,128)}, f32[8,1024]{1,0:T(8,128)}) custom-call(s32[11]{0:T(128)} %pad_add_fusion.places_ref, bf16[160,1024]{1,0:T(8,128)(2,1)} %bitcast.115, f32[1,1024]{1,0:T(1,128)} %get-tuple-element.272.gain_ref, bf16[160,1024]{1,0:T(8,128)(2,1)} %copy-done.21, bf16[160,1024]{1,0:T(8,128)(2,1)} %copy-done.41, ...), custom_call_target="tpu_custom_call" | custom-call | flops 1000 | bytes 1000 | tf_op jit(solution)/shard_map/first_norm_back/pallas_call | solution.py:499
  192.6 10.1 %collective-permute-done.43 = bf16[128,1024]{1,0:T(8,128)(2,1)S(1)} collective-permute-done((bf16[128,1024]{1,0:T(8,128)(2,1)S(1)}, bf16[128,1024]{1,0:T(8,128)(2,1)S(1)}, u32[]{:S(2)}, u32[]{:S(2)}) %collective-permute-start.43) | collective-permute-done | bytes 262176 | tf_op jit(solution)/shard_map/ppermute | solution.py:34
  206.8 2.4 %collective-permute-start.44 = (bf16[144,1024]{1,0:T(8,128)(2,1)S(1)}, bf16[144,1024]{1,0:T(8,128)(2,1)S(1)}, u32[]{:S(2)}, u32[]{:S(2)}) collective-permute-start(bf16[144,1024]{1,0:T(8,128)(2,1)S(1)} %pad_maximum_fusion.7), channel_id=1, source_target_pairs={{0,16},{4,20},{8,24},{12,28},{16,0},{20,4},{24,8},{28,12},{1,17},{... | collective-permute-start | bytes 884744 | tf_op jit(solution)/shard_map/ppermute | solution.py:34
  209.2 5.8 %collective-permute-done.46 = bf16[128,1024]{1,0:T(8,128)(2,1)S(1)} collective-permute-done((bf16[128,1024]{1,0:T(8,128)(2,1)}, bf16[128,1024]{1,0:T(8,128)(2,1)S(1)}, u32[]{:S(2)}, u32[]{:S(2)}) %collective-permute-start.46) | collective-permute-done | bytes 262176 | tf_op jit(solution)/shard_map/ppermute | solution.py:34
  216.3 5.2 %collective-permute-done.44 = bf16[144,1024]{1,0:T(8,128)(2,1)S(1)} collective-permute-done((bf16[144,1024]{1,0:T(8,128)(2,1)S(1)}, bf16[144,1024]{1,0:T(8,128)(2,1)S(1)}, u32[]{:S(2)}, u32[]{:S(2)}) %collective-permute-start.44) | collective-permute-done | bytes 294944 | tf_op jit(solution)/shard_map/ppermute | solution.py:34
  (305 shorter events, 92.8 us)
Async XLA Ops:
  8.3 16.9 %collective-permute-start.3 = (bf16[136,1024]{1,0:T(8,128)(2,1)S(1)}, bf16[136,1024]{1,0:T(8,128)(2,1)S(1)}, u32[]{:S(2)}, u32[]{:S(2)}) collective-permute-start(bf16[136,1024]{1,0:T(8,128)(2,1)S(1)} %pad_maximum_fusion.8.refs_0_), channel_id=1, source_target_pairs={{0,16},{4,20},{8,24},{12,28},{16,0},{20,4},{24,8},{28,12},{1,17},{... | collective-permute-start | bytes 835592 | tf_op jit(solution)/shard_map/ppermute | solution.py:34
  12.4 12.8 %collective-permute-start.4 = (bf16[136,1024]{1,0:T(8,128)(2,1)S(1)}, bf16[136,1024]{1,0:T(8,128)(2,1)S(1)}, u32[]{:S(2)}, u32[]{:S(2)}) collective-permute-start(bf16[136,1024]{1,0:T(8,128)(2,1)S(1)} %pad_maximum_fusion.8.refs_0_), channel_id=1, source_target_pairs={{0,4},{4,0},{8,12},{12,8},{16,20},{20,16},{24,28},{28,24},{1,5},{5... | collective-permute-start | bytes 835592 | tf_op jit(solution)/shard_map/ppermute | solution.py:34
  16.4 15.1 %collective-permute-start.2 = (bf16[160,1024]{1,0:T(8,128)(2,1)S(1)}, bf16[160,1024]{1,0:T(8,128)(2,1)S(1)}, u32[]{:S(2)}, u32[]{:S(2)}) collective-permute-start(bf16[160,1024]{1,0:T(8,128)(2,1)S(1)} %bitcast.111), channel_id=1, source_target_pairs={{0,2},{2,0},{1,3},{3,1},{4,6},{6,4},{5,7},{7,5},{8,10},{10,8},{9,1... | collective-permute-start | bytes 983048 | tf_op jit(solution)/shard_map/ppermute | solution.py:29
  25.3 20.4 %collective-permute-start.8 = (bf16[272,1024]{1,0:T(8,128)(2,1)S(1)}, bf16[272,1024]{1,0:T(8,128)(2,1)S(1)}, u32[]{:S(2)}, u32[]{:S(2)}) collective-permute-start(bf16[272,1024]{1,0:T(8,128)(2,1)S(1)} %pad_maximum_fusion.2), channel_id=1, source_target_pairs={{0,8},{4,12},{8,0},{12,4},{16,24},{20,28},{24,16},{28,20},{1,9},{5... | collective-permute-start | bytes 1671176 | tf_op jit(solution)/shard_map/ppermute | solution.py:34
  26.2 19.5 %collective-permute-start.10 = (bf16[136,1024]{1,0:T(8,128)(2,1)S(1)}, bf16[136,1024]{1,0:T(8,128)(2,1)S(1)}, u32[]{:S(2)}, u32[]{:S(2)}) collective-permute-start(bf16[136,1024]{1,0:T(8,128)(2,1)S(1)} %collective-permute-done.3.refs_1_), channel_id=1, source_target_pairs={{0,4},{4,0},{8,12},{12,8},{16,20},{20,16},{24,28},{28,24},{1,5},{5... | collective-permute-start | bytes 835592 | tf_op jit(solution)/shard_map/ppermute | solution.py:34
  27.6 16.1 %collective-permute-start.9 = (bf16[128,1024]{1,0:T(8,128)(2,1)S(1)}, bf16[128,1024]{1,0:T(8,128)(2,1)S(1)}, u32[]{:S(2)}, u32[]{:S(2)}) collective-permute-start(bf16[128,1024]{1,0:T(8,128)(2,1)S(1)} %maximum_select_fusion.3.refs_0_), channel_id=1, source_target_pairs={{0,16},{4,20},{8,24},{12,28},{16,0},{20,4},{24,8},{28,12},{1,17},{... | collective-permute-start | bytes 786440 | tf_op jit(solution)/shard_map/ppermute | solution.py:34
  31.6 14.1 %collective-permute-start.12 = (bf16[128,1024]{1,0:T(8,128)(2,1)S(1)}, bf16[128,1024]{1,0:T(8,128)(2,1)S(1)}, u32[]{:S(2)}, u32[]{:S(2)}) collective-permute-start(bf16[128,1024]{1,0:T(8,128)(2,1)S(1)} %maximum_select_fusion.4.refs_6_.refs_0_), channel_id=1, source_target_pairs={{0,4},{4,0},{8,12},{12,8},{16,20},{20,16},{24,28},{28,24},{1,5},{5... | collective-permute-start | bytes 786440 | tf_op jit(solution)/shard_map/ppermute | solution.py:34
  45.7 20.9 %collective-permute-start.14 = (bf16[272,1024]{1,0:T(8,128)(2,1)S(1)}, bf16[272,1024]{1,0:T(8,128)(2,1)S(1)}, u32[]{:S(2)}, u32[]{:S(2)}) collective-permute-start(bf16[272,1024]{1,0:T(8,128)(2,1)S(1)} %collective-permute-done.8.refs_2_), channel_id=1, source_target_pairs={{0,4},{4,0},{8,12},{12,8},{16,20},{20,16},{24,28},{28,24},{1,5},{5... | collective-permute-start | bytes 1671176 | tf_op jit(solution)/shard_map/ppermute | solution.py:34
  47.3 19.3 %collective-permute-start.16 = (bf16[256,1024]{1,0:T(8,128)(2,1)S(1)}, bf16[256,1024]{1,0:T(8,128)(2,1)}, u32[]{:S(2)}, u32[]{:S(2)}) collective-permute-start(bf16[256,1024]{1,0:T(8,128)(2,1)S(1)} %pad_maximum_fusion.3), channel_id=1, source_target_pairs={{0,8},{4,12},{8,0},{12,4},{16,24},{20,28},{24,16},{28,20},{1,9},{5... | collective-permute-start | bytes 1572872 | tf_op jit(solution)/shard_map/ppermute | solution.py:34
  50.0 15.7 %collective-permute-start.15 = (bf16[128,1024]{1,0:T(8,128)(2,1)S(1)}, bf16[128,1024]{1,0:T(8,128)(2,1)S(1)}, u32[]{:S(2)}, u32[]{:S(2)}) collective-permute-start(bf16[128,1024]{1,0:T(8,128)(2,1)S(1)} %collective-permute-done.9.refs_1_), channel_id=1, source_target_pairs={{0,4},{4,0},{8,12},{12,8},{16,20},{20,16},{24,28},{28,24},{1,5},{5... | collective-permute-start | bytes 786440 | tf_op jit(solution)/shard_map/ppermute | solution.py:34
  50.6 15.1 %collective-permute-start.13 = (bf16[128,1024]{1,0:T(8,128)(2,1)S(1)}, bf16[128,1024]{1,0:T(8,128)(2,1)S(1)}, u32[]{:S(2)}, u32[]{:S(2)}) collective-permute-start(bf16[128,1024]{1,0:T(8,128)(2,1)S(1)} %maximum_select_fusion.4.refs_6_.refs_0_), channel_id=1, source_target_pairs={{0,16},{4,20},{8,24},{12,28},{16,0},{20,4},{24,8},{28,12},{1,17},{... | collective-permute-start | bytes 786440 | tf_op jit(solution)/shard_map/ppermute | solution.py:34
  88.4 19.5 %collective-permute-start.23 = (bf16[384,1024]{1,0:T(8,128)(2,1)}, bf16[384,1024]{1,0:T(8,128)(2,1)S(1)}, u32[]{:S(2)}, u32[]{:S(2)}) collective-permute-start(bf16[384,1024]{1,0:T(8,128)(2,1)} %pad_maximum_fusion), channel_id=1, source_target_pairs={{0,4},{4,0},{8,12},{12,8},{16,20},{20,16},{24,28},{28,24},{1,5},{5... | collective-permute-start | bytes 2359304 | tf_op jit(solution)/shard_map/ppermute | solution.py:34
  95.9 13.1 %collective-permute-start.21 = (bf16[160,1024]{1,0:T(8,128)(2,1)S(1)}, bf16[160,1024]{1,0:T(8,128)(2,1)S(1)}, u32[]{:S(2)}, u32[]{:S(2)}) collective-permute-start(bf16[160,1024]{1,0:T(8,128)(2,1)S(1)} %bitcast.117), channel_id=1, source_target_pairs={{0,2},{2,0},{1,3},{3,1},{4,6},{6,4},{5,7},{7,5},{8,10},{10,8},{9,1... | collective-permute-start | bytes 983048 | tf_op jit(solution)/shard_map/ppermute | solution.py:29
  107.9 22.9 %collective-permute-start.26 = (bf16[480,1024]{1,0:T(8,128)(2,1)}, bf16[480,1024]{1,0:T(8,128)(2,1)S(1)}, u32[]{:S(2)}, u32[]{:S(2)}) collective-permute-start(bf16[480,1024]{1,0:T(8,128)(2,1)} %get-tuple-element.183.values_ref.refs_0_), channel_id=1, source_target_pairs={{0,4},{4,0},{8,12},{12,8},{16,20},{20,16},{24,28},{28,24},{1,5},{5... | collective-permute-start | bytes 2949128 | tf_op jit(solution)/shard_map/ppermute | solution.py:34
  134.7 20.7 %collective-permute-start.27 = (bf16[320,1024]{1,0:T(8,128)(2,1)S(1)}, bf16[320,1024]{1,0:T(8,128)(2,1)}, u32[]{:S(2)}, u32[]{:S(2)}) collective-permute-start(bf16[320,1024]{1,0:T(8,128)(2,1)S(1)} %copy-done.35), channel_id=1, source_target_pairs={{0,4},{4,0},{8,12},{12,8},{16,20},{20,16},{24,28},{28,24},{1,5},{5... | collective-permute-start | bytes 1966088 | tf_op jit(solution)/shard_map/ppermute | solution.py:34
  141.1 14.3 %collective-permute-start.31 = (bf16[256,1024]{1,0:T(8,128)(2,1)}, bf16[256,1024]{1,0:T(8,128)(2,1)S(1)}, u32[]{:S(2)}, u32[]{:S(2)}) collective-permute-start(bf16[256,1024]{1,0:T(8,128)(2,1)} %get-tuple-element.197), channel_id=1, source_target_pairs={{0,8},{4,12},{8,0},{12,4},{16,24},{20,28},{24,16},{28,20},{1,9},{5... | collective-permute-start | bytes 1572872 | tf_op jit(solution)/shard_map/ppermute | solution.py:34
  141.8 13.6 %collective-permute-start.33 = (bf16[160,1024]{1,0:T(8,128)(2,1)S(1)}, bf16[160,1024]{1,0:T(8,128)(2,1)S(1)}, u32[]{:S(2)}, u32[]{:S(2)}) collective-permute-start(bf16[160,1024]{1,0:T(8,128)(2,1)S(1)} %reduce-precision_convert_fusion.1.low_ref), channel_id=1, source_target_pairs={{0,1},{1,0},{2,3},{3,2},{4,5},{5,4},{6,7},{7,6},{8,9},{9,8},{10,11... | collective-permute-start | bytes 983048 | tf_op jit(solution)/shard_map/ppermute | solution.py:29
  145.7 13.0 %collective-permute-start.35 = (bf16[160,1024]{1,0:T(8,128)(2,1)}, bf16[160,1024]{1,0:T(8,128)(2,1)S(1)}, u32[]{:S(2)}, u32[]{:S(2)}) collective-permute-start(bf16[160,1024]{1,0:T(8,128)(2,1)} %slice.192), channel_id=1, source_target_pairs={{0,2},{2,0},{1,3},{3,1},{4,6},{6,4},{5,7},{7,5},{8,10},{10,8},{9,1... | collective-permute-start | bytes 983048 | tf_op jit(solution)/shard_map/ppermute | solution.py:29
  155.6 20.9 %collective-permute-start.34 = (bf16[320,1024]{1,0:T(8,128)(2,1)}, bf16[320,1024]{1,0:T(8,128)(2,1)S(1)}, u32[]{:S(2)}, u32[]{:S(2)}) collective-permute-start(bf16[320,1024]{1,0:T(8,128)(2,1)} %get-tuple-element.211.refs_0_), channel_id=1, source_target_pairs={{0,4},{4,0},{8,12},{12,8},{16,20},{20,16},{24,28},{28,24},{1,5},{5... | collective-permute-start | bytes 1966088 | tf_op jit(solution)/shard_map/ppermute | solution.py:34
  157.5 14.9 %collective-permute-start.38 = (bf16[128,1024]{1,0:T(8,128)(2,1)}, bf16[128,1024]{1,0:T(8,128)(2,1)S(1)}, u32[]{:S(2)}, u32[]{:S(2)}) collective-permute-start(bf16[128,1024]{1,0:T(8,128)(2,1)} %reduce-precision_convert_fusion.6), channel_id=1, source_target_pairs={{0,16},{4,20},{8,24},{12,28},{16,0},{20,4},{24,8},{28,12},{1,17},{... | collective-permute-start | bytes 786440 | tf_op jit(solution)/shard_map/ppermute | solution.py:34
  163.2 19.5 %collective-permute-start.40 = (bf16[256,1024]{1,0:T(8,128)(2,1)}, bf16[256,1024]{1,0:T(8,128)(2,1)}, u32[]{:S(2)}, u32[]{:S(2)}) collective-permute-start(bf16[256,1024]{1,0:T(8,128)(2,1)} %get-tuple-element.221), channel_id=1, source_target_pairs={{0,8},{4,12},{8,0},{12,4},{16,24},{20,28},{24,16},{28,20},{1,9},{5... | collective-permute-start | bytes 1572872 | tf_op jit(solution)/shard_map/ppermute | solution.py:34
  188.5 14.2 %collective-permute-start.43 = (bf16[128,1024]{1,0:T(8,128)(2,1)S(1)}, bf16[128,1024]{1,0:T(8,128)(2,1)S(1)}, u32[]{:S(2)}, u32[]{:S(2)}) collective-permute-start(bf16[128,1024]{1,0:T(8,128)(2,1)S(1)} %reduce-precision_convert_fusion.5), channel_id=1, source_target_pairs={{0,16},{4,20},{8,24},{12,28},{16,0},{20,4},{24,8},{28,12},{1,17},{... | collective-permute-start | bytes 786440 | tf_op jit(solution)/shard_map/ppermute | solution.py:34
  191.5 13.2 %collective-permute-start.42 = (bf16[144,1024]{1,0:T(8,128)(2,1)S(1)}, bf16[144,1024]{1,0:T(8,128)(2,1)S(1)}, u32[]{:S(2)}, u32[]{:S(2)}) collective-permute-start(bf16[144,1024]{1,0:T(8,128)(2,1)S(1)} %pad_maximum_fusion.6), channel_id=1, source_target_pairs={{0,8},{4,12},{8,0},{12,4},{16,24},{20,28},{24,16},{28,20},{1,9},{5... | collective-permute-start | bytes 884744 | tf_op jit(solution)/shard_map/ppermute | solution.py:34
  206.8 14.6 %collective-permute-start.44 = (bf16[144,1024]{1,0:T(8,128)(2,1)S(1)}, bf16[144,1024]{1,0:T(8,128)(2,1)S(1)}, u32[]{:S(2)}, u32[]{:S(2)}) collective-permute-start(bf16[144,1024]{1,0:T(8,128)(2,1)S(1)} %pad_maximum_fusion.7), channel_id=1, source_target_pairs={{0,16},{4,20},{8,24},{12,28},{16,0},{20,4},{24,8},{28,12},{1,17},{... | collective-permute-start | bytes 884744 | tf_op jit(solution)/shard_map/ppermute | solution.py:34
  (81 other events, 805.1 us)

commit v5 on v4

--- a/solution.py
+++ b/solution.py
@@ -675,9 +675,13 @@
         d_near, u_near_x, d_far, att_own, att_other = tie(
             d_near, u_near_x, d_far, att_own, att_other
         )
-        d_rest_x = flip(rows_of(d_far, d_near), X_BIT)
+        d_rest = rows_of(d_far, d_near)
         up_pieces = [u, u_far, u_near, u_x, u_far_x, u_near_x]
-    att_low, att_tp = halves_low(att_own, att_other)
+    att_low = round_low(att_own + swap(att_other, "ctx").astype(F32))
+    if cube:
+        att_low, d_rest = tie(att_low, d_rest)
+        d_rest_x = flip(d_rest, X_BIT)
+    att_tp = swap(att_low, "tp")
     attended = att_low.astype(F32) + att_tp.astype(F32) + proj_bias
     entering = entering_all[:own_slots]
     middle = entering + attended

time: 230 us -> 227 us (0.987)
    unnamed x121 -> x123, local copies, waits for them, and re-layouts: 6.98 us -> 6.97 us
where the time goes in v5:
time: 227 us
  waiting for transfers between devices  90.3 us (40%)
  Pallas kernels  52 us (23%)
  starting transfers between devices  41.7 us (18%)
  other arithmetic  19.9 us (9%)
  local copies, waits for them, and re-layouts  19.7 us (9%)
  between operations  2.93 us (1%)
    ppermute x27, waiting for transfers between devices, flip(): return lax.ppermute(array, 'fsdp', [(i, i ^ bit) for i in range(n)])  74.9 us
    ppermute x27, starting transfers between devices, flip(): return lax.ppermute(array, 'fsdp', [(i, i ^ bit) for i in range(n)])  35 us
    ppermute x23, waiting for transfers between devices, swap(): return lax.ppermute(array, axis, [(0, 1), (1, 0)])  15.4 us
    pallas_call x3, Pallas kernels, weight_grad(): pl.pallas_call(kernel, name='weight_grad', out_shape=[shape_of(size, colu...  11.8 us
    pallas_call x1, Pallas kernels, attention_back(): pl.pallas_call(kernel, name='attention_back', out_shape=[shape_of(slots,...  7.91 us
    pallas_call x1, Pallas kernels, attention(): pl.pallas_call(kernel, name='attention', in_specs=[pl.BlockSpec(memory_sp...  7.27 us
    unnamed x123, local copies, waits for them, and re-layouts  6.97 us
    ppermute x23, starting transfers between devices, swap(): return lax.ppermute(array, axis, [(0, 1), (1, 0)])  6.77 us
  transfers between devices with their start and end apart: 50, of which 26 were waited for; matrix products, arithmetic and copies ran while one was open for 13% of the time, Pallas kernels for 20%

profile of v5, /device:TPU:0, one launch (start us, length us, event | category | flops | bytes accessed | tf_op | source)
XLA Modules:
  0.0 226.6 jit_solution(8201673113554797908)
XLA Ops:
  8.3 4.1 %collective-permute-start.3 = (bf16[136,1024]{1,0:T(8,128)(2,1)S(1)}, bf16[136,1024]{1,0:T(8,128)(2,1)S(1)}, u32[]{:S(2)}, u32[]{:S(2)}) collective-permute-start(bf16[136,1024]{1,0:T(8,128)(2,1)S(1)} %pad_maximum_fusion.8.refs_0_), channel_id=1, source_target_pairs={{0,16},{4,20},{8,24},{12,28},{16,0},{20,4},{24,8},{28,12},{1,17},{... | collective-permute-start | bytes 835592 | tf_op jit(solution)/shard_map/ppermute | solution.py:34
  17.6 6.7 %collective-permute-done.5.refs_4_ = bf16[160,512]{1,0:T(8,128)(2,1)S(1)} collective-permute-done((bf16[160,512]{1,0:T(8,128)(2,1)S(1)}, bf16[160,512]{1,0:T(8,128)(2,1)S(1)}, u32[]{:S(2)}, u32[]{:S(2)}) %collective-permute-start.5) | collective-permute-done | bytes 163872 | tf_op jit(solution)/shard_map/ppermute | solution.py:34
  27.6 3.4 %collective-permute-start.9 = (bf16[128,1024]{1,0:T(8,128)(2,1)S(1)}, bf16[128,1024]{1,0:T(8,128)(2,1)S(1)}, u32[]{:S(2)}, u32[]{:S(2)}) collective-permute-start(bf16[128,1024]{1,0:T(8,128)(2,1)S(1)} %maximum_select_fusion.3.refs_0_), channel_id=1, source_target_pairs={{0,16},{4,20},{8,24},{12,28},{16,0},{20,4},{24,8},{28,12},{1,17},{... | collective-permute-start | bytes 786440 | tf_op jit(solution)/shard_map/ppermute | solution.py:34
  33.4 10.4 %collective-permute-done.9.refs_1_ = bf16[128,1024]{1,0:T(8,128)(2,1)S(1)} collective-permute-done((bf16[128,1024]{1,0:T(8,128)(2,1)S(1)}, bf16[128,1024]{1,0:T(8,128)(2,1)S(1)}, u32[]{:S(2)}, u32[]{:S(2)}) %collective-permute-start.9) | collective-permute-done | bytes 262176 | tf_op jit(solution)/shard_map/ppermute | solution.py:34
  54.0 11.8 %collective-permute-done.13.refs_7_.refs_1_ = bf16[128,1024]{1,0:T(8,128)(2,1)S(1)} collective-permute-done((bf16[128,1024]{1,0:T(8,128)(2,1)S(1)}, bf16[128,1024]{1,0:T(8,128)(2,1)S(1)}, u32[]{:S(2)}, u32[]{:S(2)}) %collective-permute-start.13) | collective-permute-done | bytes 262176 | tf_op jit(solution)/shard_map/ppermute | solution.py:34
  71.5 7.3 %attention.1 = (bf16[320,256]{1,0:T(8,128)(2,1)}, bf16[320,256]{1,0:T(8,128)(2,1)}, bf16[320,256]{1,0:T(8,128)(2,1)}, bf16[320,256]{1,0:T(8,128)(2,1)}, f32[160,...) custom-call(s32[11]{0:T(128)} %pad_add_fusion.places_ref, ...), custom_call_target="tpu_custom_call" | custom-call | flops 1000 | bytes 1000 | tf_op jit(solution)/shard_map/attention/pallas_call | solution.py:201
  87.4 5.6 %collective-permute-done.20 = bf16[160,1024]{1,0:T(8,128)(2,1)S(1)} collective-permute-done((bf16[160,1024]{1,0:T(8,128)(2,1)S(1)}, bf16[160,1024]{1,0:T(8,128)(2,1)S(1)}, u32[]{:S(2)}, u32[]{:S(2)}) %collective-permute-start.20) | collective-permute-done | bytes 327712 | tf_op jit(solution)/shard_map/ppermute | solution.py:29
  97.1 5.0 %hidden_layer.1 = (bf16[480,1024]{1,0:T(8,128)(2,1)}, f32[320,1024]{1,0:T(8,128)}) custom-call(bf16[160,1024]{1,0:T(8,128)(2,1)} %copy-done.11, bf16[160,1024]{1,0:T(8,128)(2,1)} %copy-done.23, bf16[320,1024]{1,0:T(8,128)(2,1)} %get-tuple-element.171.normed_ref.refs_2_, f32[1,1024]{1,0:T(1,128)} %constant_dynamic-slice_fusion.7.bias_ref, ...), custom_call_target="tpu_custom_call" | custom-call | flops 1000 | bytes 1000 | tf_op jit(solution)/shard_map/hidden_layer/pallas_call | solution.py:279
  102.1 3.8 %collective-permute-done.23.refs_10_.refs_4_ = bf16[384,1024]{1,0:T(8,128)(2,1)S(1)} collective-permute-done((bf16[384,1024]{1,0:T(8,128)(2,1)}, bf16[384,1024]{1,0:T(8,128)(2,1)S(1)}, u32[]{:S(2)}, u32[]{:S(2)}) %collective-permute-start.23) | collective-permute-done | bytes 786464 | tf_op jit(solution)/shard_map/ppermute | solution.py:34
  107.7 6.4 %hidden_back.1 = (bf16[320,1024]{1,0:T(8,128)(2,1)}, f32[160,1024]{1,0:T(8,128)}, bf16[160,1024]{1,0:T(8,128)(2,1)}, f32[1,1024]{1,0:T(1,128)}) custom-call(bf16[160,1024]{1,0:T(8,128)(2,1)} %bitcast.118, bf16[160,1024]{1,0:T(8,128)(2,1)} %copy-done.20, f32[320,1024]{1,0:T(8,128)} %get-tuple-element.179.slope_ref, bf16[128,1024]{1,0:T(8,128)(2,1)} %copy-done.8, ...), custom_call_target="tpu_custom_call" | custom-call | flops 1000 | bytes 1000 | tf_op jit(solution)/shard_map/hidden_back/pallas_call | solution.py:306
  117.7 4.1 %project_back.1 = (f32[160,1024]{1,0:T(8,128)}, bf16[160,1024]{1,0:T(8,128)(2,1)}) custom-call(bf16[480,1024]{1,0:T(8,128)(2,1)} %get-tuple-element.187.values_ref.refs_0_, bf16[128,1024]{1,0:T(8,128)(2,1)} %copy-done.6, bf16[128,1024]{1,0:T(8,128)(2,1)} %copy-done.7, bf16[256,1024]{1,0:T(8,128)(2,1)} %copy-done.4, bf16[128,1024]{1,0:T(8,128)(2,1)} %copy-done.27, ...), custom_call_target="tpu_custom_call" | custom-call | flops 1000 | bytes 1000 | tf_op jit(solution)/shard_map/project_back/pallas_call | solution.py:328
  121.8 5.2 %collective-permute-done.25.other_ref = bf16[160,1024]{1,0:T(8,128)(2,1)S(1)} collective-permute-done((bf16[160,1024]{1,0:T(8,128)(2,1)S(1)}, bf16[160,1024]{1,0:T(8,128)(2,1)S(1)}, u32[]{:S(2)}, u32[]{:S(2)}) %collective-permute-start.25) | collective-permute-done | bytes 327712 | tf_op jit(solution)/shard_map/ppermute | solution.py:29
  128.7 3.3 %second_norm_back.1 = (f32[160,1024]{1,0:T(8,128)}, bf16[160,1024]{1,0:T(8,128)(2,1)}, f32[4,1024]{1,0:T(4,128)}) custom-call(f32[160,1024]{1,0:T(8,128)} %copy-done, f32[1,1024]{1,0:T(1,128)} %copy-done.55, bf16[160,1024]{1,0:T(8,128)(2,1)} %copy-done.22, bf16[160,1024]{1,0:T(8,128)(2,1)} %copy-done.43, bf16[160,1024]{1,0:T(8,128)(2,1)} %bitcast.119), custom_call_target="tpu_custom_call" | custom-call | flops 1000 | bytes 1000 | tf_op jit(solution)/shard_map/second_norm_back/pallas_call | solution.py:421
  135.3 3.8 %weight_grad.3 = (bf16[256,1024]{1,0:T(8,128)(2,1)}, f32[256,1024]{1,0:T(8,128)}) custom-call(bf16[480,1024]{1,0:T(8,128)(2,1)} %get-tuple-element.187.values_ref.refs_0_, bf16[480,1024]{1,0:T(8,128)(2,1)} %copy-done.1, bf16[160,1024]{1,0:T(8,128)(2,1)} %bitcast.120, bf16[160,1024]{1,0:T(8,128)(2,1)} %copy-done.20, bf16[160,512]{1,0:T(8,128)(2,1)} %copy-done.51, ...), custom_call_target="tpu_custom_call" | custom-call | flops 1000 | bytes 1000 | tf_op jit(solution)/shard_map/weight_grad/pallas_call | solution.py:371
  143.6 7.9 %attention_back.1 = (bf16[320,1024]{1,0:T(8,128)(2,1)}, f32[160,1024]{1,0:T(8,128)}, bf16[160,1024]{1,0:T(8,128)(2,1)}, f32[1,512]{1,0:T(1,128)}) custom-call(bf16[160,1024]{1,0:T(8,128)(2,1)} %get-tuple-element.197.grad_own.refs_5_, bf16[160,1024]{1,0:T(8,128)(2,1)} %copy-done.19, bf16[320,256]{1,0:T(8,128)(2,1)} %get-tuple-element.203.context_ref, ...), custom_call_target="tpu_custom_call" | custom-call | flops 1000 | bytes 1000 | tf_op jit(solution)/shard_map/attention_back/pallas_call | solution.py:248
  157.3 3.9 %weight_grad.5 = (bf16[256,1024]{1,0:T(8,128)(2,1)}, f32[256,1024]{1,0:T(8,128)}) custom-call(bf16[320,1024]{1,0:T(8,128)(2,1)} %get-tuple-element.190.refs_0_, bf16[320,1024]{1,0:T(8,128)(2,1)} %collective-permute-done.27.refs_1_, bf16[160,1024]{1,0:T(8,128)(2,1)} %copy-done.11, bf16[160,1024]{1,0:T(8,128)(2,1)} %copy-done.23, bf16[480,1024]{1,0:T(8,128)(2,1)} %copy-done.1, ...), custom_call_target="tpu_custom_call" | custom-call | flops 1000 | bytes 1000 | tf_op jit(solution)/shard_map/weight_grad/pallas_call | solution.py:371
  163.6 6.7 %collective-permute-done.38 = bf16[128,1024]{1,0:T(8,128)(2,1)S(1)} collective-permute-done((bf16[128,1024]{1,0:T(8,128)(2,1)}, bf16[128,1024]{1,0:T(8,128)(2,1)S(1)}, u32[]{:S(2)}, u32[]{:S(2)}) %collective-permute-start.38) | collective-permute-done | bytes 262176 | tf_op jit(solution)/shard_map/ppermute | solution.py:34
  171.1 3.2 %finish.1 = (bf16[160,1024]{1,0:T(8,128)(2,1)}, f32[1,128]{1,0:T(1,128)}) custom-call(s32[11]{0:T(128)} %pad_add_fusion.places_ref, f32[160,1024]{1,0:T(8,128)} %copy-done, f32[160,1024]{1,0:T(8,128)} %get-tuple-element.253.entering_ref, f32[160,1024]{1,0:T(8,128)} %get-tuple-element.252.attended_ref, bf16[160,1024]{1,0:T(8,128)(2,1)} %copy-done.24, ...), custom_call_target="tpu_custom_call" | custom-call | flops 1000 | bytes 1000 | tf_op jit(solution)/shard_map/finish/pallas_call | solution.py:464
  175.8 4.2 %weight_grad.4 = (bf16[128,1024]{1,0:T(8,128)(2,1)}, bf16[128,1024]{1,0:T(8,128)(2,1)}, f32[256,1024]{1,0:T(8,128)}) custom-call(bf16[320,1024]{1,0:T(8,128)(2,1)} %get-tuple-element.215.refs_0_, bf16[320,1024]{1,0:T(8,128)(2,1)} %copy-done.37, bf16[320,1024]{1,0:T(8,128)(2,1)} %get-tuple-element.171.normed_ref.refs_2_, bf16[480,1024]{1,0:T(8,128)(2,1)} %copy-done.1, ...), custom_call_target="tpu_custom_call" | custom-call | flops 1000 | bytes 1000 | tf_op jit(solution)/shard_map/weight_grad/pallas_call | solution.py:371
  181.4 3.0 %first_norm_back.1 = (f32[160,1024]{1,0:T(8,128)}, f32[8,1024]{1,0:T(8,128)}) custom-call(s32[11]{0:T(128)} %pad_add_fusion.places_ref, bf16[160,1024]{1,0:T(8,128)(2,1)} %bitcast.115, f32[1,1024]{1,0:T(1,128)} %get-tuple-element.276.gain_ref, bf16[160,1024]{1,0:T(8,128)(2,1)} %copy-done.21, bf16[160,1024]{1,0:T(8,128)(2,1)} %copy-done.42, ...), custom_call_target="tpu_custom_call" | custom-call | flops 1000 | bytes 1000 | tf_op jit(solution)/shard_map/first_norm_back/pallas_call | solution.py:499
  190.6 10.0 %collective-permute-done.43 = bf16[128,1024]{1,0:T(8,128)(2,1)S(1)} collective-permute-done((bf16[128,1024]{1,0:T(8,128)(2,1)S(1)}, bf16[128,1024]{1,0:T(8,128)(2,1)S(1)}, u32[]{:S(2)}, u32[]{:S(2)}) %collective-permute-start.43) | collective-permute-done | bytes 262176 | tf_op jit(solution)/shard_map/ppermute | solution.py:34
  204.7 2.4 %collective-permute-start.44 = (bf16[144,1024]{1,0:T(8,128)(2,1)S(1)}, bf16[144,1024]{1,0:T(8,128)(2,1)S(1)}, u32[]{:S(2)}, u32[]{:S(2)}) collective-permute-start(bf16[144,1024]{1,0:T(8,128)(2,1)S(1)} %pad_maximum_fusion.7), channel_id=1, source_target_pairs={{0,16},{4,20},{8,24},{12,28},{16,0},{20,4},{24,8},{28,12},{1,17},{... | collective-permute-start | bytes 884744 | tf_op jit(solution)/shard_map/ppermute | solution.py:34
  207.1 5.8 %collective-permute-done.46 = bf16[128,1024]{1,0:T(8,128)(2,1)S(1)} collective-permute-done((bf16[128,1024]{1,0:T(8,128)(2,1)}, bf16[128,1024]{1,0:T(8,128)(2,1)S(1)}, u32[]{:S(2)}, u32[]{:S(2)}) %collective-permute-start.46) | collective-permute-done | bytes 262176 | tf_op jit(solution)/shard_map/ppermute | solution.py:34
  214.1 5.2 %collective-permute-done.44 = bf16[144,1024]{1,0:T(8,128)(2,1)S(1)} collective-permute-done((bf16[144,1024]{1,0:T(8,128)(2,1)S(1)}, bf16[144,1024]{1,0:T(8,128)(2,1)S(1)}, u32[]{:S(2)}, u32[]{:S(2)}) %collective-permute-start.44) | collective-permute-done | bytes 294944 | tf_op jit(solution)/shard_map/ppermute | solution.py:34
  (307 shorter events, 90.7 us)
Async XLA Ops:
  8.3 16.9 %collective-permute-start.3 = (bf16[136,1024]{1,0:T(8,128)(2,1)S(1)}, bf16[136,1024]{1,0:T(8,128)(2,1)S(1)}, u32[]{:S(2)}, u32[]{:S(2)}) collective-permute-start(bf16[136,1024]{1,0:T(8,128)(2,1)S(1)} %pad_maximum_fusion.8.refs_0_), channel_id=1, source_target_pairs={{0,16},{4,20},{8,24},{12,28},{16,0},{20,4},{24,8},{28,12},{1,17},{... | collective-permute-start | bytes 835592 | tf_op jit(solution)/shard_map/ppermute | solution.py:34
  12.4 12.8 %collective-permute-start.4 = (bf16[136,1024]{1,0:T(8,128)(2,1)S(1)}, bf16[136,1024]{1,0:T(8,128)(2,1)S(1)}, u32[]{:S(2)}, u32[]{:S(2)}) collective-permute-start(bf16[136,1024]{1,0:T(8,128)(2,1)S(1)} %pad_maximum_fusion.8.refs_0_), channel_id=1, source_target_pairs={{0,4},{4,0},{8,12},{12,8},{16,20},{20,16},{24,28},{28,24},{1,5},{5... | collective-permute-start | bytes 835592 | tf_op jit(solution)/shard_map/ppermute | solution.py:34
  16.4 15.1 %collective-permute-start.2 = (bf16[160,1024]{1,0:T(8,128)(2,1)S(1)}, bf16[160,1024]{1,0:T(8,128)(2,1)S(1)}, u32[]{:S(2)}, u32[]{:S(2)}) collective-permute-start(bf16[160,1024]{1,0:T(8,128)(2,1)S(1)} %bitcast.111), channel_id=1, source_target_pairs={{0,2},{2,0},{1,3},{3,1},{4,6},{6,4},{5,7},{7,5},{8,10},{10,8},{9,1... | collective-permute-start | bytes 983048 | tf_op jit(solution)/shard_map/ppermute | solution.py:29
  25.3 20.4 %collective-permute-start.8 = (bf16[272,1024]{1,0:T(8,128)(2,1)S(1)}, bf16[272,1024]{1,0:T(8,128)(2,1)S(1)}, u32[]{:S(2)}, u32[]{:S(2)}) collective-permute-start(bf16[272,1024]{1,0:T(8,128)(2,1)S(1)} %pad_maximum_fusion.2), channel_id=1, source_target_pairs={{0,8},{4,12},{8,0},{12,4},{16,24},{20,28},{24,16},{28,20},{1,9},{5... | collective-permute-start | bytes 1671176 | tf_op jit(solution)/shard_map/ppermute | solution.py:34
  26.2 19.5 %collective-permute-start.10 = (bf16[136,1024]{1,0:T(8,128)(2,1)S(1)}, bf16[136,1024]{1,0:T(8,128)(2,1)S(1)}, u32[]{:S(2)}, u32[]{:S(2)}) collective-permute-start(bf16[136,1024]{1,0:T(8,128)(2,1)S(1)} %collective-permute-done.3.refs_1_), channel_id=1, source_target_pairs={{0,4},{4,0},{8,12},{12,8},{16,20},{20,16},{24,28},{28,24},{1,5},{5... | collective-permute-start | bytes 835592 | tf_op jit(solution)/shard_map/ppermute | solution.py:34
  27.6 16.1 %collective-permute-start.9 = (bf16[128,1024]{1,0:T(8,128)(2,1)S(1)}, bf16[128,1024]{1,0:T(8,128)(2,1)S(1)}, u32[]{:S(2)}, u32[]{:S(2)}) collective-permute-start(bf16[128,1024]{1,0:T(8,128)(2,1)S(1)} %maximum_select_fusion.3.refs_0_), channel_id=1, source_target_pairs={{0,16},{4,20},{8,24},{12,28},{16,0},{20,4},{24,8},{28,12},{1,17},{... | collective-permute-start | bytes 786440 | tf_op jit(solution)/shard_map/ppermute | solution.py:34
  31.0 12.7 %collective-permute-start.11 = (bf16[128,1024]{1,0:T(8,128)(2,1)S(1)}, bf16[128,1024]{1,0:T(8,128)(2,1)S(1)}, u32[]{:S(2)}, u32[]{:S(2)}) collective-permute-start(bf16[128,1024]{1,0:T(8,128)(2,1)S(1)} %maximum_select_fusion.3.refs_0_), channel_id=1, source_target_pairs={{0,4},{4,0},{8,12},{12,8},{16,20},{20,16},{24,28},{28,24},{1,5},{5... | collective-permute-start | bytes 786440 | tf_op jit(solution)/shard_map/ppermute | solution.py:34
  31.6 14.1 %collective-permute-start.12 = (bf16[128,1024]{1,0:T(8,128)(2,1)S(1)}, bf16[128,1024]{1,0:T(8,128)(2,1)S(1)}, u32[]{:S(2)}, u32[]{:S(2)}) collective-permute-start(bf16[128,1024]{1,0:T(8,128)(2,1)S(1)} %maximum_select_fusion.4.refs_6_.refs_0_), channel_id=1, source_target_pairs={{0,4},{4,0},{8,12},{12,8},{16,20},{20,16},{24,28},{28,24},{1,5},{5... | collective-permute-start | bytes 786440 | tf_op jit(solution)/shard_map/ppermute | solution.py:34
  45.7 20.9 %collective-permute-start.14 = (bf16[272,1024]{1,0:T(8,128)(2,1)S(1)}, bf16[272,1024]{1,0:T(8,128)(2,1)S(1)}, u32[]{:S(2)}, u32[]{:S(2)}) collective-permute-start(bf16[272,1024]{1,0:T(8,128)(2,1)S(1)} %collective-permute-done.8.refs_2_), channel_id=1, source_target_pairs={{0,4},{4,0},{8,12},{12,8},{16,20},{20,16},{24,28},{28,24},{1,5},{5... | collective-permute-start | bytes 1671176 | tf_op jit(solution)/shard_map/ppermute | solution.py:34
  47.3 19.3 %collective-permute-start.16 = (bf16[256,1024]{1,0:T(8,128)(2,1)S(1)}, bf16[256,1024]{1,0:T(8,128)(2,1)}, u32[]{:S(2)}, u32[]{:S(2)}) collective-permute-start(bf16[256,1024]{1,0:T(8,128)(2,1)S(1)} %pad_maximum_fusion.3), channel_id=1, source_target_pairs={{0,8},{4,12},{8,0},{12,4},{16,24},{20,28},{24,16},{28,20},{1,9},{5... | collective-permute-start | bytes 1572872 | tf_op jit(solution)/shard_map/ppermute | solution.py:34
  50.0 15.7 %collective-permute-start.15 = (bf16[128,1024]{1,0:T(8,128)(2,1)S(1)}, bf16[128,1024]{1,0:T(8,128)(2,1)S(1)}, u32[]{:S(2)}, u32[]{:S(2)}) collective-permute-start(bf16[128,1024]{1,0:T(8,128)(2,1)S(1)} %collective-permute-done.9.refs_1_), channel_id=1, source_target_pairs={{0,4},{4,0},{8,12},{12,8},{16,20},{20,16},{24,28},{28,24},{1,5},{5... | collective-permute-start | bytes 786440 | tf_op jit(solution)/shard_map/ppermute | solution.py:34
  50.6 15.1 %collective-permute-start.13 = (bf16[128,1024]{1,0:T(8,128)(2,1)S(1)}, bf16[128,1024]{1,0:T(8,128)(2,1)S(1)}, u32[]{:S(2)}, u32[]{:S(2)}) collective-permute-start(bf16[128,1024]{1,0:T(8,128)(2,1)S(1)} %maximum_select_fusion.4.refs_6_.refs_0_), channel_id=1, source_target_pairs={{0,16},{4,20},{8,24},{12,28},{16,0},{20,4},{24,8},{28,12},{1,17},{... | collective-permute-start | bytes 786440 | tf_op jit(solution)/shard_map/ppermute | solution.py:34
  86.3 19.5 %collective-permute-start.23 = (bf16[384,1024]{1,0:T(8,128)(2,1)}, bf16[384,1024]{1,0:T(8,128)(2,1)S(1)}, u32[]{:S(2)}, u32[]{:S(2)}) collective-permute-start(bf16[384,1024]{1,0:T(8,128)(2,1)} %pad_maximum_fusion), channel_id=1, source_target_pairs={{0,4},{4,0},{8,12},{12,8},{16,20},{20,16},{24,28},{28,24},{1,5},{5... | collective-permute-start | bytes 2359304 | tf_op jit(solution)/shard_map/ppermute | solution.py:34
  105.8 22.9 %collective-permute-start.26 = (bf16[480,1024]{1,0:T(8,128)(2,1)}, bf16[480,1024]{1,0:T(8,128)(2,1)S(1)}, u32[]{:S(2)}, u32[]{:S(2)}) collective-permute-start(bf16[480,1024]{1,0:T(8,128)(2,1)} %get-tuple-element.187.values_ref.refs_0_), channel_id=1, source_target_pairs={{0,4},{4,0},{8,12},{12,8},{16,20},{20,16},{24,28},{28,24},{1,5},{5... | collective-permute-start | bytes 2949128 | tf_op jit(solution)/shard_map/ppermute | solution.py:34
  132.6 20.7 %collective-permute-start.27 = (bf16[320,1024]{1,0:T(8,128)(2,1)S(1)}, bf16[320,1024]{1,0:T(8,128)(2,1)}, u32[]{:S(2)}, u32[]{:S(2)}) collective-permute-start(bf16[320,1024]{1,0:T(8,128)(2,1)S(1)} %copy-done.36), channel_id=1, source_target_pairs={{0,4},{4,0},{8,12},{12,8},{16,20},{20,16},{24,28},{28,24},{1,5},{5... | collective-permute-start | bytes 1966088 | tf_op jit(solution)/shard_map/ppermute | solution.py:34
  139.1 14.3 %collective-permute-start.31 = (bf16[256,1024]{1,0:T(8,128)(2,1)}, bf16[256,1024]{1,0:T(8,128)(2,1)S(1)}, u32[]{:S(2)}, u32[]{:S(2)}) collective-permute-start(bf16[256,1024]{1,0:T(8,128)(2,1)} %get-tuple-element.201), channel_id=1, source_target_pairs={{0,8},{4,12},{8,0},{12,4},{16,24},{20,28},{24,16},{28,20},{1,9},{5... | collective-permute-start | bytes 1572872 | tf_op jit(solution)/shard_map/ppermute | solution.py:34
  139.8 13.6 %collective-permute-start.33 = (bf16[160,1024]{1,0:T(8,128)(2,1)S(1)}, bf16[160,1024]{1,0:T(8,128)(2,1)S(1)}, u32[]{:S(2)}, u32[]{:S(2)}) collective-permute-start(bf16[160,1024]{1,0:T(8,128)(2,1)S(1)} %reduce-precision_convert_fusion.1.low_ref), channel_id=1, source_target_pairs={{0,1},{1,0},{2,3},{3,2},{4,5},{5,4},{6,7},{7,6},{8,9},{9,8},{10,11... | collective-permute-start | bytes 983048 | tf_op jit(solution)/shard_map/ppermute | solution.py:29
  143.6 12.9 %collective-permute-start.35 = (bf16[160,1024]{1,0:T(8,128)(2,1)}, bf16[160,1024]{1,0:T(8,128)(2,1)S(1)}, u32[]{:S(2)}, u32[]{:S(2)}) collective-permute-start(bf16[160,1024]{1,0:T(8,128)(2,1)} %slice.192), channel_id=1, source_target_pairs={{0,2},{2,0},{1,3},{3,1},{4,6},{6,4},{5,7},{7,5},{8,10},{10,8},{9,1... | collective-permute-start | bytes 983048 | tf_op jit(solution)/shard_map/ppermute | solution.py:29
  153.5 20.9 %collective-permute-start.34 = (bf16[320,1024]{1,0:T(8,128)(2,1)}, bf16[320,1024]{1,0:T(8,128)(2,1)S(1)}, u32[]{:S(2)}, u32[]{:S(2)}) collective-permute-start(bf16[320,1024]{1,0:T(8,128)(2,1)} %get-tuple-element.215.refs_0_), channel_id=1, source_target_pairs={{0,4},{4,0},{8,12},{12,8},{16,20},{20,16},{24,28},{28,24},{1,5},{5... | collective-permute-start | bytes 1966088 | tf_op jit(solution)/shard_map/ppermute | solution.py:34
  155.4 14.9 %collective-permute-start.38 = (bf16[128,1024]{1,0:T(8,128)(2,1)}, bf16[128,1024]{1,0:T(8,128)(2,1)S(1)}, u32[]{:S(2)}, u32[]{:S(2)}) collective-permute-start(bf16[128,1024]{1,0:T(8,128)(2,1)} %reduce-precision_convert_fusion.6), channel_id=1, source_target_pairs={{0,16},{4,20},{8,24},{12,28},{16,0},{20,4},{24,8},{28,12},{1,17},{... | collective-permute-start | bytes 786440 | tf_op jit(solution)/shard_map/ppermute | solution.py:34
  161.1 19.5 %collective-permute-start.40 = (bf16[256,1024]{1,0:T(8,128)(2,1)}, bf16[256,1024]{1,0:T(8,128)(2,1)}, u32[]{:S(2)}, u32[]{:S(2)}) collective-permute-start(bf16[256,1024]{1,0:T(8,128)(2,1)} %get-tuple-element.225), channel_id=1, source_target_pairs={{0,8},{4,12},{8,0},{12,4},{16,24},{20,28},{24,16},{28,20},{1,9},{5... | collective-permute-start | bytes 1572872 | tf_op jit(solution)/shard_map/ppermute | solution.py:34
  186.4 14.2 %collective-permute-start.43 = (bf16[128,1024]{1,0:T(8,128)(2,1)S(1)}, bf16[128,1024]{1,0:T(8,128)(2,1)S(1)}, u32[]{:S(2)}, u32[]{:S(2)}) collective-permute-start(bf16[128,1024]{1,0:T(8,128)(2,1)S(1)} %reduce-precision_convert_fusion.5), channel_id=1, source_target_pairs={{0,16},{4,20},{8,24},{12,28},{16,0},{20,4},{24,8},{28,12},{1,17},{... | collective-permute-start | bytes 786440 | tf_op jit(solution)/shard_map/ppermute | solution.py:34
  189.4 13.2 %collective-permute-start.42 = (bf16[144,1024]{1,0:T(8,128)(2,1)S(1)}, bf16[144,1024]{1,0:T(8,128)(2,1)S(1)}, u32[]{:S(2)}, u32[]{:S(2)}) collective-permute-start(bf16[144,1024]{1,0:T(8,128)(2,1)S(1)} %pad_maximum_fusion.6), channel_id=1, source_target_pairs={{0,8},{4,12},{8,0},{12,4},{16,24},{20,28},{24,16},{28,20},{1,9},{5... | collective-permute-start | bytes 884744 | tf_op jit(solution)/shard_map/ppermute | solution.py:34
  204.7 14.6 %collective-permute-start.44 = (bf16[144,1024]{1,0:T(8,128)(2,1)S(1)}, bf16[144,1024]{1,0:T(8,128)(2,1)S(1)}, u32[]{:S(2)}, u32[]{:S(2)}) collective-permute-start(bf16[144,1024]{1,0:T(8,128)(2,1)S(1)} %pad_maximum_fusion.7), channel_id=1, source_target_pairs={{0,16},{4,20},{8,24},{12,28},{16,0},{20,4},{24,8},{28,12},{1,17},{... | collective-permute-start | bytes 884744 | tf_op jit(solution)/shard_map/ppermute | solution.py:34
  (82 other events, 789.0 us)

commit v6 on v5

--- a/solution.py
+++ b/solution.py
@@ -628,6 +628,7 @@
     entering_all = with_other(inputs_own).astype(F32) * row_valid
     grads = (grad_own, swap(grad_own, "ctx"))
     normal_one, _ = norm_of(entering_all)
+    entering = entering_all[:own_slots]
     slots = 2 * own_slots
     f = first_shard
     if cube:
@@ -640,8 +641,8 @@
         f_near, u_far, f_far_x, u_x, d_x, u, d = tie(f_near, u_far, f_far_x, u_x, d_x, u, d)
         u_near = flip(rows_of(u, u_far), NEAR_BIT)
         d_far, f_near_x, u_far_x = flip(d, FAR_BIT), flip(f_near, X_BIT), flip(u_far, X_BIT)
-        d_far, f_near_x, u_far_x, u_near, d, normal_one = tie(
-            d_far, f_near_x, u_far_x, u_near, d, normal_one
+        d_far, f_near_x, u_far_x, u_near, d, normal_one, entering = tie(
+            d_far, f_near_x, u_far_x, u_near, d, normal_one, entering
         )
         d_near = flip(rows_of(d, d_far), NEAR_BIT)
         u_near_x = flip(u_near, X_BIT)
@@ -683,7 +684,6 @@
         d_rest_x = flip(d_rest, X_BIT)
     att_tp = swap(att_low, "tp")
     attended = att_low.astype(F32) + att_tp.astype(F32) + proj_bias
-    entering = entering_all[:own_slots]
     middle = entering + attended
     normal_two, _ = norm_of(middle)
     normed_two_own = (normal_two * gain_two + shift_two).astype(BF16)

time: 227 us -> 228 us (level)
  transfers between devices with their start and end apart: 50 -> 50, of which waited for: 26 -> 25; matrix products, arithmetic and copies ran while one was open for 13% -> 13% of each run, Pallas kernels for 20% -> 20%
where the time goes in v6:
time: 228 us; the launch traced here: 227 us
  waiting for transfers between devices  90.9 us (40%)
  Pallas kernels  52 us (23%)
  starting transfers between devices  41.8 us (18%)
  local copies, waits for them, and re-layouts  19.8 us (9%)
  other arithmetic  19.3 us (8%)
  between operations  2.96 us (1%)
    ppermute x27, waiting for transfers between devices, flip(): return lax.ppermute(array, 'fsdp', [(i, i ^ bit) for i in range(n)])  75.7 us
    ppermute x27, starting transfers between devices, flip(): return lax.ppermute(array, 'fsdp', [(i, i ^ bit) for i in range(n)])  35 us
    ppermute x23, waiting for transfers between devices, swap(): return lax.ppermute(array, axis, [(0, 1), (1, 0)])  15.2 us
    pallas_call x3, Pallas kernels, weight_grad(): pl.pallas_call(kernel, name='weight_grad', out_shape=[shape_of(size, colu...  11.8 us
    pallas_call x1, Pallas kernels, attention_back(): pl.pallas_call(kernel, name='attention_back', out_shape=[shape_of(slots,...  7.92 us
    pallas_call x1, Pallas kernels, attention(): pl.pallas_call(kernel, name='attention', in_specs=[pl.BlockSpec(memory_sp...  7.26 us
    unnamed x123, local copies, waits for them, and re-layouts  6.99 us
    ppermute x23, starting transfers between devices, swap(): return lax.ppermute(array, axis, [(0, 1), (1, 0)])  6.77 us
  transfers between devices with their start and end apart: 50, of which 25 were waited for; matrix products, arithmetic and copies ran while one was open for 13% of the time, Pallas kernels for 20%

profile of v6, /device:TPU:0, one launch (start us, length us, event | category | flops | bytes accessed | tf_op | source)
XLA Modules:
  0.0 226.7 jit_solution(11696586474963571227)
XLA Ops:
  8.3 4.1 %collective-permute-start.2 = (bf16[136,1024]{1,0:T(8,128)(2,1)S(1)}, bf16[136,1024]{1,0:T(8,128)(2,1)S(1)}, u32[]{:S(2)}, u32[]{:S(2)}) collective-permute-start(bf16[136,1024]{1,0:T(8,128)(2,1)S(1)} %pad_maximum_fusion.8.refs_0_), channel_id=1, source_target_pairs={{0,16},{4,20},{8,24},{12,28},{16,0},{20,4},{24,8},{28,12},{1,17},{... | collective-permute-start | bytes 835592 | tf_op jit(solution)/shard_map/ppermute | solution.py:34
  17.4 6.8 %collective-permute-done.4.refs_4_ = bf16[160,512]{1,0:T(8,128)(2,1)S(1)} collective-permute-done((bf16[160,512]{1,0:T(8,128)(2,1)S(1)}, bf16[160,512]{1,0:T(8,128)(2,1)S(1)}, u32[]{:S(2)}, u32[]{:S(2)}) %collective-permute-start.4) | collective-permute-done | bytes 163872 | tf_op jit(solution)/shard_map/ppermute | solution.py:34
  27.7 3.4 %collective-permute-start.8 = (bf16[128,1024]{1,0:T(8,128)(2,1)S(1)}, bf16[128,1024]{1,0:T(8,128)(2,1)S(1)}, u32[]{:S(2)}, u32[]{:S(2)}) collective-permute-start(bf16[128,1024]{1,0:T(8,128)(2,1)S(1)} %maximum_select_fusion.3.refs_0_), channel_id=1, source_target_pairs={{0,16},{4,20},{8,24},{12,28},{16,0},{20,4},{24,8},{28,12},{1,17},{... | collective-permute-start | bytes 786440 | tf_op jit(solution)/shard_map/ppermute | solution.py:34
  33.4 10.4 %collective-permute-done.8.refs_1_ = bf16[128,1024]{1,0:T(8,128)(2,1)S(1)} collective-permute-done((bf16[128,1024]{1,0:T(8,128)(2,1)S(1)}, bf16[128,1024]{1,0:T(8,128)(2,1)S(1)}, u32[]{:S(2)}, u32[]{:S(2)}) %collective-permute-start.8) | collective-permute-done | bytes 262176 | tf_op jit(solution)/shard_map/ppermute | solution.py:34
  53.7 12.1 %collective-permute-done.12.refs_7_.refs_1_ = bf16[128,1024]{1,0:T(8,128)(2,1)S(1)} collective-permute-done((bf16[128,1024]{1,0:T(8,128)(2,1)S(1)}, bf16[128,1024]{1,0:T(8,128)(2,1)S(1)}, u32[]{:S(2)}, u32[]{:S(2)}) %collective-permute-start.12) | collective-permute-done | bytes 262176 | tf_op jit(solution)/shard_map/ppermute | solution.py:34
  71.7 7.3 %attention.1 = (bf16[320,256]{1,0:T(8,128)(2,1)}, bf16[320,256]{1,0:T(8,128)(2,1)}, bf16[320,256]{1,0:T(8,128)(2,1)}, bf16[320,256]{1,0:T(8,128)(2,1)}, f32[160,...) custom-call(s32[11]{0:T(128)} %pad_add_fusion.places_ref, ...), custom_call_target="tpu_custom_call" | custom-call | flops 1000 | bytes 1000 | tf_op jit(solution)/shard_map/attention/pallas_call | solution.py:201
  87.5 5.7 %collective-permute-done.20 = bf16[160,1024]{1,0:T(8,128)(2,1)S(1)} collective-permute-done((bf16[160,1024]{1,0:T(8,128)(2,1)S(1)}, bf16[160,1024]{1,0:T(8,128)(2,1)S(1)}, u32[]{:S(2)}, u32[]{:S(2)}) %collective-permute-start.20) | collective-permute-done | bytes 327712 | tf_op jit(solution)/shard_map/ppermute | solution.py:29
  97.0 4.9 %hidden_layer.1 = (bf16[480,1024]{1,0:T(8,128)(2,1)}, f32[320,1024]{1,0:T(8,128)}) custom-call(bf16[160,1024]{1,0:T(8,128)(2,1)} %copy-done.11, bf16[160,1024]{1,0:T(8,128)(2,1)} %copy-done.23, bf16[320,1024]{1,0:T(8,128)(2,1)} %get-tuple-element.173.normed_ref.refs_2_, f32[1,1024]{1,0:T(1,128)} %constant_dynamic-slice_fusion.7.bias_ref, ...), custom_call_target="tpu_custom_call" | custom-call | flops 1000 | bytes 1000 | tf_op jit(solution)/shard_map/hidden_layer/pallas_call | solution.py:279
  101.9 4.1 %collective-permute-done.23.refs_10_.refs_4_ = bf16[384,1024]{1,0:T(8,128)(2,1)S(1)} collective-permute-done((bf16[384,1024]{1,0:T(8,128)(2,1)}, bf16[384,1024]{1,0:T(8,128)(2,1)S(1)}, u32[]{:S(2)}, u32[]{:S(2)}) %collective-permute-start.23) | collective-permute-done | bytes 786464 | tf_op jit(solution)/shard_map/ppermute | solution.py:34
  107.7 6.5 %hidden_back.1 = (bf16[320,1024]{1,0:T(8,128)(2,1)}, f32[160,1024]{1,0:T(8,128)}, bf16[160,1024]{1,0:T(8,128)(2,1)}, f32[1,1024]{1,0:T(1,128)}) custom-call(bf16[160,1024]{1,0:T(8,128)(2,1)} %bitcast.118, bf16[160,1024]{1,0:T(8,128)(2,1)} %copy-done.20, f32[320,1024]{1,0:T(8,128)} %get-tuple-element.181.slope_ref, bf16[128,1024]{1,0:T(8,128)(2,1)} %copy-done.9, ...), custom_call_target="tpu_custom_call" | custom-call | flops 1000 | bytes 1000 | tf_op jit(solution)/shard_map/hidden_back/pallas_call | solution.py:306
  117.8 4.1 %project_back.1 = (f32[160,1024]{1,0:T(8,128)}, bf16[160,1024]{1,0:T(8,128)(2,1)}) custom-call(bf16[480,1024]{1,0:T(8,128)(2,1)} %get-tuple-element.189.values_ref.refs_0_, bf16[128,1024]{1,0:T(8,128)(2,1)} %copy-done.7, bf16[128,1024]{1,0:T(8,128)(2,1)} %copy-done.8, bf16[256,1024]{1,0:T(8,128)(2,1)} %copy-done.5, bf16[128,1024]{1,0:T(8,128)(2,1)} %copy-done.27, ...), custom_call_target="tpu_custom_call" | custom-call | flops 1000 | bytes 1000 | tf_op jit(solution)/shard_map/project_back/pallas_call | solution.py:328
  121.9 5.1 %collective-permute-done.25.other_ref = bf16[160,1024]{1,0:T(8,128)(2,1)S(1)} collective-permute-done((bf16[160,1024]{1,0:T(8,128)(2,1)S(1)}, bf16[160,1024]{1,0:T(8,128)(2,1)S(1)}, u32[]{:S(2)}, u32[]{:S(2)}) %collective-permute-start.25) | collective-permute-done | bytes 327712 | tf_op jit(solution)/shard_map/ppermute | solution.py:29
  128.9 3.3 %second_norm_back.1 = (f32[160,1024]{1,0:T(8,128)}, bf16[160,1024]{1,0:T(8,128)(2,1)}, f32[4,1024]{1,0:T(4,128)}) custom-call(f32[160,1024]{1,0:T(8,128)} %copy-done, f32[1,1024]{1,0:T(1,128)} %copy-done.55, bf16[160,1024]{1,0:T(8,128)(2,1)} %copy-done.22, bf16[160,1024]{1,0:T(8,128)(2,1)} %copy-done.43, bf16[160,1024]{1,0:T(8,128)(2,1)} %bitcast.119), custom_call_target="tpu_custom_call" | custom-call | flops 1000 | bytes 1000 | tf_op jit(solution)/shard_map/second_norm_back/pallas_call | solution.py:421
  135.4 3.7 %weight_grad.3 = (bf16[256,1024]{1,0:T(8,128)(2,1)}, f32[256,1024]{1,0:T(8,128)}) custom-call(bf16[480,1024]{1,0:T(8,128)(2,1)} %get-tuple-element.189.values_ref.refs_0_, bf16[480,1024]{1,0:T(8,128)(2,1)} %copy-done.1, bf16[160,1024]{1,0:T(8,128)(2,1)} %bitcast.120, bf16[160,1024]{1,0:T(8,128)(2,1)} %copy-done.20, bf16[160,512]{1,0:T(8,128)(2,1)} %copy-done.51, ...), custom_call_target="tpu_custom_call" | custom-call | flops 1000 | bytes 1000 | tf_op jit(solution)/shard_map/weight_grad/pallas_call | solution.py:371
  143.7 7.9 %attention_back.1 = (bf16[320,1024]{1,0:T(8,128)(2,1)}, f32[160,1024]{1,0:T(8,128)}, bf16[160,1024]{1,0:T(8,128)(2,1)}, f32[1,512]{1,0:T(1,128)}) custom-call(bf16[160,1024]{1,0:T(8,128)(2,1)} %get-tuple-element.199.grad_own.refs_5_, bf16[160,1024]{1,0:T(8,128)(2,1)} %copy-done.19, bf16[320,256]{1,0:T(8,128)(2,1)} %get-tuple-element.205.context_ref, ...), custom_call_target="tpu_custom_call" | custom-call | flops 1000 | bytes 1000 | tf_op jit(solution)/shard_map/attention_back/pallas_call | solution.py:248
  157.3 3.8 %weight_grad.5 = (bf16[256,1024]{1,0:T(8,128)(2,1)}, f32[256,1024]{1,0:T(8,128)}) custom-call(bf16[320,1024]{1,0:T(8,128)(2,1)} %get-tuple-element.192.refs_0_, bf16[320,1024]{1,0:T(8,128)(2,1)} %collective-permute-done.27.refs_1_, bf16[160,1024]{1,0:T(8,128)(2,1)} %copy-done.11, bf16[160,1024]{1,0:T(8,128)(2,1)} %copy-done.23, bf16[480,1024]{1,0:T(8,128)(2,1)} %copy-done.1, ...), custom_call_target="tpu_custom_call" | custom-call | flops 1000 | bytes 1000 | tf_op jit(solution)/shard_map/weight_grad/pallas_call | solution.py:371
  163.7 6.6 %collective-permute-done.38 = bf16[128,1024]{1,0:T(8,128)(2,1)S(1)} collective-permute-done((bf16[128,1024]{1,0:T(8,128)(2,1)}, bf16[128,1024]{1,0:T(8,128)(2,1)S(1)}, u32[]{:S(2)}, u32[]{:S(2)}) %collective-permute-start.38) | collective-permute-done | bytes 262176 | tf_op jit(solution)/shard_map/ppermute | solution.py:34
  171.1 3.2 %finish.1 = (bf16[160,1024]{1,0:T(8,128)(2,1)}, f32[1,128]{1,0:T(1,128)}) custom-call(s32[11]{0:T(128)} %pad_add_fusion.places_ref, f32[160,1024]{1,0:T(8,128)} %copy-done, f32[160,1024]{1,0:T(8,128)} %copy-done.4, f32[160,1024]{1,0:T(8,128)} %get-tuple-element.254.attended_ref, bf16[160,1024]{1,0:T(8,128)(2,1)} %copy-done.24, bf16[160,1024]{1,0:T(8,128)(2,1)} %copy-done.44, ...), custom_call_target="tpu_custom_call" | custom-call | flops 1000 | bytes 1000 | tf_op jit(solution)/shard_map/finish/pallas_call | solution.py:464
  175.9 4.2 %weight_grad.4 = (bf16[128,1024]{1,0:T(8,128)(2,1)}, bf16[128,1024]{1,0:T(8,128)(2,1)}, f32[256,1024]{1,0:T(8,128)}) custom-call(bf16[320,1024]{1,0:T(8,128)(2,1)} %get-tuple-element.217.refs_0_, bf16[320,1024]{1,0:T(8,128)(2,1)} %copy-done.37, bf16[320,1024]{1,0:T(8,128)(2,1)} %get-tuple-element.173.normed_ref.refs_2_, bf16[480,1024]{1,0:T(8,128)(2,1)} %copy-done.1, ...), custom_call_target="tpu_custom_call" | custom-call | flops 1000 | bytes 1000 | tf_op jit(solution)/shard_map/weight_grad/pallas_call | solution.py:371
  181.4 3.0 %first_norm_back.1 = (f32[160,1024]{1,0:T(8,128)}, f32[8,1024]{1,0:T(8,128)}) custom-call(s32[11]{0:T(128)} %pad_add_fusion.places_ref, bf16[160,1024]{1,0:T(8,128)(2,1)} %bitcast.115, f32[1,1024]{1,0:T(1,128)} %get-tuple-element.277.gain_ref, bf16[160,1024]{1,0:T(8,128)(2,1)} %copy-done.21, bf16[160,1024]{1,0:T(8,128)(2,1)} %copy-done.42, ...), custom_call_target="tpu_custom_call" | custom-call | flops 1000 | bytes 1000 | tf_op jit(solution)/shard_map/first_norm_back/pallas_call | solution.py:499
  190.6 10.1 %collective-permute-done.43 = bf16[128,1024]{1,0:T(8,128)(2,1)S(1)} collective-permute-done((bf16[128,1024]{1,0:T(8,128)(2,1)S(1)}, bf16[128,1024]{1,0:T(8,128)(2,1)S(1)}, u32[]{:S(2)}, u32[]{:S(2)}) %collective-permute-start.43) | collective-permute-done | bytes 262176 | tf_op jit(solution)/shard_map/ppermute | solution.py:34
  204.8 2.4 %collective-permute-start.44 = (bf16[144,1024]{1,0:T(8,128)(2,1)S(1)}, bf16[144,1024]{1,0:T(8,128)(2,1)S(1)}, u32[]{:S(2)}, u32[]{:S(2)}) collective-permute-start(bf16[144,1024]{1,0:T(8,128)(2,1)S(1)} %pad_maximum_fusion.7), channel_id=1, source_target_pairs={{0,16},{4,20},{8,24},{12,28},{16,0},{20,4},{24,8},{28,12},{1,17},{... | collective-permute-start | bytes 884744 | tf_op jit(solution)/shard_map/ppermute | solution.py:34
  207.2 5.8 %collective-permute-done.46 = bf16[128,1024]{1,0:T(8,128)(2,1)S(1)} collective-permute-done((bf16[128,1024]{1,0:T(8,128)(2,1)}, bf16[128,1024]{1,0:T(8,128)(2,1)S(1)}, u32[]{:S(2)}, u32[]{:S(2)}) %collective-permute-start.46) | collective-permute-done | bytes 262176 | tf_op jit(solution)/shard_map/ppermute | solution.py:34
  214.3 5.1 %collective-permute-done.44 = bf16[144,1024]{1,0:T(8,128)(2,1)S(1)} collective-permute-done((bf16[144,1024]{1,0:T(8,128)(2,1)S(1)}, bf16[144,1024]{1,0:T(8,128)(2,1)S(1)}, u32[]{:S(2)}, u32[]{:S(2)}) %collective-permute-start.44) | collective-permute-done | bytes 294944 | tf_op jit(solution)/shard_map/ppermute | solution.py:34
  (308 shorter events, 89.9 us)
Async XLA Ops:
  8.3 16.9 %collective-permute-start.2 = (bf16[136,1024]{1,0:T(8,128)(2,1)S(1)}, bf16[136,1024]{1,0:T(8,128)(2,1)S(1)}, u32[]{:S(2)}, u32[]{:S(2)}) collective-permute-start(bf16[136,1024]{1,0:T(8,128)(2,1)S(1)} %pad_maximum_fusion.8.refs_0_), channel_id=1, source_target_pairs={{0,16},{4,20},{8,24},{12,28},{16,0},{20,4},{24,8},{28,12},{1,17},{... | collective-permute-start | bytes 835592 | tf_op jit(solution)/shard_map/ppermute | solution.py:34
  12.4 12.8 %collective-permute-start.3 = (bf16[136,1024]{1,0:T(8,128)(2,1)S(1)}, bf16[136,1024]{1,0:T(8,128)(2,1)S(1)}, u32[]{:S(2)}, u32[]{:S(2)}) collective-permute-start(bf16[136,1024]{1,0:T(8,128)(2,1)S(1)} %pad_maximum_fusion.8.refs_0_), channel_id=1, source_target_pairs={{0,4},{4,0},{8,12},{12,8},{16,20},{20,16},{24,28},{28,24},{1,5},{5... | collective-permute-start | bytes 835592 | tf_op jit(solution)/shard_map/ppermute | solution.py:34
  17.2 14.4 %collective-permute-start.16 = (bf16[160,1024]{1,0:T(8,128)(2,1)S(1)}, bf16[160,1024]{1,0:T(8,128)(2,1)S(1)}, u32[]{:S(2)}, u32[]{:S(2)}) collective-permute-start(bf16[160,1024]{1,0:T(8,128)(2,1)S(1)} %bitcast.111), channel_id=1, source_target_pairs={{0,2},{2,0},{1,3},{3,1},{4,6},{6,4},{5,7},{7,5},{8,10},{10,8},{9,1... | collective-permute-start | bytes 983048 | tf_op jit(solution)/shard_map/ppermute | solution.py:29
  25.3 20.4 %collective-permute-start.7 = (bf16[272,1024]{1,0:T(8,128)(2,1)S(1)}, bf16[272,1024]{1,0:T(8,128)(2,1)S(1)}, u32[]{:S(2)}, u32[]{:S(2)}) collective-permute-start(bf16[272,1024]{1,0:T(8,128)(2,1)S(1)} %pad_maximum_fusion.2), channel_id=1, source_target_pairs={{0,8},{4,12},{8,0},{12,4},{16,24},{20,28},{24,16},{28,20},{1,9},{5... | collective-permute-start | bytes 1671176 | tf_op jit(solution)/shard_map/ppermute | solution.py:34
  26.2 19.5 %collective-permute-start.9 = (bf16[136,1024]{1,0:T(8,128)(2,1)S(1)}, bf16[136,1024]{1,0:T(8,128)(2,1)S(1)}, u32[]{:S(2)}, u32[]{:S(2)}) collective-permute-start(bf16[136,1024]{1,0:T(8,128)(2,1)S(1)} %collective-permute-done.2.refs_1_), channel_id=1, source_target_pairs={{0,4},{4,0},{8,12},{12,8},{16,20},{20,16},{24,28},{28,24},{1,5},{5... | collective-permute-start | bytes 835592 | tf_op jit(solution)/shard_map/ppermute | solution.py:34
  27.7 16.1 %collective-permute-start.8 = (bf16[128,1024]{1,0:T(8,128)(2,1)S(1)}, bf16[128,1024]{1,0:T(8,128)(2,1)S(1)}, u32[]{:S(2)}, u32[]{:S(2)}) collective-permute-start(bf16[128,1024]{1,0:T(8,128)(2,1)S(1)} %maximum_select_fusion.3.refs_0_), channel_id=1, source_target_pairs={{0,16},{4,20},{8,24},{12,28},{16,0},{20,4},{24,8},{28,12},{1,17},{... | collective-permute-start | bytes 786440 | tf_op jit(solution)/shard_map/ppermute | solution.py:34
  31.0 12.7 %collective-permute-start.10 = (bf16[128,1024]{1,0:T(8,128)(2,1)S(1)}, bf16[128,1024]{1,0:T(8,128)(2,1)S(1)}, u32[]{:S(2)}, u32[]{:S(2)}) collective-permute-start(bf16[128,1024]{1,0:T(8,128)(2,1)S(1)} %maximum_select_fusion.3.refs_0_), channel_id=1, source_target_pairs={{0,4},{4,0},{8,12},{12,8},{16,20},{20,16},{24,28},{28,24},{1,5},{5... | collective-permute-start | bytes 786440 | tf_op jit(solution)/shard_map/ppermute | solution.py:34
  31.6 14.1 %collective-permute-start.11 = (bf16[128,1024]{1,0:T(8,128)(2,1)S(1)}, bf16[128,1024]{1,0:T(8,128)(2,1)S(1)}, u32[]{:S(2)}, u32[]{:S(2)}) collective-permute-start(bf16[128,1024]{1,0:T(8,128)(2,1)S(1)} %maximum_select_fusion.4.refs_6_.refs_0_), channel_id=1, source_target_pairs={{0,4},{4,0},{8,12},{12,8},{16,20},{20,16},{24,28},{28,24},{1,5},{5... | collective-permute-start | bytes 786440 | tf_op jit(solution)/shard_map/ppermute | solution.py:34
  45.7 20.9 %collective-permute-start.13 = (bf16[272,1024]{1,0:T(8,128)(2,1)S(1)}, bf16[272,1024]{1,0:T(8,128)(2,1)S(1)}, u32[]{:S(2)}, u32[]{:S(2)}) collective-permute-start(bf16[272,1024]{1,0:T(8,128)(2,1)S(1)} %collective-permute-done.7.refs_2_), channel_id=1, source_target_pairs={{0,4},{4,0},{8,12},{12,8},{16,20},{20,16},{24,28},{28,24},{1,5},{5... | collective-permute-start | bytes 1671176 | tf_op jit(solution)/shard_map/ppermute | solution.py:34
  47.4 19.3 %collective-permute-start.15 = (bf16[256,1024]{1,0:T(8,128)(2,1)S(1)}, bf16[256,1024]{1,0:T(8,128)(2,1)}, u32[]{:S(2)}, u32[]{:S(2)}) collective-permute-start(bf16[256,1024]{1,0:T(8,128)(2,1)S(1)} %pad_maximum_fusion.3), channel_id=1, source_target_pairs={{0,8},{4,12},{8,0},{12,4},{16,24},{20,28},{24,16},{28,20},{1,9},{5... | collective-permute-start | bytes 1572872 | tf_op jit(solution)/shard_map/ppermute | solution.py:34
  50.1 15.7 %collective-permute-start.14 = (bf16[128,1024]{1,0:T(8,128)(2,1)S(1)}, bf16[128,1024]{1,0:T(8,128)(2,1)S(1)}, u32[]{:S(2)}, u32[]{:S(2)}) collective-permute-start(bf16[128,1024]{1,0:T(8,128)(2,1)S(1)} %collective-permute-done.8.refs_1_), channel_id=1, source_target_pairs={{0,4},{4,0},{8,12},{12,8},{16,20},{20,16},{24,28},{28,24},{1,5},{5... | collective-permute-start | bytes 786440 | tf_op jit(solution)/shard_map/ppermute | solution.py:34
  50.7 15.1 %collective-permute-start.12 = (bf16[128,1024]{1,0:T(8,128)(2,1)S(1)}, bf16[128,1024]{1,0:T(8,128)(2,1)S(1)}, u32[]{:S(2)}, u32[]{:S(2)}) collective-permute-start(bf16[128,1024]{1,0:T(8,128)(2,1)S(1)} %maximum_select_fusion.4.refs_6_.refs_0_), channel_id=1, source_target_pairs={{0,16},{4,20},{8,24},{12,28},{16,0},{20,4},{24,8},{28,12},{1,17},{... | collective-permute-start | bytes 786440 | tf_op jit(solution)/shard_map/ppermute | solution.py:34
  86.5 19.5 %collective-permute-start.23 = (bf16[384,1024]{1,0:T(8,128)(2,1)}, bf16[384,1024]{1,0:T(8,128)(2,1)S(1)}, u32[]{:S(2)}, u32[]{:S(2)}) collective-permute-start(bf16[384,1024]{1,0:T(8,128)(2,1)} %pad_maximum_fusion), channel_id=1, source_target_pairs={{0,4},{4,0},{8,12},{12,8},{16,20},{20,16},{24,28},{28,24},{1,5},{5... | collective-permute-start | bytes 2359304 | tf_op jit(solution)/shard_map/ppermute | solution.py:34
  106.0 22.9 %collective-permute-start.26 = (bf16[480,1024]{1,0:T(8,128)(2,1)}, bf16[480,1024]{1,0:T(8,128)(2,1)S(1)}, u32[]{:S(2)}, u32[]{:S(2)}) collective-permute-start(bf16[480,1024]{1,0:T(8,128)(2,1)} %get-tuple-element.189.values_ref.refs_0_), channel_id=1, source_target_pairs={{0,4},{4,0},{8,12},{12,8},{16,20},{20,16},{24,28},{28,24},{1,5},{5... | collective-permute-start | bytes 2949128 | tf_op jit(solution)/shard_map/ppermute | solution.py:34
  132.8 20.7 %collective-permute-start.27 = (bf16[320,1024]{1,0:T(8,128)(2,1)S(1)}, bf16[320,1024]{1,0:T(8,128)(2,1)}, u32[]{:S(2)}, u32[]{:S(2)}) collective-permute-start(bf16[320,1024]{1,0:T(8,128)(2,1)S(1)} %copy-done.36), channel_id=1, source_target_pairs={{0,4},{4,0},{8,12},{12,8},{16,20},{20,16},{24,28},{28,24},{1,5},{5... | collective-permute-start | bytes 1966088 | tf_op jit(solution)/shard_map/ppermute | solution.py:34
  139.2 14.3 %collective-permute-start.31 = (bf16[256,1024]{1,0:T(8,128)(2,1)}, bf16[256,1024]{1,0:T(8,128)(2,1)S(1)}, u32[]{:S(2)}, u32[]{:S(2)}) collective-permute-start(bf16[256,1024]{1,0:T(8,128)(2,1)} %get-tuple-element.203), channel_id=1, source_target_pairs={{0,8},{4,12},{8,0},{12,4},{16,24},{20,28},{24,16},{28,20},{1,9},{5... | collective-permute-start | bytes 1572872 | tf_op jit(solution)/shard_map/ppermute | solution.py:34
  139.8 13.7 %collective-permute-start.33 = (bf16[160,1024]{1,0:T(8,128)(2,1)S(1)}, bf16[160,1024]{1,0:T(8,128)(2,1)S(1)}, u32[]{:S(2)}, u32[]{:S(2)}) collective-permute-start(bf16[160,1024]{1,0:T(8,128)(2,1)S(1)} %reduce-precision_convert_fusion.1.low_ref), channel_id=1, source_target_pairs={{0,1},{1,0},{2,3},{3,2},{4,5},{5,4},{6,7},{7,6},{8,9},{9,8},{10,11... | collective-permute-start | bytes 983048 | tf_op jit(solution)/shard_map/ppermute | solution.py:29
  143.6 12.9 %collective-permute-start.35 = (bf16[160,1024]{1,0:T(8,128)(2,1)}, bf16[160,1024]{1,0:T(8,128)(2,1)S(1)}, u32[]{:S(2)}, u32[]{:S(2)}) collective-permute-start(bf16[160,1024]{1,0:T(8,128)(2,1)} %slice.192), channel_id=1, source_target_pairs={{0,2},{2,0},{1,3},{3,1},{4,6},{6,4},{5,7},{7,5},{8,10},{10,8},{9,1... | collective-permute-start | bytes 983048 | tf_op jit(solution)/shard_map/ppermute | solution.py:29
  153.6 20.8 %collective-permute-start.34 = (bf16[320,1024]{1,0:T(8,128)(2,1)}, bf16[320,1024]{1,0:T(8,128)(2,1)S(1)}, u32[]{:S(2)}, u32[]{:S(2)}) collective-permute-start(bf16[320,1024]{1,0:T(8,128)(2,1)} %get-tuple-element.217.refs_0_), channel_id=1, source_target_pairs={{0,4},{4,0},{8,12},{12,8},{16,20},{20,16},{24,28},{28,24},{1,5},{5... | collective-permute-start | bytes 1966088 | tf_op jit(solution)/shard_map/ppermute | solution.py:34
  155.4 14.9 %collective-permute-start.38 = (bf16[128,1024]{1,0:T(8,128)(2,1)}, bf16[128,1024]{1,0:T(8,128)(2,1)S(1)}, u32[]{:S(2)}, u32[]{:S(2)}) collective-permute-start(bf16[128,1024]{1,0:T(8,128)(2,1)} %reduce-precision_convert_fusion.6), channel_id=1, source_target_pairs={{0,16},{4,20},{8,24},{12,28},{16,0},{20,4},{24,8},{28,12},{1,17},{... | collective-permute-start | bytes 786440 | tf_op jit(solution)/shard_map/ppermute | solution.py:34
  161.2 19.5 %collective-permute-start.40 = (bf16[256,1024]{1,0:T(8,128)(2,1)}, bf16[256,1024]{1,0:T(8,128)(2,1)}, u32[]{:S(2)}, u32[]{:S(2)}) collective-permute-start(bf16[256,1024]{1,0:T(8,128)(2,1)} %get-tuple-element.227), channel_id=1, source_target_pairs={{0,8},{4,12},{8,0},{12,4},{16,24},{20,28},{24,16},{28,20},{1,9},{5... | collective-permute-start | bytes 1572872 | tf_op jit(solution)/shard_map/ppermute | solution.py:34
  186.5 14.2 %collective-permute-start.43 = (bf16[128,1024]{1,0:T(8,128)(2,1)S(1)}, bf16[128,1024]{1,0:T(8,128)(2,1)S(1)}, u32[]{:S(2)}, u32[]{:S(2)}) collective-permute-start(bf16[128,1024]{1,0:T(8,128)(2,1)S(1)} %reduce-precision_convert_fusion.5), channel_id=1, source_target_pairs={{0,16},{4,20},{8,24},{12,28},{16,0},{20,4},{24,8},{28,12},{1,17},{... | collective-permute-start | bytes 786440 | tf_op jit(solution)/shard_map/ppermute | solution.py:34
  189.4 13.2 %collective-permute-start.42 = (bf16[144,1024]{1,0:T(8,128)(2,1)S(1)}, bf16[144,1024]{1,0:T(8,128)(2,1)S(1)}, u32[]{:S(2)}, u32[]{:S(2)}) collective-permute-start(bf16[144,1024]{1,0:T(8,128)(2,1)S(1)} %pad_maximum_fusion.6), channel_id=1, source_target_pairs={{0,8},{4,12},{8,0},{12,4},{16,24},{20,28},{24,16},{28,20},{1,9},{5... | collective-permute-start | bytes 884744 | tf_op jit(solution)/shard_map/ppermute | solution.py:34
  204.8 14.7 %collective-permute-start.44 = (bf16[144,1024]{1,0:T(8,128)(2,1)S(1)}, bf16[144,1024]{1,0:T(8,128)(2,1)S(1)}, u32[]{:S(2)}, u32[]{:S(2)}) collective-permute-start(bf16[144,1024]{1,0:T(8,128)(2,1)S(1)} %pad_maximum_fusion.7), channel_id=1, source_target_pairs={{0,16},{4,20},{8,24},{12,28},{16,0},{20,4},{24,8},{28,12},{1,17},{... | collective-permute-start | bytes 884744 | tf_op jit(solution)/shard_map/ppermute | solution.py:34
  (82 other events, 822.2 us)
